TPU v7x, 32 devices: a whole 2x2x4 slice. The times are simulated.
32 devices in a mesh: dp: 8 (over y, x, core), seq: 4 (over z).
Axes of the slice: x: 2, y: 2, z: 4, core: 2. Of those that a mesh axis runs over, the one named last changes fastest.
Arguments:
- block_in: bfloat16 [8, 1024, 1024], P('dp', 'seq'), may hold values from -6 to 6
- segment_ids: int32 [8, 1024], P('dp'), may hold values from 0 to 2, never falling along the last dimension, each value on 1 to 512 neighbouring positions
- mamba_z: bfloat16 [1024, 1536], P(('dp', 'seq')), may hold values from -0.1875 to 0.1875
- mamba_x: bfloat16 [1024, 1536], P(('dp', 'seq')), may hold values from -0.1875 to 0.1875
- mamba_bc: bfloat16 [1024, 256], P(('dp', 'seq')), may hold values from -0.1875 to 0.1875
- mamba_dt: bfloat16 [1024, 24], P(('dp', 'seq')), may hold values from -0.1875 to 0.1875
- mamba_out: bfloat16 [1024, 1536], P(('dp', 'seq')), may hold values from -0.15625 to 0.15625
- attn_q: bfloat16 [1024, 512], P(('dp', 'seq')), may hold values from -0.1875 to 0.1875
- attn_kv: bfloat16 [1024, 256], P(('dp', 'seq')), may hold values from -0.1875 to 0.1875
- attn_out: bfloat16 [1024, 512], P(('dp', 'seq')), may hold values from -2 to 2
- ffn_gate: bfloat16 [1024, 2048], P(('dp', 'seq')), may hold values from -0.1875 to 0.1875
- ffn_up: bfloat16 [1024, 2048], P(('dp', 'seq')), may hold values from -0.1875 to 0.1875
- ffn_down: bfloat16 [1024, 2048], P(('dp', 'seq')), may hold values from -0.125 to 0.125
- mixer_norm: bfloat16 [1024], P(('dp', 'seq')), may hold values from 0.5 to 1.5
- ffn_norm: bfloat16 [1024], P(('dp', 'seq')), may hold values from 0.5 to 1.5
- conv_weight: float32 [4, 1792], replicated, may hold values from -3 to 3
- conv_bias: float32 [1792], replicated, may hold values from -0.5 to 0.5
- dt_bias: float32 [24], replicated, may hold values from -1 to 1
- a_log: float32 [24], replicated, may hold values from -6.5 to -3
- d_skip: float32 [24], replicated, may hold values from 0.5 to 1.5
- inner_norm: float32 [1536], replicated, may hold values from 0.5 to 1.5
- grad_out: bfloat16 [8, 1024, 1024], P('dp', 'seq'), may hold values from -6 to 6
Outputs:
- block_out: bfloat16 [8, 1024, 1024], P('dp', 'seq')
- grad_in: bfloat16 [8, 1024, 1024], P('dp', 'seq')
- grad_mamba_z: float32 [1024, 1536], P(('dp', 'seq'))
- grad_mamba_x: float32 [1024, 1536], P(('dp', 'seq'))
- grad_mamba_bc: float32 [1024, 256], P(('dp', 'seq'))
- grad_mamba_dt: float32 [1024, 24], P(('dp', 'seq'))
- grad_mamba_out: float32 [1024, 1536], P(('dp', 'seq'))
- grad_attn_q: float32 [1024, 512], P(('dp', 'seq'))
- grad_attn_kv: float32 [1024, 256], P(('dp', 'seq'))
- grad_attn_out: float32 [1024, 512], P(('dp', 'seq'))
- grad_ffn_gate: float32 [1024, 2048], P(('dp', 'seq'))
- grad_ffn_up: float32 [1024, 2048], P(('dp', 'seq'))
- grad_ffn_down: float32 [1024, 2048], P(('dp', 'seq'))
- grad_mixer_norm: float32 [1024], P(('dp', 'seq'))
- grad_ffn_norm: float32 [1024], P(('dp', 'seq'))
- grad_conv_weight: float32 [4, 1792], replicated
- grad_conv_bias: float32 [1792], replicated
- grad_dt_bias: float32 [24], replicated
- grad_a_log: float32 [24], replicated
- grad_d_skip: float32 [24], replicated
- grad_inner_norm: float32 [1536], replicated
Inputs may be any that keep to these rules, and one draw needn't show every extreme that they name: `segment_ids`: along each sequence the ids start at 0 and never fall, so that equal ids form one run of tokens; a document has at most 512 tokens.
All inputs are finite; a program needn't handle non-finite values.
Results may differ from a plain program's by a relative error of at most 0.013.
Values may be sent and summed in bfloat16 or wider, within the bound.
No kernel may reach another device: no remote copies, remote signals or barrier semaphores. Data moves between devices by JAX's collectives and lax.ppermute only.
A program may use at most 256 MiB of HBM per device.

v0:
```python
import jax
import jax.numpy as jnp
from jax import lax
from jax.sharding import PartitionSpec as P

SSM_HEADS = 24
SSM_HEAD = 64
STATE = 128
Q_HEADS = 8
KV_HEADS = 2
HEAD = 64


EPSILON = 1e-05
ROPE_BASE = 100000000000.0


def passed_along(block, axis, distance):
    devices = range(lax.axis_size(axis))
    route = [(i - distance, i) for i in devices if i - distance in devices]
    return lax.ppermute(block, axis, route)


def silu_grad(value):
    sigma = jax.nn.sigmoid(value)
    return sigma * (1.0 + value * (1.0 - sigma))


def rms_forward(value, gain):
    factor = lax.rsqrt(jnp.mean(value * value, axis=-1, keepdims=True) + EPSILON)
    return (value * factor * gain, factor)


def rms_backward(value, factor, gain, upstream):
    weighted = upstream * gain
    gain_grad = jnp.sum(upstream * value * factor, axis=0)
    inward = factor * weighted - value * factor * factor * factor * jnp.mean(
        weighted * value, axis=-1, keepdims=True
    )
    return (inward, gain_grad)


def matmul(left, right):
    return jnp.dot(left, right, preferred_element_type=jnp.float32)


def matmul_nt(left, right):
    return lax.dot_general(
        left, right, (((1,), (1,)), ((), ())), preferred_element_type=jnp.float32
    )


def matmul_tn(left, right):
    return lax.dot_general(
        left, right, (((0,), (0,)), ((), ())), preferred_element_type=jnp.float32
    )


def rope_tables(positions, head_size):
    half = head_size // 2
    freq_scale = ROPE_BASE ** (-jnp.arange(half, dtype=jnp.float32) / half)
    angles = positions.astype(jnp.float32)[:, None] * freq_scale[None, :]
    return (jnp.cos(angles), jnp.sin(angles))


def rotate(value, cosine, sine):
    half = value.shape[-1] // 2
    first = value[..., :half]
    second = value[..., half:]
    return jnp.concatenate(
        [first * cosine - second * sine, second * cosine + first * sine], axis=-1
    )


def rotate_back(grad, cosine, sine):
    half = grad.shape[-1] // 2
    first = grad[..., :half]
    second = grad[..., half:]
    return jnp.concatenate(
        [first * cosine + second * sine, second * cosine - first * sine], axis=-1
    )


def block_masks(local_ids, prior_id):
    count = local_ids.shape[1]
    order = jnp.arange(count)
    pair = (order[:, None] >= order[None, :])[None] & (
        local_ids[:, :, None] == local_ids[:, None, :]
    )
    inbound = (local_ids == prior_id[:, None]).astype(jnp.float32)
    outbound = (local_ids == local_ids[:, -1:]).astype(jnp.float32)
    return (pair, inbound, outbound)


def block_summary(xs, bmat, step, a_log, inbound, outbound):
    decay = jnp.cumsum(step * -jnp.exp(a_log), axis=1)
    tail = jnp.exp(decay[:, -1:, :] - decay) * outbound[:, :, None] * step
    state_out = jnp.einsum("suh,suhp,sun->shpn", tail, xs, bmat, precision=lax.Precision.HIGHEST)
    carry = jnp.exp(decay[:, -1, :]) * inbound[:, -1:]
    return (state_out, carry)


def block_output(xs, bmat, cmat, step, a_log, d_skip, state_in, pair, inbound):
    decay = jnp.cumsum(step * -jnp.exp(a_log), axis=1)
    spread = decay[:, :, None, :] - decay[:, None, :, :]
    mask = pair[:, :, :, None]
    kernel = jnp.where(mask, jnp.exp(jnp.where(mask, spread, 0.0)), 0.0)
    intersection_cb = jnp.einsum("stn,sun->stu", cmat, bmat, precision=lax.Precision.HIGHEST)
    mixed = kernel * intersection_cb[:, :, :, None] * step[:, None, :, :]
    local_part = jnp.einsum("stuh,suhp->sthp", mixed, xs, precision=lax.Precision.HIGHEST)
    entry = jnp.exp(decay) * inbound[:, :, None]
    carried = entry[:, :, :, None] * jnp.einsum(
        "stn,shpn->sthp", cmat, state_in, precision=lax.Precision.HIGHEST
    )
    return local_part + carried + d_skip[:, None] * xs


def local(
    block_in,
    segment_ids,
    mamba_z,
    mamba_x,
    mamba_bc,
    mamba_dt,
    mamba_out,
    attn_q,
    attn_kv,
    attn_out,
    ffn_gate,
    ffn_up,
    ffn_down,
    mixer_norm,
    ffn_norm,
    conv_weight,
    conv_bias,
    dt_bias,
    a_log,
    d_skip,
    inner_norm,
    grad_out,
):
    sequences, rows, width = block_in.shape
    length = segment_ids.shape[1]
    taps = conv_weight.shape[0]
    group = Q_HEADS // KV_HEADS
    inner_width = SSM_HEADS * SSM_HEAD
    total_rows = sequences * rows
    inv_root = HEAD ** (-0.5)
    offset = lax.axis_index("seq") * rows
    positions = offset + jnp.arange(rows, dtype=jnp.int32)
    local_ids = lax.dynamic_slice_in_dim(segment_ids, offset, rows, 1)
    padded_ids = jnp.concatenate(
        [jnp.full((sequences, taps - 1), -1, jnp.int32), segment_ids], axis=1
    )
    window_ids = lax.dynamic_slice_in_dim(padded_ids, offset, rows + taps - 1, 1)
    prior_id = window_ids[:, taps - 2]
    tap_masks = [
        (window_ids[:, tap : tap + rows] == local_ids).astype(jnp.float32)[:, :, None]
        for tap in range(taps)
    ]
    cosine, sine = rope_tables(positions, HEAD)
    cos_b = cosine[:, None, :]
    sin_b = sine[:, None, :]
    key_order = jnp.arange(length, dtype=jnp.int32)
    allowed = (key_order[None, None, :] <= positions[None, :, None]) & (
        segment_ids[:, None, :] == local_ids[:, :, None]
    )
    gathered = (
        lax.all_gather(mamba_z, ("dp", "seq"), axis=0, tiled=True),
        lax.all_gather(mamba_x, ("dp", "seq"), axis=0, tiled=True),
        lax.all_gather(mamba_bc, ("dp", "seq"), axis=0, tiled=True),
        lax.all_gather(mamba_dt, ("dp", "seq"), axis=0, tiled=True),
        lax.all_gather(mamba_out, ("dp", "seq"), axis=0, tiled=True),
        lax.all_gather(attn_q, ("dp", "seq"), axis=0, tiled=True),
        lax.all_gather(attn_kv, ("dp", "seq"), axis=0, tiled=True),
        lax.all_gather(attn_out, ("dp", "seq"), axis=0, tiled=True),
        lax.all_gather(ffn_gate, ("dp", "seq"), axis=0, tiled=True),
        lax.all_gather(ffn_up, ("dp", "seq"), axis=0, tiled=True),
        lax.all_gather(ffn_down, ("dp", "seq"), axis=0, tiled=True),
        lax.all_gather(mixer_norm, ("dp", "seq"), axis=0, tiled=True),
        lax.all_gather(ffn_norm, ("dp", "seq"), axis=0, tiled=True),
    )
    (
        full_z,
        full_x,
        full_bc,
        full_dt,
        full_mout,
        full_q,
        full_kv,
        full_o,
        full_gate,
        full_up,
        full_down,
        gain_raw,
        gain_ffn_raw,
    ) = gathered
    gain_one = gain_raw.astype(jnp.float32)
    gain_two = gain_ffn_raw.astype(jnp.float32)
    x_in = block_in.reshape(total_rows, width).astype(jnp.float32)
    normed, factor_one = rms_forward(x_in, gain_one)
    normed_b = normed.astype(jnp.bfloat16)
    gate_z = matmul(normed_b, full_z)
    inner_u = jnp.concatenate([matmul(normed_b, full_x), matmul(normed_b, full_bc)], axis=1)
    step_raw = matmul(normed_b, full_dt)
    channels = inner_u.shape[1]
    conv_in = inner_u.reshape(sequences, rows, channels)
    edge_in = passed_along(conv_in[:, rows - taps + 1 :, :], "seq", 1)
    extended = jnp.concatenate([edge_in, conv_in], axis=1)
    conv_pre = jnp.zeros_like(conv_in) + conv_bias
    for tap in range(taps):
        conv_pre = conv_pre + conv_weight[tap] * extended[:, tap : tap + rows] * tap_masks[tap]
    activated = jax.nn.silu(conv_pre)
    xs = activated[:, :, :inner_width].reshape(sequences, rows, SSM_HEADS, SSM_HEAD)
    bmat = activated[:, :, inner_width : inner_width + STATE]
    cmat = activated[:, :, inner_width + STATE :]
    step = jax.nn.softplus(step_raw + dt_bias).reshape(sequences, rows, SSM_HEADS)
    pair, inbound, outbound = block_masks(local_ids, prior_id)
    state_local, carry = block_summary(xs, bmat, step, a_log, inbound, outbound)
    outgoing = state_local
    incoming = jnp.zeros_like(state_local)
    for hop in range(lax.axis_size("seq") - 1):
        incoming = passed_along(outgoing.astype(jnp.bfloat16), "seq", 1).astype(outgoing.dtype)
        outgoing = carry[:, :, None, None] * incoming + state_local
    ssm_out = block_output(xs, bmat, cmat, step, a_log, d_skip, incoming, pair, inbound)
    silu_z = jax.nn.silu(gate_z)
    gated = ssm_out.reshape(total_rows, inner_width) * silu_z
    mixed_norm, factor_m = rms_forward(gated, inner_norm)
    mixed_b = mixed_norm.astype(jnp.bfloat16)
    mixer_a = matmul_nt(mixed_b, full_mout)
    query = matmul(normed_b, full_q).reshape(sequences, rows, Q_HEADS, HEAD)
    keyval = matmul(normed_b, full_kv).reshape(sequences, rows, 2 * KV_HEADS, HEAD)
    query_b = rotate(query, cos_b, sin_b).astype(jnp.bfloat16)
    keys_local = rotate(keyval[:, :, :KV_HEADS], cos_b, sin_b)
    kv_local = jnp.concatenate([keys_local, keyval[:, :, KV_HEADS:]], axis=2).astype(jnp.bfloat16)
    kv_all = lax.all_gather(
        kv_local.reshape(sequences, rows, 2 * KV_HEADS * HEAD), "seq", axis=1, tiled=True
    )
    kv_all = kv_all.reshape(sequences, length, 2 * KV_HEADS, HEAD)
    keys = kv_all[:, :, :KV_HEADS]
    values = kv_all[:, :, KV_HEADS:]
    query_g = query_b.reshape(sequences, rows, KV_HEADS, group, HEAD)

    def attention_scores():
        raw = (
            jnp.einsum("stkgd,slkd->skgtl", query_g, keys, preferred_element_type=jnp.float32)
            * inv_root
        )
        return jnp.where(allowed[:, None, None], raw, -1e30)

    scores = attention_scores()
    top = jnp.max(scores, axis=-1, keepdims=True)
    lse = top + jnp.log(jnp.sum(jnp.exp(scores - top), axis=-1, keepdims=True))
    probs_b = jnp.exp(scores - lse).astype(jnp.bfloat16)
    attended = jnp.einsum("skgtl,slkd->stkgd", probs_b, values, preferred_element_type=jnp.float32)
    attended_b = attended.reshape(total_rows, Q_HEADS * HEAD).astype(jnp.bfloat16)
    attn_a = matmul_nt(attended_b, full_o)
    mid = x_in + mixer_a + attn_a
    fnormed, factor_two = rms_forward(mid, gain_two)
    fnormed_b = fnormed.astype(jnp.bfloat16)
    gate_h = matmul(fnormed_b, full_gate)
    up_h = matmul(fnormed_b, full_up)
    hidden_b = (jax.nn.silu(gate_h) * up_h).astype(jnp.bfloat16)
    block_out = (
        (mid + matmul_nt(hidden_b, full_down)).astype(jnp.bfloat16).reshape(sequences, rows, width)
    )
    regathered = (
        lax.all_gather(mamba_z, ("dp", "seq"), axis=0, tiled=True),
        lax.all_gather(mamba_x, ("dp", "seq"), axis=0, tiled=True),
        lax.all_gather(mamba_bc, ("dp", "seq"), axis=0, tiled=True),
        lax.all_gather(mamba_dt, ("dp", "seq"), axis=0, tiled=True),
        lax.all_gather(mamba_out, ("dp", "seq"), axis=0, tiled=True),
        lax.all_gather(attn_q, ("dp", "seq"), axis=0, tiled=True),
        lax.all_gather(attn_kv, ("dp", "seq"), axis=0, tiled=True),
        lax.all_gather(attn_out, ("dp", "seq"), axis=0, tiled=True),
        lax.all_gather(ffn_gate, ("dp", "seq"), axis=0, tiled=True),
        lax.all_gather(ffn_up, ("dp", "seq"), axis=0, tiled=True),
        lax.all_gather(ffn_down, ("dp", "seq"), axis=0, tiled=True),
        lax.all_gather(mixer_norm, ("dp", "seq"), axis=0, tiled=True),
        lax.all_gather(ffn_norm, ("dp", "seq"), axis=0, tiled=True),
    )
    (
        back_z,
        back_x,
        back_bc,
        back_dt,
        back_mout,
        back_q,
        back_kv,
        back_o,
        back_gate,
        back_up,
        back_down,
        back_gain,
        back_gain_ffn,
    ) = regathered
    gain_one_b = back_gain.astype(jnp.float32)
    gain_two_b = back_gain_ffn.astype(jnp.float32)
    grad_flat = grad_out.reshape(total_rows, width)
    g_down = matmul_tn(grad_flat, hidden_b)
    d_hidden = matmul(grad_flat, back_down)
    d_gate_b = (d_hidden * up_h * silu_grad(gate_h)).astype(jnp.bfloat16)
    d_up_b = (d_hidden * jax.nn.silu(gate_h)).astype(jnp.bfloat16)
    g_gate = matmul_tn(fnormed_b, d_gate_b)
    g_up = matmul_tn(fnormed_b, d_up_b)
    d_fnorm = matmul_nt(d_gate_b, back_gate) + matmul_nt(d_up_b, back_up)
    d_mid_norm, g_fnorm = rms_backward(mid, factor_two, gain_two_b, d_fnorm)
    d_mid = grad_flat.astype(jnp.float32) + d_mid_norm
    d_mid_b = d_mid.astype(jnp.bfloat16)
    g_mout = matmul_tn(d_mid_b, mixed_b)
    d_mnorm = matmul(d_mid_b, back_mout)
    d_gated, g_inner = rms_backward(gated, factor_m, inner_norm, d_mnorm)
    d_ssm = (d_gated * silu_z).reshape(sequences, rows, SSM_HEADS, SSM_HEAD)
    d_z = d_gated * ssm_out.reshape(total_rows, inner_width) * silu_grad(gate_z)
    entry = jnp.exp(jnp.cumsum(step * -jnp.exp(a_log), axis=1)) * inbound[:, :, None]
    direct = jnp.einsum("sth,sthp,stn->shpn", entry, d_ssm, cmat, precision=lax.Precision.HIGHEST)
    backlog = direct
    later_grad = jnp.zeros_like(direct)
    for hop in range(lax.axis_size("seq") - 1):
        later_grad = passed_along(backlog.astype(jnp.bfloat16), "seq", -1).astype(backlog.dtype)
        backlog = direct + carry[:, :, None, None] * later_grad
    d_carry = jnp.sum(later_grad * incoming, axis=(2, 3))

    def local_ssm(xs_a, bmat_a, cmat_a, step_a, alog_a, skip_a):
        result = block_output(xs_a, bmat_a, cmat_a, step_a, alog_a, skip_a, incoming, pair, inbound)
        summary, carry_a = block_summary(xs_a, bmat_a, step_a, alog_a, inbound, outbound)
        return (result, summary, carry_a)

    primal, pullback = jax.vjp(local_ssm, xs, bmat, cmat, step, a_log, d_skip)
    d_xs, d_bmat, d_cmat, d_step, g_alog, g_skip = pullback((d_ssm, later_grad, d_carry))
    d_act = jnp.concatenate([d_xs.reshape(sequences, rows, inner_width), d_bmat, d_cmat], axis=2)
    d_pre = d_act * silu_grad(conv_pre)
    g_cbias = jnp.sum(d_pre, axis=(0, 1))
    g_cweight = jnp.stack(
        [
            jnp.sum(d_pre * extended[:, tap : tap + rows] * tap_masks[tap], axis=(0, 1))
            for tap in range(taps)
        ]
    )
    d_padded = jnp.zeros_like(extended)
    for tap in range(taps):
        d_padded = d_padded + jnp.pad(
            d_pre * tap_masks[tap] * conv_weight[tap], ((0, 0), (tap, taps - 1 - tap), (0, 0))
        )
    edge_grad = passed_along(d_padded[:, : taps - 1], "seq", -1)
    d_inner = d_padded[:, taps - 1 :] + jnp.pad(edge_grad, ((0, 0), (rows - taps + 1, 0), (0, 0)))
    d_inner = d_inner.reshape(total_rows, channels)
    d_step_raw = d_step.reshape(total_rows, SSM_HEADS) * jax.nn.sigmoid(step_raw + dt_bias)
    g_dtb = jnp.sum(d_step_raw, axis=0)
    d_att_b = matmul(d_mid_b, back_o).astype(jnp.bfloat16)
    g_aout = matmul_tn(d_mid_b, attended_b)
    d_att_g = d_att_b.reshape(sequences, rows, KV_HEADS, group, HEAD)
    probs = jnp.exp(attention_scores() - lse)
    d_probs = jnp.einsum("stkgd,slkd->skgtl", d_att_g, values, preferred_element_type=jnp.float32)
    d_scores_b = (probs * (d_probs - jnp.sum(probs * d_probs, axis=-1, keepdims=True))).astype(
        jnp.bfloat16
    )
    d_query = (
        jnp.einsum("skgtl,slkd->stkgd", d_scores_b, keys, preferred_element_type=jnp.float32)
        * inv_root
    )
    d_keys = (
        jnp.einsum("skgtl,stkgd->slkd", d_scores_b, query_g, preferred_element_type=jnp.float32)
        * inv_root
    )
    d_values = jnp.einsum("skgtl,stkgd->slkd", probs_b, d_att_g, preferred_element_type=jnp.float32)
    d_kv_all = jnp.concatenate([d_keys, d_values], axis=2).reshape(
        sequences, length, 2 * KV_HEADS * HEAD
    )
    d_kv_local = (
        lax.psum_scatter(d_kv_all.astype(jnp.bfloat16), "seq", scatter_dimension=1, tiled=True)
        .astype(jnp.float32)
        .reshape(sequences, rows, 2 * KV_HEADS, HEAD)
    )
    d_key_local = rotate_back(d_kv_local[:, :, :KV_HEADS], cos_b, sin_b)
    d_kv_b = (
        jnp.concatenate([d_key_local, d_kv_local[:, :, KV_HEADS:]], axis=2)
        .reshape(total_rows, 2 * KV_HEADS * HEAD)
        .astype(jnp.bfloat16)
    )
    d_q_b = (
        rotate_back(d_query.reshape(sequences, rows, Q_HEADS, HEAD), cos_b, sin_b)
        .reshape(total_rows, Q_HEADS * HEAD)
        .astype(jnp.bfloat16)
    )
    d_z_b = d_z.astype(jnp.bfloat16)
    d_x_b = d_inner[:, :inner_width].astype(jnp.bfloat16)
    d_bc_b = d_inner[:, inner_width:].astype(jnp.bfloat16)
    d_st_b = d_step_raw.astype(jnp.bfloat16)
    g_z = matmul_tn(normed_b, d_z_b)
    g_x = matmul_tn(normed_b, d_x_b)
    g_bc = matmul_tn(normed_b, d_bc_b)
    g_dt = matmul_tn(normed_b, d_st_b)
    g_q = matmul_tn(normed_b, d_q_b)
    g_kv = matmul_tn(normed_b, d_kv_b)
    d_norm = matmul_nt(d_z_b, back_z) + matmul_nt(d_x_b, back_x) + matmul_nt(d_bc_b, back_bc)
    d_norm = (
        d_norm + matmul_nt(d_st_b, back_dt) + matmul_nt(d_q_b, back_q) + matmul_nt(d_kv_b, back_kv)
    )
    d_in_norm, g_mnorm = rms_backward(x_in, factor_one, gain_one_b, d_norm)
    grad_in = (d_mid + d_in_norm).astype(jnp.bfloat16).reshape(sequences, rows, width)
    owned = (
        lax.psum_scatter(g_z, ("dp", "seq"), scatter_dimension=0, tiled=True),
        lax.psum_scatter(g_x, ("dp", "seq"), scatter_dimension=0, tiled=True),
        lax.psum_scatter(g_bc, ("dp", "seq"), scatter_dimension=0, tiled=True),
        lax.psum_scatter(g_dt, ("dp", "seq"), scatter_dimension=0, tiled=True),
        lax.psum_scatter(g_mout, ("dp", "seq"), scatter_dimension=0, tiled=True),
        lax.psum_scatter(g_q, ("dp", "seq"), scatter_dimension=0, tiled=True),
        lax.psum_scatter(g_kv, ("dp", "seq"), scatter_dimension=0, tiled=True),
        lax.psum_scatter(g_aout, ("dp", "seq"), scatter_dimension=0, tiled=True),
        lax.psum_scatter(g_gate, ("dp", "seq"), scatter_dimension=0, tiled=True),
        lax.psum_scatter(g_up, ("dp", "seq"), scatter_dimension=0, tiled=True),
        lax.psum_scatter(g_down, ("dp", "seq"), scatter_dimension=0, tiled=True),
        lax.psum_scatter(g_mnorm, ("dp", "seq"), scatter_dimension=0, tiled=True),
        lax.psum_scatter(g_fnorm, ("dp", "seq"), scatter_dimension=0, tiled=True),
    )
    summed = lax.psum((g_cweight, g_cbias, g_dtb, g_alog, g_skip, g_inner), ("dp", "seq"))
    return (
        block_out,
        grad_in,
        owned[0],
        owned[1],
        owned[2],
        owned[3],
        owned[4],
        owned[5],
        owned[6],
        owned[7],
        owned[8],
        owned[9],
        owned[10],
        owned[11],
        owned[12],
        summed[0],
        summed[1],
        summed[2],
        summed[3],
        summed[4],
        summed[5],
    )


def solution(mesh):
    in_specs = (
        P("dp", "seq", None),
        P("dp", None),
        P(("dp", "seq"), None),
        P(("dp", "seq"), None),
        P(("dp", "seq"), None),
        P(("dp", "seq"), None),
        P(("dp", "seq"), None),
        P(("dp", "seq"), None),
        P(("dp", "seq"), None),
        P(("dp", "seq"), None),
        P(("dp", "seq"), None),
        P(("dp", "seq"), None),
        P(("dp", "seq"), None),
        P(("dp", "seq")),
        P(("dp", "seq")),
        P(),
        P(),
        P(),
        P(),
        P(),
        P(),
        P("dp", "seq", None),
    )
    out_specs = (
        P("dp", "seq", None),
        P("dp", "seq", None),
        P(("dp", "seq"), None),
        P(("dp", "seq"), None),
        P(("dp", "seq"), None),
        P(("dp", "seq"), None),
        P(("dp", "seq"), None),
        P(("dp", "seq"), None),
        P(("dp", "seq"), None),
        P(("dp", "seq"), None),
        P(("dp", "seq"), None),
        P(("dp", "seq"), None),
        P(("dp", "seq"), None),
        P(("dp", "seq")),
        P(("dp", "seq")),
        P(),
        P(),
        P(),
        P(),
        P(),
        P(),
    )
    return jax.shard_map(local, mesh=mesh, in_specs=in_specs, out_specs=out_specs, check_vma=False)
```

profile of v0, /device:TPU:0, one launch (start us, length us, event | category | flops | bytes accessed | tf_op | source)
XLA Modules:
  0.0 2234.4 jit_solution(12320917414109699205)
XLA Ops:
  15.0 42.0 %all-reduce.13 = (bf16[1024]{0:T(1024)(128)(2,1)S(1)}, bf16[1024]{0:T(1024)(128)(2,1)S(1)}) all-reduce(bf16[1024]{0:T(1024)(128)(2,1)S(1)} %dynamic-update-slice, bf16[1024]{0:T(1024)(128)(2,1)S(1)} %dynamic-update-slice.1), channel_id=1, replica_groups=mesh['dp'=8,'seq'=4] {'dp','seq'}, use_global_device_ids=true, to_apply=%add.8 | all-reduce | flops 2048 | bytes 8192
  58.2 72.5 %all_gather.61 = bf16[1024,256]{1,0:T(8,128)(2,1)S(1)} all-gather(bf16[32,256]{1,0:T(8,128)(2,1)} %param.30), channel_id=1, replica_groups=mesh['dp'=8,'seq'=4] {'dp','seq'}, dimensions={0}, use_global_device_ids=true | all-gather | bytes 540672 | tf_op jit(solution)/shard_map/all_gather | solution.py:175
  131.7 16.2 all_gather.62
  149.2 69.5 %all_gather.57 = bf16[1024,256]{1,0:T(8,128)(2,1)S(1)} all-gather(bf16[32,256]{1,0:T(8,128)(2,1)S(1)} %copy-done.130), channel_id=1, replica_groups=mesh['dp'=8,'seq'=4] {'dp','seq'}, dimensions={0}, use_global_device_ids=true | all-gather | bytes 540672 | tf_op jit(solution)/shard_map/all_gather | solution.py:171
  219.8 67.6 %all-gather = bf16[32,32,24]{1,2,0:T(8,128)(2,1)S(1)} all-gather(bf16[1,32,24]{1,2,0:T(8,128)(2,1)S(1)} %bitcast.614), channel_id=1, replica_groups=mesh['dp'=8,'seq'=4] {'dp','seq'}, dimensions={0}, use_global_device_ids=true | all-gather | bytes 50688 | tf_op jit(solution)/shard_map/all_gather | solution.py:172
  336.9 12.4 collective-permute-done.2
  358.0 9.4 collective-permute-done.3
  398.9 37.5 %all-gather.22.cloned.1.call-done = bf16[1024,2048]{1,0:T(8,128)(2,1)} async-done(((bf16[32,2048]{1,0:T(8,128)(2,1)}), bf16[1024,2048]{1,0:T(8,128)(2,1)}) %all-gather.22.cloned.1.call-update) | async-done | bytes 4194320 | tf_op jit(solution)/shard_map/all_gather | solution.py:178
  441.4 58.4 %all-gather.24.cloned.1.call-done = bf16[1024,2048]{1,0:T(8,128)(2,1)} async-done(((bf16[32,2048]{1,0:T(8,128)(2,1)}), bf16[1024,2048]{1,0:T(8,128)(2,1)}) %all-gather.24.cloned.1.call-update) | async-done | bytes 4194320 | tf_op jit(solution)/shard_map/all_gather | solution.py:179
  545.1 10.9 fusion.12
  577.3 15.6 collective-permute-done.5
  623.1 9.0 bitcast_add_fusion
  694.7 9.2 copy.207
  717.2 41.0 %all-reduce.12 = (f32[1024]{0:T(1024)S(1)}, f32[1024]{0:T(1024)S(1)}, f32[4,1792]{1,0:T(4,128)}, f32[1792]{0:T(1024)}, f32[24]{0:T(128)}, /*index=5*/f32[24]{0:T(128)}, f32[24]{0:T(128)}, f32[1536]{0:T(1024)}) all-reduce(f32[1024]{0:T(1024)S(1)} %get-tuple-element.121, ...), channel_id=14, replica_groups=mesh['dp'=8,'seq'=4] {'dp','seq'}, use_global_device_ids=true, to_apply=%region_35.36.clone | all-reduce | flops 12616 | bytes 100928
  763.5 129.2 %reduce-scatter.29.cloned.1.call-done = f32[32,256]{1,0:T(8,128)} async-done(((f32[1024,256]{1,0:T(8,128)}), f32[32,256]{1,0:T(8,128)}) %reduce-scatter.29.cloned.1.call-update) | async-done | bytes 32784 | tf_op jit(solution)/shard_map/reduce_scatter | solution.py:409
  892.8 136.3 %reduce-scatter.23.cloned.1.call-done = f32[32,256]{1,0:T(8,128)} async-done(((f32[1024,256]{1,0:T(8,128)}), f32[32,256]{1,0:T(8,128)}) %reduce-scatter.23.cloned.1.call-update) | async-done | bytes 32784 | tf_op jit(solution)/shard_map/reduce_scatter | solution.py:405
  1029.0 139.2 %reduce-scatter.31.cloned.1.call-done = f32[32,512]{1,0:T(8,128)} async-done(((f32[1024,512]{1,0:T(8,128)}), f32[32,512]{1,0:T(8,128)}) %reduce-scatter.31.cloned.1.call-update) | async-done | bytes 65552 | tf_op jit(solution)/shard_map/reduce_scatter | solution.py:410
  1168.2 140.3 %reduce-scatter.27.cloned.1.call-done = f32[32,512]{1,0:T(8,128)} async-done(((f32[1024,512]{1,0:T(8,128)}), f32[32,512]{1,0:T(8,128)}) %reduce-scatter.27.cloned.1.call-update) | async-done | bytes 65552 | tf_op jit(solution)/shard_map/reduce_scatter | solution.py:408
  1308.5 118.7 %reduce-scatter.25.cloned.1.call-done = f32[32,1536]{1,0:T(8,128)} async-done(((f32[1024,1536]{1,0:T(8,128)}), f32[32,1536]{1,0:T(8,128)}) %reduce-scatter.25.cloned.1.call-update) | async-done | bytes 196624 | tf_op jit(solution)/shard_map/reduce_scatter | solution.py:407
  1427.2 120.1 %reduce-scatter.19.cloned.1.call-done = f32[32,1536]{1,0:T(8,128)} async-done(((f32[1024,1536]{1,0:T(8,128)}), f32[32,1536]{1,0:T(8,128)}) %reduce-scatter.19.cloned.1.call-update) | async-done | bytes 196624 | tf_op jit(solution)/shard_map/reduce_scatter | solution.py:403
  1547.3 120.0 %reduce-scatter.21.cloned.1.call-done = f32[32,1536]{1,0:T(8,128)} async-done(((f32[1024,1536]{1,0:T(8,128)}), f32[32,1536]{1,0:T(8,128)}) %reduce-scatter.21.cloned.1.call-update) | async-done | bytes 196624 | tf_op jit(solution)/shard_map/reduce_scatter | solution.py:404
  1667.2 187.5 %reduce-scatter.33.cloned.1.call-done = f32[32,2048]{1,0:T(8,128)} async-done(((f32[1024,2048]{1,0:T(8,128)}), f32[32,2048]{1,0:T(8,128)}) %reduce-scatter.33.cloned.1.call-update) | async-done | bytes 262160 | tf_op jit(solution)/shard_map/reduce_scatter | solution.py:411
  1854.7 186.3 %reduce-scatter.35.cloned.1.call-done = f32[32,2048]{1,0:T(8,128)} async-done(((f32[1024,2048]{1,0:T(8,128)}), f32[32,2048]{1,0:T(8,128)}) %reduce-scatter.35.cloned.1.call-update) | async-done | bytes 262160 | tf_op jit(solution)/shard_map/reduce_scatter | solution.py:412
  2041.0 186.2 %reduce-scatter.39.cloned.1.call-done = f32[32,2048]{1,0:T(8,128)} async-done(((f32[1024,2048]{1,0:T(8,128)}), f32[32,2048]{1,0:T(8,128)}) %reduce-scatter.39.cloned.1.call-update) | async-done | bytes 262160
  (561 shorter events, 282.5 us)
Async XLA Ops:
  7.2 290.0 %all-gather.16.cloned.1.call-start = ((), (), s32[]{:S(2)}) async-start(), calls=%async_computation.15 | async-start | bytes 1081344 | tf_op jit(solution)/shard_map/all_gather | solution.py:174
  7.9 291.4 %all-gather.10.cloned.1.call-start = ((), (), s32[]{:S(2)}) async-start(), calls=%async_computation.12 | async-start | bytes 3244032 | tf_op jit(solution)/shard_map/all_gather | solution.py:170
  8.7 372.4 %all-gather.12.cloned.1.call-start = ((), (), s32[]{:S(2)}) async-start(), calls=%async_computation.13 | async-start | bytes 3244032 | tf_op jit(solution)/shard_map/all_gather | solution.py:169
  9.4 376.9 %all-gather.14.cloned.1.call-start = ((), (), s32[]{:S(2)}) async-start(), calls=%async_computation.14 | async-start | bytes 3244032 | tf_op jit(solution)/shard_map/all_gather | solution.py:173
  10.0 380.8 %all-gather.18.cloned.1.call-start = ((), (), s32[]{:S(2)}) async-start(), calls=%async_computation.16 | async-start | bytes 1081344 | tf_op jit(solution)/shard_map/all_gather | solution.py:176
  10.6 383.3 %all-gather.20.cloned.1.call-start = ((), (), s32[]{:S(2)}) async-start(), calls=%async_computation.17 | async-start | bytes 4325376 | tf_op jit(solution)/shard_map/all_gather | solution.py:177
  11.2 425.3 %all-gather.22.cloned.1.call-start = ((), (), s32[]{:S(2)}) async-start(), calls=%async_computation.18 | async-start | bytes 4325376 | tf_op jit(solution)/shard_map/all_gather | solution.py:178
  11.9 487.9 %all-gather.24.cloned.1.call-start = ((), (), s32[]{:S(2)}) async-start(), calls=%async_computation.19 | async-start | bytes 4325376 | tf_op jit(solution)/shard_map/all_gather | solution.py:179
  12.7 584.7 %reduce-scatter.17.cloned.1.call-start = ((), (), s32[]{:S(2)}) async-start(), calls=%async_computation.20 | async-start | bytes 655360 | tf_op jit(solution)/shard_map/reduce_scatter | solution.py:371
  330.5 18.7 collective-permute-start.2
  349.4 18.0 collective-permute-start.3
  543.7 26.1 %collective-permute-start.4 = (bf16[1,24,64,128]{3,2,1,0:T(8,128)(2,1)}, bf16[1,24,64,128]{3,2,1,0:T(8,128)(2,1)}, u32[]{:S(2)}, u32[]{:S(2)}) collective-permute-start(bf16[1,24,64,128]{3,2,1,0:T(8,128)(2,1)} %convert_bitcast_fusion.1), channel_id=1, source_target_pairs={{1,0},{2,1},{3,2},{5,4},{6,5},{7,6},{9,8},{10,9},{11,10},{13,12},{... | collective-permute-start | bytes 1179656 | tf_op jit(solution)/shard_map/ppermute | solution.py:21
  568.4 193.7 %reduce-scatter.37.cloned.1.call-start = ((), (), s32[]{:S(2)}) async-start(), calls=%async_computation.30 | async-start | bytes 540672
  571.4 21.5 collective-permute-start.5
  621.2 271.5 %reduce-scatter.29.cloned.1.call-start = ((), (), s32[]{:S(2)}) async-start(), calls=%async_computation.26 | async-start | bytes 1081344 | tf_op jit(solution)/shard_map/reduce_scatter | solution.py:409
  622.8 406.2 %reduce-scatter.23.cloned.1.call-start = ((), (), s32[]{:S(2)}) async-start(), calls=%async_computation.23 | async-start | bytes 1081344 | tf_op jit(solution)/shard_map/reduce_scatter | solution.py:405
  653.4 514.8 %reduce-scatter.31.cloned.1.call-start = ((), (), s32[]{:S(2)}) async-start(), calls=%async_computation.27 | async-start | bytes 2162688 | tf_op jit(solution)/shard_map/reduce_scatter | solution.py:410
  655.3 653.2 %reduce-scatter.27.cloned.1.call-start = ((), (), s32[]{:S(2)}) async-start(), calls=%async_computation.25 | async-start | bytes 2162688 | tf_op jit(solution)/shard_map/reduce_scatter | solution.py:408
  660.5 766.7 %reduce-scatter.25.cloned.1.call-start = ((), (), s32[]{:S(2)}) async-start(), calls=%async_computation.24 | async-start | bytes 6488064 | tf_op jit(solution)/shard_map/reduce_scatter | solution.py:407
  665.3 882.0 %reduce-scatter.19.cloned.1.call-start = ((), (), s32[]{:S(2)}) async-start(), calls=%async_computation.21 | async-start | bytes 6488064 | tf_op jit(solution)/shard_map/reduce_scatter | solution.py:403
  670.3 997.0 %reduce-scatter.21.cloned.1.call-start = ((), (), s32[]{:S(2)}) async-start(), calls=%async_computation.22 | async-start | bytes 6488064 | tf_op jit(solution)/shard_map/reduce_scatter | solution.py:404
  675.1 1179.6 %reduce-scatter.33.cloned.1.call-start = ((), (), s32[]{:S(2)}) async-start(), calls=%async_computation.28 | async-start | bytes 8650752 | tf_op jit(solution)/shard_map/reduce_scatter | solution.py:411
  682.0 1359.0 %reduce-scatter.35.cloned.1.call-start = ((), (), s32[]{:S(2)}) async-start(), calls=%async_computation.29 | async-start | bytes 8650752 | tf_op jit(solution)/shard_map/reduce_scatter | solution.py:412
  687.9 1539.2 %reduce-scatter.39.cloned.1.call-start = ((), (), s32[]{:S(2)}) async-start(), calls=%async_computation.31 | async-start | bytes 8650752
  (168 other events, 3070.9 us)
Sparse Core Ops, SparseCore 0:
  11.0 56.6 all-gather.15
  70.6 59.0 all-gather.9
  132.5 58.5 all-gather.11
  193.9 58.5 all-gather.13
  255.3 52.5 all-gather.17
  310.8 61.7 all-gather.19
  375.6 60.7 all-gather.21
  439.4 60.4 all-gather.23
  568.5 27.6 reduce-scatter.16
  621.3 135.0 reduce-scatter.36
  759.2 133.4 reduce-scatter.28
  895.4 133.5 reduce-scatter.22
  1031.8 136.3 reduce-scatter.30
  1170.9 137.5 reduce-scatter.26
  1314.6 112.6 reduce-scatter.24
  1433.3 113.9 reduce-scatter.18
  1553.3 113.8 reduce-scatter.20
  1669.9 184.7 reduce-scatter.32
  1857.6 183.3 reduce-scatter.34
  2043.7 183.4 reduce-scatter.38
where the time goes:
time: 2240 us; the launch traced here: 2230 us
  waiting for transfers between devices  1620 us (72%)
  blocking collectives  309 us (14%)
  matrix products  160 us (7%)
  local copies, waits for them, and re-layouts  52.2 us (2%)
  other arithmetic  52.1 us (2%)
    unnamed x22, waiting for transfers between devices  191 us
    reduce_scatter x1, waiting for transfers between devices, local(): lax.psum_scatter(g_gate, ('dp', 'seq'), scatter_dimension=0, tiled=True)  187 us
    reduce_scatter x1, waiting for transfers between devices, local(): lax.psum_scatter(g_up, ('dp', 'seq'), scatter_dimension=0, tiled=True)  186 us
    reduce_scatter x1, waiting for transfers between devices, local(): lax.psum_scatter(g_q, ('dp', 'seq'), scatter_dimension=0, tiled=True)  140 us
    reduce_scatter x1, waiting for transfers between devices, local(): lax.psum_scatter(g_aout, ('dp', 'seq'), scatter_dimension=0, tiled=True)  139 us
    reduce_scatter x1, waiting for transfers between devices, local(): lax.psum_scatter(g_bc, ('dp', 'seq'), scatter_dimension=0, tiled=True)  136 us
    reduce_scatter x1, waiting for transfers between devices, local(): lax.psum_scatter(g_kv, ('dp', 'seq'), scatter_dimension=0, tiled=True)  129 us
    reduce_scatter x1, waiting for transfers between devices, local(): lax.psum_scatter(g_z, ('dp', 'seq'), scatter_dimension=0, tiled=True)  120 us
  transfers between devices with their start and end apart: 28, of which 19 were waited for; matrix products, arithmetic and copies ran while one was open for 9% of the time, Pallas kernels for 0%

commit v1 on v0

--- a/solution.py
+++ b/solution.py
@@ -13,12 +13,19 @@
 
 EPSILON = 1e-05
 ROPE_BASE = 100000000000.0
+MAX_DOC = 512
+LANES = 128
 
 
 def passed_along(block, axis, distance):
     devices = range(lax.axis_size(axis))
     route = [(i - distance, i) for i in devices if i - distance in devices]
     return lax.ppermute(block, axis, route)
+
+
+def scattered(grad):
+    part = lax.psum_scatter(grad, "dp", scatter_dimension=0, tiled=True)
+    return lax.psum_scatter(part, "seq", scatter_dimension=0, tiled=True).astype(jnp.float32)
 
 
 def silu_grad(value):
@@ -161,48 +168,58 @@
     cosine, sine = rope_tables(positions, HEAD)
     cos_b = cosine[:, None, :]
     sin_b = sine[:, None, :]
-    key_order = jnp.arange(length, dtype=jnp.int32)
-    allowed = (key_order[None, None, :] <= positions[None, :, None]) & (
-        segment_ids[:, None, :] == local_ids[:, :, None]
-    )
-    gathered = (
-        lax.all_gather(mamba_z, ("dp", "seq"), axis=0, tiled=True),
-        lax.all_gather(mamba_x, ("dp", "seq"), axis=0, tiled=True),
-        lax.all_gather(mamba_bc, ("dp", "seq"), axis=0, tiled=True),
-        lax.all_gather(mamba_dt, ("dp", "seq"), axis=0, tiled=True),
-        lax.all_gather(mamba_out, ("dp", "seq"), axis=0, tiled=True),
-        lax.all_gather(attn_q, ("dp", "seq"), axis=0, tiled=True),
-        lax.all_gather(attn_kv, ("dp", "seq"), axis=0, tiled=True),
-        lax.all_gather(attn_out, ("dp", "seq"), axis=0, tiled=True),
-        lax.all_gather(ffn_gate, ("dp", "seq"), axis=0, tiled=True),
-        lax.all_gather(ffn_up, ("dp", "seq"), axis=0, tiled=True),
-        lax.all_gather(ffn_down, ("dp", "seq"), axis=0, tiled=True),
-        lax.all_gather(mixer_norm, ("dp", "seq"), axis=0, tiled=True),
-        lax.all_gather(ffn_norm, ("dp", "seq"), axis=0, tiled=True),
-    )
-    (
-        full_z,
-        full_x,
-        full_bc,
-        full_dt,
-        full_mout,
-        full_q,
-        full_kv,
-        full_o,
-        full_gate,
-        full_up,
-        full_down,
-        gain_raw,
-        gain_ffn_raw,
-    ) = gathered
-    gain_one = gain_raw.astype(jnp.float32)
-    gain_two = gain_ffn_raw.astype(jnp.float32)
+    behind = min(lax.axis_size("seq") - 1, (MAX_DOC - 2) // rows + 1) * rows
+    key_ids = lax.dynamic_slice_in_dim(
+        jnp.concatenate([jnp.full((sequences, behind), -1, jnp.int32), segment_ids], axis=1),
+        offset,
+        behind + rows,
+        1,
+    )
+    key_order = jnp.arange(behind + rows, dtype=jnp.int32) - behind
+    allowed = (key_order[None, None, :] <= jnp.arange(rows, dtype=jnp.int32)[None, :, None]) & (
+        key_ids[:, None, :] == local_ids[:, :, None]
+    )
+    hops = min(lax.axis_size("seq") - 1, (MAX_DOC - 2) // rows + 1)
+    spare = -(mamba_dt.shape[1] + 2) % LANES
+    shard_in = jnp.concatenate(
+        [
+            mamba_z,
+            mamba_x,
+            mamba_bc,
+            attn_q,
+            attn_kv,
+            mamba_dt,
+            mixer_norm[:, None],
+            ffn_norm[:, None],
+            jnp.zeros((mixer_norm.shape[0], spare), jnp.bfloat16),
+        ],
+        axis=1,
+    )
+    shard_out = jnp.concatenate([mamba_out, attn_out, ffn_gate, ffn_up, ffn_down], axis=1)
+    full_in = lax.all_gather(shard_in, ("dp", "seq"), axis=0, tiled=True)
+    full_out = lax.all_gather(shard_out, ("dp", "seq"), axis=0, tiled=True)
+    bc_width = mamba_bc.shape[1]
+    q_width = attn_q.shape[1]
+    kv_width = attn_kv.shape[1]
+    hidden_width = ffn_gate.shape[1]
+    at_u = inner_width
+    at_q = at_u + inner_width + bc_width
+    at_kv = at_q + q_width
+    at_dt = at_kv + kv_width
+    at_gain = at_dt + SSM_HEADS
+    mixer_width = inner_width + q_width
+    full_mixer = full_out[:, :mixer_width]
+    full_gateup = full_out[:, mixer_width : mixer_width + 2 * hidden_width]
+    full_down = full_out[:, mixer_width + 2 * hidden_width :]
+    gain_one = full_in[:, at_gain].astype(jnp.float32)
+    gain_two = full_in[:, at_gain + 1].astype(jnp.float32)
     x_in = block_in.reshape(total_rows, width).astype(jnp.float32)
     normed, factor_one = rms_forward(x_in, gain_one)
     normed_b = normed.astype(jnp.bfloat16)
-    gate_z = matmul(normed_b, full_z)
-    inner_u = jnp.concatenate([matmul(normed_b, full_x), matmul(normed_b, full_bc)], axis=1)
-    step_raw = matmul(normed_b, full_dt)
+    projected = matmul(normed_b, full_in)
+    gate_z = projected[:, :at_u]
+    inner_u = projected[:, at_u:at_q]
+    step_raw = projected[:, at_dt:at_gain]
     channels = inner_u.shape[1]
     conv_in = inner_u.reshape(sequences, rows, channels)
     edge_in = passed_along(conv_in[:, rows - taps + 1 :, :], "seq", 1)
@@ -219,7 +236,7 @@
     state_local, carry = block_summary(xs, bmat, step, a_log, inbound, outbound)
     outgoing = state_local
     incoming = jnp.zeros_like(state_local)
-    for hop in range(lax.axis_size("seq") - 1):
+    for hop in range(hops):
         incoming = passed_along(outgoing.astype(jnp.bfloat16), "seq", 1).astype(outgoing.dtype)
         outgoing = carry[:, :, None, None] * incoming + state_local
     ssm_out = block_output(xs, bmat, cmat, step, a_log, d_skip, incoming, pair, inbound)
@@ -227,16 +244,17 @@
     gated = ssm_out.reshape(total_rows, inner_width) * silu_z
     mixed_norm, factor_m = rms_forward(gated, inner_norm)
     mixed_b = mixed_norm.astype(jnp.bfloat16)
-    mixer_a = matmul_nt(mixed_b, full_mout)
-    query = matmul(normed_b, full_q).reshape(sequences, rows, Q_HEADS, HEAD)
-    keyval = matmul(normed_b, full_kv).reshape(sequences, rows, 2 * KV_HEADS, HEAD)
+    query = projected[:, at_q:at_kv].reshape(sequences, rows, Q_HEADS, HEAD)
+    keyval = projected[:, at_kv:at_dt].reshape(sequences, rows, 2 * KV_HEADS, HEAD)
     query_b = rotate(query, cos_b, sin_b).astype(jnp.bfloat16)
     keys_local = rotate(keyval[:, :, :KV_HEADS], cos_b, sin_b)
     kv_local = jnp.concatenate([keys_local, keyval[:, :, KV_HEADS:]], axis=2).astype(jnp.bfloat16)
-    kv_all = lax.all_gather(
-        kv_local.reshape(sequences, rows, 2 * KV_HEADS * HEAD), "seq", axis=1, tiled=True
-    )
-    kv_all = kv_all.reshape(sequences, length, 2 * KV_HEADS, HEAD)
+    kv_flat = kv_local.reshape(sequences, rows, kv_width)
+    kv_all = jnp.concatenate(
+        [passed_along(kv_flat, "seq", far) for far in range(hops, 0, -1)] + [kv_flat], axis=1
+    )
+    window = kv_all.shape[1]
+    kv_all = kv_all.reshape(sequences, window, 2 * KV_HEADS, HEAD)
     keys = kv_all[:, :, :KV_HEADS]
     values = kv_all[:, :, KV_HEADS:]
     query_g = query_b.reshape(sequences, rows, KV_HEADS, group, HEAD)
@@ -254,61 +272,32 @@
     probs_b = jnp.exp(scores - lse).astype(jnp.bfloat16)
     attended = jnp.einsum("skgtl,slkd->stkgd", probs_b, values, preferred_element_type=jnp.float32)
     attended_b = attended.reshape(total_rows, Q_HEADS * HEAD).astype(jnp.bfloat16)
-    attn_a = matmul_nt(attended_b, full_o)
-    mid = x_in + mixer_a + attn_a
+    mixers_b = jnp.concatenate([mixed_b, attended_b], axis=1)
+    mid = x_in + matmul_nt(mixers_b, full_mixer)
     fnormed, factor_two = rms_forward(mid, gain_two)
     fnormed_b = fnormed.astype(jnp.bfloat16)
-    gate_h = matmul(fnormed_b, full_gate)
-    up_h = matmul(fnormed_b, full_up)
+    gateup_h = matmul(fnormed_b, full_gateup)
+    gate_h = gateup_h[:, :hidden_width]
+    up_h = gateup_h[:, hidden_width:]
     hidden_b = (jax.nn.silu(gate_h) * up_h).astype(jnp.bfloat16)
     block_out = (
         (mid + matmul_nt(hidden_b, full_down)).astype(jnp.bfloat16).reshape(sequences, rows, width)
     )
-    regathered = (
-        lax.all_gather(mamba_z, ("dp", "seq"), axis=0, tiled=True),
-        lax.all_gather(mamba_x, ("dp", "seq"), axis=0, tiled=True),
-        lax.all_gather(mamba_bc, ("dp", "seq"), axis=0, tiled=True),
-        lax.all_gather(mamba_dt, ("dp", "seq"), axis=0, tiled=True),
-        lax.all_gather(mamba_out, ("dp", "seq"), axis=0, tiled=True),
-        lax.all_gather(attn_q, ("dp", "seq"), axis=0, tiled=True),
-        lax.all_gather(attn_kv, ("dp", "seq"), axis=0, tiled=True),
-        lax.all_gather(attn_out, ("dp", "seq"), axis=0, tiled=True),
-        lax.all_gather(ffn_gate, ("dp", "seq"), axis=0, tiled=True),
-        lax.all_gather(ffn_up, ("dp", "seq"), axis=0, tiled=True),
-        lax.all_gather(ffn_down, ("dp", "seq"), axis=0, tiled=True),
-        lax.all_gather(mixer_norm, ("dp", "seq"), axis=0, tiled=True),
-        lax.all_gather(ffn_norm, ("dp", "seq"), axis=0, tiled=True),
-    )
-    (
-        back_z,
-        back_x,
-        back_bc,
-        back_dt,
-        back_mout,
-        back_q,
-        back_kv,
-        back_o,
-        back_gate,
-        back_up,
-        back_down,
-        back_gain,
-        back_gain_ffn,
-    ) = regathered
-    gain_one_b = back_gain.astype(jnp.float32)
-    gain_two_b = back_gain_ffn.astype(jnp.float32)
     grad_flat = grad_out.reshape(total_rows, width)
-    g_down = matmul_tn(grad_flat, hidden_b)
-    d_hidden = matmul(grad_flat, back_down)
+    g_down = matmul_tn(grad_flat, hidden_b).astype(jnp.bfloat16)
+    d_hidden = matmul(grad_flat, full_down)
     d_gate_b = (d_hidden * up_h * silu_grad(gate_h)).astype(jnp.bfloat16)
     d_up_b = (d_hidden * jax.nn.silu(gate_h)).astype(jnp.bfloat16)
-    g_gate = matmul_tn(fnormed_b, d_gate_b)
-    g_up = matmul_tn(fnormed_b, d_up_b)
-    d_fnorm = matmul_nt(d_gate_b, back_gate) + matmul_nt(d_up_b, back_up)
-    d_mid_norm, g_fnorm = rms_backward(mid, factor_two, gain_two_b, d_fnorm)
+    d_gateup_b = jnp.concatenate([d_gate_b, d_up_b], axis=1)
+    g_gateup = matmul_tn(fnormed_b, d_gateup_b).astype(jnp.bfloat16)
+    owned_ffn = scattered(jnp.concatenate([g_gateup, g_down], axis=1))
+    d_fnorm = matmul_nt(d_gateup_b, full_gateup)
+    d_mid_norm, g_fnorm = rms_backward(mid, factor_two, gain_two, d_fnorm)
     d_mid = grad_flat.astype(jnp.float32) + d_mid_norm
     d_mid_b = d_mid.astype(jnp.bfloat16)
-    g_mout = matmul_tn(d_mid_b, mixed_b)
-    d_mnorm = matmul(d_mid_b, back_mout)
+    g_mixers = matmul_tn(d_mid_b, mixers_b).astype(jnp.bfloat16)
+    d_mixers = matmul(d_mid_b, full_mixer)
+    d_mnorm = d_mixers[:, :inner_width]
     d_gated, g_inner = rms_backward(gated, factor_m, inner_norm, d_mnorm)
     d_ssm = (d_gated * silu_z).reshape(sequences, rows, SSM_HEADS, SSM_HEAD)
     d_z = d_gated * ssm_out.reshape(total_rows, inner_width) * silu_grad(gate_z)
@@ -316,7 +305,7 @@
     direct = jnp.einsum("sth,sthp,stn->shpn", entry, d_ssm, cmat, precision=lax.Precision.HIGHEST)
     backlog = direct
     later_grad = jnp.zeros_like(direct)
-    for hop in range(lax.axis_size("seq") - 1):
+    for hop in range(hops):
         later_grad = passed_along(backlog.astype(jnp.bfloat16), "seq", -1).astype(backlog.dtype)
         backlog = direct + carry[:, :, None, None] * later_grad
     d_carry = jnp.sum(later_grad * incoming, axis=(2, 3))
@@ -347,8 +336,7 @@
     d_inner = d_inner.reshape(total_rows, channels)
     d_step_raw = d_step.reshape(total_rows, SSM_HEADS) * jax.nn.sigmoid(step_raw + dt_bias)
     g_dtb = jnp.sum(d_step_raw, axis=0)
-    d_att_b = matmul(d_mid_b, back_o).astype(jnp.bfloat16)
-    g_aout = matmul_tn(d_mid_b, attended_b)
+    d_att_b = d_mixers[:, inner_width:].astype(jnp.bfloat16)
     d_att_g = d_att_b.reshape(sequences, rows, KV_HEADS, group, HEAD)
     probs = jnp.exp(attention_scores() - lse)
     d_probs = jnp.einsum("stkgd,slkd->skgtl", d_att_g, values, preferred_element_type=jnp.float32)
@@ -364,14 +352,13 @@
         * inv_root
     )
     d_values = jnp.einsum("skgtl,stkgd->slkd", probs_b, d_att_g, preferred_element_type=jnp.float32)
-    d_kv_all = jnp.concatenate([d_keys, d_values], axis=2).reshape(
-        sequences, length, 2 * KV_HEADS * HEAD
-    )
-    d_kv_local = (
-        lax.psum_scatter(d_kv_all.astype(jnp.bfloat16), "seq", scatter_dimension=1, tiled=True)
-        .astype(jnp.float32)
-        .reshape(sequences, rows, 2 * KV_HEADS, HEAD)
-    )
+    d_kv_all = jnp.concatenate([d_keys, d_values], axis=2).reshape(sequences, window, kv_width)
+    d_kv_local = d_kv_all[:, window - rows :]
+    for far in range(1, hops + 1):
+        start = window - (far + 1) * rows
+        term = d_kv_all[:, start : start + rows].astype(jnp.bfloat16)
+        d_kv_local = d_kv_local + passed_along(term, "seq", -far).astype(jnp.float32)
+    d_kv_local = d_kv_local.reshape(sequences, rows, 2 * KV_HEADS, HEAD)
     d_key_local = rotate_back(d_kv_local[:, :, :KV_HEADS], cos_b, sin_b)
     d_kv_b = (
         jnp.concatenate([d_key_local, d_kv_local[:, :, KV_HEADS:]], axis=2)
@@ -387,50 +374,47 @@
     d_x_b = d_inner[:, :inner_width].astype(jnp.bfloat16)
     d_bc_b = d_inner[:, inner_width:].astype(jnp.bfloat16)
     d_st_b = d_step_raw.astype(jnp.bfloat16)
-    g_z = matmul_tn(normed_b, d_z_b)
-    g_x = matmul_tn(normed_b, d_x_b)
-    g_bc = matmul_tn(normed_b, d_bc_b)
-    g_dt = matmul_tn(normed_b, d_st_b)
-    g_q = matmul_tn(normed_b, d_q_b)
-    g_kv = matmul_tn(normed_b, d_kv_b)
-    d_norm = matmul_nt(d_z_b, back_z) + matmul_nt(d_x_b, back_x) + matmul_nt(d_bc_b, back_bc)
-    d_norm = (
-        d_norm + matmul_nt(d_st_b, back_dt) + matmul_nt(d_q_b, back_q) + matmul_nt(d_kv_b, back_kv)
-    )
-    d_in_norm, g_mnorm = rms_backward(x_in, factor_one, gain_one_b, d_norm)
+    d_projected = jnp.concatenate(
+        [
+            d_z_b,
+            d_x_b,
+            d_bc_b,
+            d_q_b,
+            d_kv_b,
+            d_st_b,
+            jnp.zeros((total_rows, spare + 2), jnp.bfloat16),
+        ],
+        axis=1,
+    )
+    g_projected = matmul_tn(normed_b, d_projected).astype(jnp.bfloat16)
+    owned_rest = scattered(jnp.concatenate([g_projected, g_mixers], axis=1))
+    d_norm = matmul_nt(d_projected, full_in)
+    d_in_norm, g_mnorm = rms_backward(x_in, factor_one, gain_one, d_norm)
     grad_in = (d_mid + d_in_norm).astype(jnp.bfloat16).reshape(sequences, rows, width)
-    owned = (
-        lax.psum_scatter(g_z, ("dp", "seq"), scatter_dimension=0, tiled=True),
-        lax.psum_scatter(g_x, ("dp", "seq"), scatter_dimension=0, tiled=True),
-        lax.psum_scatter(g_bc, ("dp", "seq"), scatter_dimension=0, tiled=True),
-        lax.psum_scatter(g_dt, ("dp", "seq"), scatter_dimension=0, tiled=True),
-        lax.psum_scatter(g_mout, ("dp", "seq"), scatter_dimension=0, tiled=True),
-        lax.psum_scatter(g_q, ("dp", "seq"), scatter_dimension=0, tiled=True),
-        lax.psum_scatter(g_kv, ("dp", "seq"), scatter_dimension=0, tiled=True),
-        lax.psum_scatter(g_aout, ("dp", "seq"), scatter_dimension=0, tiled=True),
-        lax.psum_scatter(g_gate, ("dp", "seq"), scatter_dimension=0, tiled=True),
-        lax.psum_scatter(g_up, ("dp", "seq"), scatter_dimension=0, tiled=True),
-        lax.psum_scatter(g_down, ("dp", "seq"), scatter_dimension=0, tiled=True),
-        lax.psum_scatter(g_mnorm, ("dp", "seq"), scatter_dimension=0, tiled=True),
-        lax.psum_scatter(g_fnorm, ("dp", "seq"), scatter_dimension=0, tiled=True),
-    )
-    summed = lax.psum((g_cweight, g_cbias, g_dtb, g_alog, g_skip, g_inner), ("dp", "seq"))
+    summed = lax.psum(
+        (g_cweight, g_cbias, g_dtb, g_alog, g_skip, g_inner, g_mnorm, g_fnorm), ("dp", "seq")
+    )
+    gain_rows = mixer_norm.shape[0]
+    first_row = (lax.axis_index("dp") * lax.axis_size("seq") + lax.axis_index("seq")) * gain_rows
+    g_mnorm_own = lax.dynamic_slice_in_dim(summed[6], first_row, gain_rows, 0)
+    g_fnorm_own = lax.dynamic_slice_in_dim(summed[7], first_row, gain_rows, 0)
+    at_mixers = shard_in.shape[1]
     return (
         block_out,
         grad_in,
-        owned[0],
-        owned[1],
-        owned[2],
-        owned[3],
-        owned[4],
-        owned[5],
-        owned[6],
-        owned[7],
-        owned[8],
-        owned[9],
-        owned[10],
-        owned[11],
-        owned[12],
+        owned_rest[:, :at_u],
+        owned_rest[:, at_u : at_u + inner_width],
+        owned_rest[:, at_u + inner_width : at_q],
+        owned_rest[:, at_dt:at_gain],
+        owned_rest[:, at_mixers : at_mixers + inner_width],
+        owned_rest[:, at_q:at_kv],
+        owned_rest[:, at_kv:at_dt],
+        owned_rest[:, at_mixers + inner_width :],
+        owned_ffn[:, :hidden_width],
+        owned_ffn[:, hidden_width : 2 * hidden_width],
+        owned_ffn[:, 2 * hidden_width :],
+        g_mnorm_own,
+        g_fnorm_own,
         summed[0],
         summed[1],
         summed[2],

time: 2240 us -> 602 us (0.27)
  waiting for transfers between devices: 1620 us -> 242 us
  blocking collectives: 309 us -> 41.8 us
  matrix products: 160 us -> 115 us
  other arithmetic: 52.1 us -> 78.5 us
    reduce_scatter x10 -> x4, waiting for transfers between devices: 1280 us -> 112 us  [the longest x2 96.8 us: scattered(): part = lax.psum_scatter(grad, 'dp', scatter_dimension=0, tiled=True)]
    all_gather x4 -> x0, blocking collectives: 226 us -> none  [the longest x1 72.5 us: local(): lax.all_gather(attn_kv, ('dp', 'seq'), axis=0, tiled=True)]
    unnamed x22 -> x6, waiting for transfers between devices: 191 us -> 0.59 us
    unnamed x2 -> x0, blocking collectives: 83 us -> none
    psum x0 -> x1, blocking collectives: none -> 41.8 us  [local(): lax.psum((g_cweight, g_cbias, g_dtb, g_alog, g_skip, g_inner, g_mnorm, g_...]
    dot_general x10 -> x4, matrix products: 36.3 us -> 11.2 us  [matmul_tn(): lax.dot_general(left, right, (((0,), (0,)), ((), ())), preferred_element_...]
    ppermute x8 -> x10, waiting for transfers between devices: 57 us -> 35.5 us  [passed_along(): return lax.ppermute(block, axis, route)]
    all_gather x8 -> x2, waiting for transfers between devices: 96 us -> 93.6 us  [the longest x1 70.5 us: local(): full_in = lax.all_gather(shard_in, ('dp', 'seq'), axis=0, tiled=True)]
  transfers between devices with their start and end apart: 28 -> 16, of which waited for: 19 -> 7; matrix products, arithmetic and copies ran while one was open for 9% -> 36% of each run, Pallas kernels for 0% -> 0%
where the time goes in v1:
time: 602 us; the launch traced here: 593 us
  waiting for transfers between devices  242 us (40%)
  matrix products  115 us (19%)
  other arithmetic  78.5 us (13%)
  local copies, waits for them, and re-layouts  64.7 us (11%)
  blocking collectives  41.8 us (7%)
  starting transfers between devices  33.7 us (6%)
  between operations  16.7 us (3%)
    reduce_scatter x2, waiting for transfers between devices, scattered(): part = lax.psum_scatter(grad, 'dp', scatter_dimension=0, tiled=True)  96.8 us
    all_gather x1, waiting for transfers between devices, local(): full_in = lax.all_gather(shard_in, ('dp', 'seq'), axis=0, tiled=True)  70.5 us
    psum x1, blocking collectives, local(): lax.psum((g_cweight, g_cbias, g_dtb, g_alog, g_skip, g_inner, g_mnorm, g_...  41.8 us
    ppermute x10, waiting for transfers between devices, passed_along(): return lax.ppermute(block, axis, route)  35.5 us
    ppermute x10, starting transfers between devices, passed_along(): return lax.ppermute(block, axis, route)  33.5 us
    dot_general x3, matrix products, block_output(): jnp.einsum('stuh,suhp->sthp', mixed, xs, precision=lax.Precision.HIGHEST)  25.5 us
    dot_general x4, matrix products, matmul_nt(): lax.dot_general(left, right, (((1,), (1,)), ((), ())), preferred_element_...  23.5 us
    all_gather x1, waiting for transfers between devices, local(): full_out = lax.all_gather(shard_out, ('dp', 'seq'), axis=0, tiled=True)  23.1 us
  transfers between devices with their start and end apart: 16, of which 7 were waited for; matrix products, arithmetic and copies ran while one was open for 36% of the time, Pallas kernels for 0%

profile of v1, /device:TPU:0, one launch (start us, length us, event | category | flops | bytes accessed | tf_op | source)
XLA Modules:
  0.0 592.5 jit_solution(10024623257134418276)
XLA Ops:
  21.7 70.5 %all-gather.3.cloned.1.call-done = bf16[1024,4224]{1,0:T(8,128)(2,1)} async-done(((bf16[32,4224]{1,0:T(8,128)(2,1)}), bf16[1024,4224]{1,0:T(8,128)(2,1)}) %all-gather.3.cloned.1.call-update) | async-done | bytes 8650768 | tf_op jit(solution)/shard_map/all_gather | solution.py:199
  93.7 6.0 %fusion.115 = f32[256,4224]{1,0:T(8,128)S(1)} fusion(bf16[1024,4224]{1,0:T(8,128)(2,1)} %all-gather.3.cloned.1.call-done, bf16[1,256,1024]{2,1,0:T(8,128)(2,1)S(1)} %copy-done.24, f32[1024]{0:T(1024)S(1)} %get-tuple-element.106, f32[256]{0:T(256)S(1)} %add_rsqrt_fusion.2), kind=kOutput, calls=%fused_computation.193 | convolution fusion | flops 2215641088 | bytes 13505536 | tf_op jit(solution)/shard_map/dot_general | solution.py:51
  119.9 6.2 %fusion.44 = (f32[1,256,1792]{2,1,0:T(8,128)S(1)}, f32[1,256,1792]{2,1,0:T(8,128)}) fusion(f32[256]{0:T(256)S(1)} %bitcast.474, f32[256,4224]{1,0:T(8,128)} %copy-done.4, f32[1792]{0:T(1024)S(1)} %get-tuple-element.129, f32[256]{0:T(256)S(1)} %bitcast.477, f32[1,256,1792]{2,1,0:T(8,128)} %copy-done.6, f32[1,3,1792]{2,1,0:T(4,128)S(1)} %collective-permute-done, ...), kind=kLoop, calls=%fused_computation.85 | loop fusion | flops 8716288 | bytes 7401472 | tf_op jit(solution)/shard_map/jit(silu)/mul | solution.py:230
  131.1 8.0 %collective-permute-start.1 = (bf16[1,24,64,128]{3,2,1,0:T(8,128)(2,1)S(1)}, bf16[1,24,64,128]{3,2,1,0:T(8,128)(2,1)S(1)}, u32[]{:S(2)}, u32[]{:S(2)}) collective-permute-start(bf16[1,24,64,128]{3,2,1,0:T(8,128)(2,1)S(1)} %convert_bitcast_fusion.2), channel_id=1, source_target_pairs={{0,1},{1,2},{2,3},{4,5},{5,6},{6,7},{8,9},{9,10},{10,11},{12,13},{... | collective-permute-start | bytes 1179656 | tf_op jit(solution)/shard_map/ppermute | solution.py:23
  143.8 13.0 %collective-permute-done.1 = bf16[1,24,64,128]{3,2,1,0:T(8,128)(2,1)S(1)} collective-permute-done((bf16[1,24,64,128]{3,2,1,0:T(8,128)(2,1)S(1)}, bf16[1,24,64,128]{3,2,1,0:T(8,128)(2,1)S(1)}, u32[]{:S(2)}, u32[]{:S(2)}) %collective-permute-start.1) | collective-permute-done | bytes 393248 | tf_op jit(solution)/shard_map/ppermute | solution.py:23
  157.7 9.7 %collective-permute-start.2 = (bf16[1,24,64,128]{3,2,1,0:T(8,128)(2,1)}, bf16[1,24,64,128]{3,2,1,0:T(8,128)(2,1)}, u32[]{:S(2)}, u32[]{:S(2)}) collective-permute-start(bf16[1,24,64,128]{3,2,1,0:T(8,128)(2,1)} %fusion.92), channel_id=1, source_target_pairs={{0,1},{1,2},{2,3},{4,5},{5,6},{6,7},{8,9},{9,10},{10,11},{12,13},{... | collective-permute-start | bytes 1179656 | tf_op jit(solution)/shard_map/ppermute | solution.py:23
  171.6 10.5 %collective-permute-done.2 = bf16[1,24,64,128]{3,2,1,0:T(8,128)(2,1)} collective-permute-done((bf16[1,24,64,128]{3,2,1,0:T(8,128)(2,1)}, bf16[1,24,64,128]{3,2,1,0:T(8,128)(2,1)}, u32[]{:S(2)}, u32[]{:S(2)}) %collective-permute-start.2) | collective-permute-done | bytes 393248 | tf_op jit(solution)/shard_map/ppermute | solution.py:23
  183.9 8.5 %fusion.45 = f32[1,256,24,64]{1,3,2,0:T(8,128)} fusion(f32[1,256,24,64]{1,3,2,0:T(8,128)S(1)} %bitcast.421, f32[256,24,64]{0,2,1:T(8,128)S(1)} %fusion.105, f32[256,24,64]{0,2,1:T(8,128)S(1)} %bitcast.422, f32[256,24]{0,1:T(8,128)S(1)} %copy-done.87, f32[256,256]{1,0:T(8,128)S(1)} %copy-done.65, f32[256,24]{0,1:T(8,128)S(1)} %copy-done.90, ...), kind=kOutput, calls=%fused_computation.89 | convolution fusion | flops 1217396736 | bytes 6692960 | tf_op jit(solution)/shard_map/stuh,suhp->sthp/dot_general | solution.py:117
  199.1 23.1 %all-gather.5.cloned.1.call-done = bf16[1024,8192]{1,0:T(8,128)(2,1)} async-done(((bf16[32,8192]{1,0:T(8,128)(2,1)}), bf16[1024,8192]{1,0:T(8,128)(2,1)}) %all-gather.5.cloned.1.call-update) | async-done | bytes 16777232 | tf_op jit(solution)/shard_map/all_gather | solution.py:200
  226.2 6.2 %fusion.2 = f32[256,4096]{1,0:T(8,128)S(1)} fusion(bf16[1024,8192]{1,0:T(8,128)(2,1)} %all-gather.5.cloned.1.call-done, f32[256,1024]{1,0:T(8,128)S(1)} %get-tuple-element.197, f32[1024]{0:T(1024)S(1)} %get-tuple-element.105, f32[256]{0:T(256)S(1)} %add_rsqrt_fusion), kind=kOutput, calls=%fused_computation.6 | convolution fusion | flops 2148270080 | bytes 13636608 | tf_op jit(solution)/shard_map/dot_general | solution.py:51
  240.7 9.2 %pad_maximum_fusion.1 = bf16[1024,6144]{1,0:T(8,128)(2,1)} fusion(bf16[1024,2048]{1,0:T(8,128)(2,1)S(1)} %convert_bitcast_fusion, bf16[1024,4096]{1,0:T(8,128)(2,1)S(1)} %convolution_convert_fusion.1), kind=kLoop, calls=%fused_computation.1 | loop fusion | flops 25165824 | bytes 25165824 | tf_op jit(solution)/shard_map/concatenate | solution.py:293
  254.4 7.5 %multiply_reduce_fusion.9 = (f32[1024]{0:T(1024)}, f32[256]{0:T(256)S(1)}, f32[256,1024]{1,0:T(8,128)S(1)}) fusion(f32[256,1024]{1,0:T(8,128)} %copy-done.28, f32[256]{0:T(256)S(1)} %add_rsqrt_fusion, f32[1024]{0:T(1024)S(1)} %get-tuple-element.105, bf16[1024,8192]{1,0:T(8,128)(2,1)} %all-gather.5.cloned.1.call-done, bf16[256,2048]{1,0:T(8,128)(2,1)} %copy-done.46, ...), kind=kOutput, calls=%fused_computation.141 | convolution fusion | flops 2153249536 | bytes 12593152 | tf_op jit(solution)/shard_map/dot_general | solution.py:55
  262.3 5.9 fusion.16
  287.9 4.9 fusion.5
  308.6 10.1 %fusion.21 = (f32[256,24]{0,1:T(8,128)S(1)}, f32[256,24]{0,1:T(8,128)S(1)}, f32[256,24]{0,1:T(8,128)S(1)}, f32[256,256]{1,0:T(8,128)S(1)}) fusion(f32[256,256]{1,0:T(8,128)S(1)} %copy-done.66, f32[256,24]{0,1:T(8,128)S(1)} %copy-done.88, f32[256,24]{0,1:T(8,128)S(1)} %copy-done.91, pred[256,256]{1,0:T(8,128)(4,1)S(1)} %copy-done.81, ...), kind=kOutput, calls=%fused_computation.38 | convolution fusion | flops 1231468544 | bytes 3858432 | tf_op jit(solution)/shard_map/transpose(jvp(stuh,suhp->sthp))/dot_general | solution.py:117
  328.8 4.8 convolution_convert_fusion.2
  340.7 12.1 %collective-permute-done.6 = bf16[1,24,64,128]{3,2,1,0:T(8,128)(2,1)S(1)} collective-permute-done((bf16[1,24,64,128]{3,2,1,0:T(8,128)(2,1)}, bf16[1,24,64,128]{3,2,1,0:T(8,128)(2,1)S(1)}, u32[]{:S(2)}, u32[]{:S(2)}) %collective-permute-start.6) | collective-permute-done | bytes 393248 | tf_op jit(solution)/shard_map/ppermute | solution.py:23
  355.2 6.8 %bitcast_add_fusion.1 = f32[1,256,24,64]{1,3,2,0:T(8,128)} fusion(f32[24,64,256]{2,1,0:T(8,128)S(1)} %get-tuple-element.202, f32[256,24,64]{0,2,1:T(8,128)S(1)} %bitcast.432, f32[24,64,256]{2,1,0:T(8,128)S(1)} %bitcast.431, f32[256,24]{0,1:T(8,128)S(1)} %copy-done.89, f32[256,256]{1,0:T(8,128)S(1)} %copy-done.67, f32[256,24]{0,1:T(8,128)S(1)} %copy-done.92, ...), kind=kOutput, calls=%fused_computation.87 | convolution fusion | flops 1217396736 | bytes 6692960 | tf_op jit(solution)/shard_map/transpose(jvp(stuh,suhp->sthp))/dot_general | solution.py:117
  399.3 7.0 %pad_maximum_fusion = bf16[1024,6272]{1,0:T(8,128)(2,1)} fusion(bf16[1024,2048]{1,0:T(8,128)(2,1)S(1)} %copy-done.1, bf16[1024,4224]{1,0:T(8,128)(2,1)S(1)} %convolution_convert_fusion), kind=kLoop, calls=%fused_computation | loop fusion | flops 25690112 | bytes 25690112 | tf_op jit(solution)/shard_map/concatenate | solution.py:390
  407.1 96.8 %reduce-scatter.5.cloned.1.call-done = bf16[128,6272]{1,0:T(8,128)(2,1)} async-done(((bf16[1024,6272]{1,0:T(8,128)(2,1)}), bf16[128,6272]{1,0:T(8,128)(2,1)}) %reduce-scatter.5.cloned.1.call-update) | async-done | bytes 1605648 | tf_op jit(solution)/shard_map/reduce_scatter | solution.py:27
  504.1 4.6 fusion.67
  509.0 7.3 %fusion.89 = (f32[1024]{0:T(1024)S(1)}, f32[256]{0:T(256)S(1)}, f32[256,1024]{1,0:T(8,128)}) fusion(bf16[1,256,1024]{2,1,0:T(8,128)(2,1)S(1)} %copy-done.26, f32[256]{0:T(256)S(1)} %copy-done.94, f32[1024]{0:T(1024)S(1)} %get-tuple-element.106, bf16[256,4224]{1,0:T(8,128)(2,1)S(1)} %concatenate.103, bf16[1024,4224]{1,0:T(8,128)(2,1)} %all-gather.3.cloned.1.call-done), kind=kOutput, calls=%fused_computation.139 | convolution fusion | flops 2216426240 | bytes 12396544 | tf_op jit(solution)/shard_map/dot_general | solution.py:55
  516.3 41.8 %all-reduce.9 = (f32[1024]{0:T(1024)S(1)}, f32[1024]{0:T(1024)S(1)}, f32[4,1792]{1,0:T(4,128)}, f32[1792]{0:T(1024)}, f32[24]{0:T(128)}, /*index=5*/f32[24]{0:T(128)}, f32[24]{0:T(128)}, f32[1536]{0:T(1024)}) all-reduce(f32[1024]{0:T(1024)S(1)} %get-tuple-element.123, ...), channel_id=1, replica_groups=mesh['dp'=8,'seq'=4] {'dp','seq'}, use_global_device_ids=true, to_apply=%region_27.28 | all-reduce | flops 12616 | bytes 100928 | tf_op jit(solution)/shard_map/psum | solution.py:394
  563.8 15.3 %reduce-scatter.7.cloned.1.call-done = bf16[32,6272]{1,0:T(8,128)(2,1)} async-done(((bf16[128,6272]{1,0:T(8,128)(2,1)}), bf16[32,6272]{1,0:T(8,128)(2,1)}) %reduce-scatter.7.cloned.1.call-update) | async-done | bytes 401424 | tf_op jit(solution)/shard_map/reduce_scatter | solution.py:28
  (438 shorter events, 179.8 us)
Async XLA Ops:
  7.2 85.0 %all-gather.3.cloned.1.call-start = ((), (), s32[]{:S(2)}) async-start(), calls=%async_computation.4 | async-start | bytes 8921088 | tf_op jit(solution)/shard_map/all_gather | solution.py:199
  11.4 210.8 %all-gather.5.cloned.1.call-start = ((), (), s32[]{:S(2)}) async-start(), calls=%async_computation.5 | async-start | bytes 17301504 | tf_op jit(solution)/shard_map/all_gather | solution.py:200
  16.7 389.8 %reduce-scatter.9.cloned.1.call-start = ((), (), s32[]{:S(2)}) async-start(), calls=%async_computation.8 | async-start | bytes 14155776 | tf_op jit(solution)/shard_map/reduce_scatter | solution.py:27
  18.8 101.1 %copy-start.74 = (f32[1792]{0:T(1024)}, f32[1792]{0:T(1024)S(1)}, u32[]{:S(2)}) copy-start(f32[1792]{0:T(1024)S(1)} %get-tuple-element.128) | copy-start | bytes 21508
  18.8 101.1 %copy-start.76 = (f32[1792]{0:T(1024)}, f32[1792]{0:T(1024)S(1)}, u32[]{:S(2)}) copy-start(f32[1792]{0:T(1024)S(1)} %get-tuple-element.129) | copy-start | bytes 21508
  18.8 101.1 %copy-start.78 = (f32[1792]{0:T(1024)}, f32[1792]{0:T(1024)S(1)}, u32[]{:S(2)}) copy-start(f32[1792]{0:T(1024)S(1)} %get-tuple-element.130) | copy-start | bytes 21508
  19.8 100.1 %copy-start.97 = (f32[1,256]{1,0:T(1,128)}, f32[1,256]{1,0:T(1,128)S(1)}, u32[]{:S(2)}) copy-start(f32[1,256]{1,0:T(1,128)S(1)} %get-tuple-element.186) | copy-start | bytes 3076
  19.8 100.1 %copy-start.99 = (f32[1,256]{1,0:T(1,128)}, f32[1,256]{1,0:T(1,128)S(1)}, u32[]{:S(2)}) copy-start(f32[1,256]{1,0:T(1,128)S(1)} %get-tuple-element.187) | copy-start | bytes 3076
  20.0 275.5 %copy-start.51 = (f32[256,32]{0,1:T(8,128)}, f32[256,32]{0,1:T(8,128)S(1)}, u32[]{:S(2)}) copy-start(f32[256,32]{0,1:T(8,128)S(1)} %get-tuple-element.191) | copy-start | bytes 98308
  20.0 275.5 %copy-start.53 = (f32[256,32]{0,1:T(8,128)}, f32[256,32]{0,1:T(8,128)S(1)}, u32[]{:S(2)}) copy-start(f32[256,32]{0,1:T(8,128)S(1)} %get-tuple-element.192) | copy-start | bytes 98308
  102.7 37.5 %collective-permute-start.4 = (bf16[1,256,256]{1,2,0:T(8,128)(2,1)}, bf16[1,256,256]{1,2,0:T(8,128)(2,1)}, u32[]{:S(2)}, u32[]{:S(2)}) collective-permute-start(bf16[1,256,256]{1,2,0:T(8,128)(2,1)} %bitcast.43), channel_id=1, source_target_pairs={{0,1},{1,2},{2,3},{4,5},{5,6},{6,7},{8,9},{9,10},{10,11},{12,13},{... | collective-permute-start | bytes 393224 | tf_op jit(solution)/shard_map/ppermute | solution.py:23
  106.8 33.5 %collective-permute-start.3 = (bf16[1,256,256]{1,2,0:T(8,128)(2,1)}, bf16[1,256,256]{1,2,0:T(8,128)(2,1)}, u32[]{:S(2)}, u32[]{:S(2)}) collective-permute-start(bf16[1,256,256]{1,2,0:T(8,128)(2,1)} %bitcast.43), channel_id=1, source_target_pairs={{0,2},{1,3},{4,6},{5,7},{8,10},{9,11},{12,14},{13,15},{16,18},{17,... | collective-permute-start | bytes 393224 | tf_op jit(solution)/shard_map/ppermute | solution.py:23
  112.9 7.0 %collective-permute-start = (f32[1,3,1792]{2,1,0:T(4,128)S(1)}, f32[1,3,1792]{2,1,0:T(4,128)S(1)}, u32[]{:S(2)}, u32[]{:S(2)}) collective-permute-start(f32[1,3,1792]{2,1,0:T(4,128)S(1)} %slice.302), channel_id=1, source_target_pairs={{0,1},{1,2},{2,3},{4,5},{5,6},{6,7},{8,9},{9,10},{10,11},{12,13},{... | collective-permute-start | bytes 64520 | tf_op jit(solution)/shard_map/ppermute | solution.py:23
  126.1 156.1 %copy-start.5 = (f32[1,256,1792]{2,1,0:T(8,128)}, f32[1,256,1792]{2,1,0:T(8,128)S(1)}, u32[]{:S(2)}) copy-start(f32[1,256,1792]{2,1,0:T(8,128)S(1)} %get-tuple-element.154) | copy-start | bytes 5505028
  131.1 25.6 %collective-permute-start.1 = (bf16[1,24,64,128]{3,2,1,0:T(8,128)(2,1)S(1)}, bf16[1,24,64,128]{3,2,1,0:T(8,128)(2,1)S(1)}, u32[]{:S(2)}, u32[]{:S(2)}) collective-permute-start(bf16[1,24,64,128]{3,2,1,0:T(8,128)(2,1)S(1)} %convert_bitcast_fusion.2), channel_id=1, source_target_pairs={{0,1},{1,2},{2,3},{4,5},{5,6},{6,7},{8,9},{9,10},{10,11},{12,13},{... | collective-permute-start | bytes 1179656 | tf_op jit(solution)/shard_map/ppermute | solution.py:23
  157.7 24.4 %collective-permute-start.2 = (bf16[1,24,64,128]{3,2,1,0:T(8,128)(2,1)}, bf16[1,24,64,128]{3,2,1,0:T(8,128)(2,1)}, u32[]{:S(2)}, u32[]{:S(2)}) collective-permute-start(bf16[1,24,64,128]{3,2,1,0:T(8,128)(2,1)} %fusion.92), channel_id=1, source_target_pairs={{0,1},{1,2},{2,3},{4,5},{5,6},{6,7},{8,9},{9,10},{10,11},{12,13},{... | collective-permute-start | bytes 1179656 | tf_op jit(solution)/shard_map/ppermute | solution.py:23
  250.0 253.9 %reduce-scatter.5.cloned.1.call-start = ((), (), s32[]{:S(2)}) async-start(), calls=%async_computation.6 | async-start | bytes 14450688 | tf_op jit(solution)/shard_map/reduce_scatter | solution.py:27
  285.3 48.2 %collective-permute-start.5 = (bf16[1,24,64,128]{3,2,1,0:T(8,128)(2,1)}, bf16[1,24,64,128]{3,2,1,0:T(8,128)(2,1)}, u32[]{:S(2)}, u32[]{:S(2)}) collective-permute-start(bf16[1,24,64,128]{3,2,1,0:T(8,128)(2,1)} %convert_bitcast_fusion.1), channel_id=1, source_target_pairs={{1,0},{2,1},{3,2},{5,4},{6,5},{7,6},{9,8},{10,9},{11,10},{13,12},{... | collective-permute-start | bytes 1179656 | tf_op jit(solution)/shard_map/ppermute | solution.py:23
  305.6 31.5 %collective-permute-start.9 = (bf16[1,256,256]{1,2,0:T(8,128)(2,1)}, bf16[1,256,256]{1,2,0:T(8,128)(2,1)}, u32[]{:S(2)}, u32[]{:S(2)}) collective-permute-start(bf16[1,256,256]{1,2,0:T(8,128)(2,1)} %get-tuple-element.179), channel_id=1, source_target_pairs={{2,0},{3,1},{6,4},{7,5},{10,8},{11,9},{14,12},{15,13},{18,16},{19,... | collective-permute-start | bytes 393224 | tf_op jit(solution)/shard_map/ppermute | solution.py:23
  307.0 30.1 %collective-permute-start.8 = (bf16[1,256,256]{1,2,0:T(8,128)(2,1)}, bf16[1,256,256]{1,2,0:T(8,128)(2,1)}, u32[]{:S(2)}, u32[]{:S(2)}) collective-permute-start(bf16[1,256,256]{1,2,0:T(8,128)(2,1)} %get-tuple-element.178), channel_id=1, source_target_pairs={{1,0},{2,1},{3,2},{5,4},{6,5},{7,6},{9,8},{10,9},{11,10},{13,12},{... | collective-permute-start | bytes 393224 | tf_op jit(solution)/shard_map/ppermute | solution.py:23
  335.5 17.2 %collective-permute-start.6 = (bf16[1,24,64,128]{3,2,1,0:T(8,128)(2,1)}, bf16[1,24,64,128]{3,2,1,0:T(8,128)(2,1)S(1)}, u32[]{:S(2)}, u32[]{:S(2)}) collective-permute-start(bf16[1,24,64,128]{3,2,1,0:T(8,128)(2,1)} %fusion.91), channel_id=1, source_target_pairs={{1,0},{2,1},{3,2},{5,4},{6,5},{7,6},{9,8},{10,9},{11,10},{13,12},{... | collective-permute-start | bytes 1179656 | tf_op jit(solution)/shard_map/ppermute | solution.py:23
  374.8 15.6 %collective-permute-start.7 = (f32[1,3,1792]{2,1,0:T(4,128)}, f32[1,3,1792]{2,1,0:T(4,128)S(1)}, u32[]{:S(2)}, u32[]{:S(2)}) collective-permute-start(f32[1,3,1792]{2,1,0:T(4,128)} %pad_add_fusion.2), channel_id=1, source_target_pairs={{1,0},{2,1},{3,2},{5,4},{6,5},{7,6},{9,8},{10,9},{11,10},{13,12},{... | collective-permute-start | bytes 64520 | tf_op jit(solution)/shard_map/ppermute | solution.py:23
  406.4 155.5 %reduce-scatter.11.cloned.1.call-start = ((), (), s32[]{:S(2)}) async-start(), calls=%async_computation.9 | async-start | bytes 1966080 | tf_op jit(solution)/shard_map/reduce_scatter | solution.py:28
  407.0 172.2 %reduce-scatter.7.cloned.1.call-start = ((), (), s32[]{:S(2)}) async-start(), calls=%async_computation.7 | async-start | bytes 2007040 | tf_op jit(solution)/shard_map/reduce_scatter | solution.py:28
  (117 other events, 1475.1 us)
Sparse Core Ops, SparseCore 0:
  11.5 80.7 all-gather.2
  95.8 126.2 all-gather.4
  250.1 96.0 reduce-scatter.8
  406.5 97.2 reduce-scatter.4
  506.0 35.8 reduce-scatter.10
  544.1 35.0 reduce-scatter.6

commit v2 on v1

--- a/solution.py
+++ b/solution.py
@@ -1,6 +1,11 @@
+import functools
+import math
+
 import jax
 import jax.numpy as jnp
 from jax import lax
+from jax.experimental import pallas as pl
+from jax.experimental.pallas import tpu as pltpu
 from jax.sharding import PartitionSpec as P
 
 SSM_HEADS = 24
@@ -15,6 +20,7 @@
 ROPE_BASE = 100000000000.0
 MAX_DOC = 512
 LANES = 128
+SSM_PAIRS = SSM_HEADS * SSM_HEAD // LANES
 
 
 def passed_along(block, axis, distance):
@@ -23,8 +29,11 @@
     return lax.ppermute(block, axis, route)
 
 
-def scattered(grad):
-    part = lax.psum_scatter(grad, "dp", scatter_dimension=0, tiled=True)
+def scattered_dp(grad):
+    return lax.psum_scatter(grad, "dp", scatter_dimension=0, tiled=True)
+
+
+def scattered_seq(part):
     return lax.psum_scatter(part, "seq", scatter_dimension=0, tiled=True).astype(jnp.float32)
 
 
@@ -88,38 +97,306 @@
     )
 
 
-def block_masks(local_ids, prior_id):
-    count = local_ids.shape[1]
-    order = jnp.arange(count)
-    pair = (order[:, None] >= order[None, :])[None] & (
-        local_ids[:, :, None] == local_ids[:, None, :]
-    )
-    inbound = (local_ids == prior_id[:, None]).astype(jnp.float32)
-    outbound = (local_ids == local_ids[:, -1:]).astype(jnp.float32)
-    return (pair, inbound, outbound)
-
-
-def block_summary(xs, bmat, step, a_log, inbound, outbound):
-    decay = jnp.cumsum(step * -jnp.exp(a_log), axis=1)
-    tail = jnp.exp(decay[:, -1:, :] - decay) * outbound[:, :, None] * step
-    state_out = jnp.einsum("suh,suhp,sun->shpn", tail, xs, bmat, precision=lax.Precision.HIGHEST)
-    carry = jnp.exp(decay[:, -1, :]) * inbound[:, -1:]
-    return (state_out, carry)
-
-
-def block_output(xs, bmat, cmat, step, a_log, d_skip, state_in, pair, inbound):
-    decay = jnp.cumsum(step * -jnp.exp(a_log), axis=1)
-    spread = decay[:, :, None, :] - decay[:, None, :, :]
-    mask = pair[:, :, :, None]
-    kernel = jnp.where(mask, jnp.exp(jnp.where(mask, spread, 0.0)), 0.0)
-    intersection_cb = jnp.einsum("stn,sun->stu", cmat, bmat, precision=lax.Precision.HIGHEST)
-    mixed = kernel * intersection_cb[:, :, :, None] * step[:, None, :, :]
-    local_part = jnp.einsum("stuh,suhp->sthp", mixed, xs, precision=lax.Precision.HIGHEST)
-    entry = jnp.exp(decay) * inbound[:, :, None]
-    carried = entry[:, :, :, None] * jnp.einsum(
-        "stn,shpn->sthp", cmat, state_in, precision=lax.Precision.HIGHEST
-    )
-    return local_part + carried + d_skip[:, None] * xs
+def half_lanes(cols, first, shape):
+    lane = lax.broadcasted_iota(jnp.int32, shape, 1)
+    return jnp.where(lane < SSM_HEAD, cols[:, first : first + 1], cols[:, first + 1 : first + 2])
+
+
+def dot_nn(left, right):
+    return lax.dot_general(
+        left, right, (((1,), (0,)), ((), ())), preferred_element_type=jnp.float32
+    )
+
+
+def ssm_local_kernel(xs_ref, b_ref, c_ref, cols_ref, rows_ref, bias_ref, out_ref, state_ref, cb_ref):
+    bmat = b_ref[...]
+
+    @pl.when(pl.program_id(0) == 0)
+    def _():
+        cb_ref[...] = lax.dot_general(
+            c_ref[...],
+            bmat,
+            (((1,), (1,)), ((), ())),
+            precision=lax.Precision.HIGHEST,
+            preferred_element_type=jnp.float32,
+        )
+
+    xs = xs_ref[...]
+    cols = cols_ref[0]
+    rows = rows_ref[0]
+    scaled = xs * half_lanes(cols, 2, xs.shape)
+    scaled_b = scaled.astype(jnp.bfloat16)
+    parts = []
+    for k in range(2):
+        kernel = jnp.exp(cols[:, k : k + 1] - rows[k : k + 1, :] + bias_ref[...])
+        parts.append(dot_nn((kernel * cb_ref[...]).astype(jnp.bfloat16), scaled_b))
+    lane = lax.broadcasted_iota(jnp.int32, xs.shape, 1)
+    out_ref[...] = jnp.where(lane < SSM_HEAD, parts[0], parts[1])
+    tailed = (scaled * half_lanes(cols, 6, xs.shape)).astype(jnp.bfloat16)
+    state_ref[0] = lax.dot_general(
+        tailed,
+        bmat.astype(jnp.bfloat16),
+        (((0,), (0,)), ((), ())),
+        preferred_element_type=jnp.float32,
+    )
+
+
+def ssm_carry_kernel(local_ref, xs_ref, c_ref, cols_ref, state_ref, skip_ref, z_ref, out_ref, gated_ref):
+    xs = xs_ref[...]
+    carried = lax.dot_general(
+        c_ref[...].astype(jnp.bfloat16),
+        state_ref[0],
+        (((1,), (1,)), ((), ())),
+        preferred_element_type=jnp.float32,
+    )
+    entry = half_lanes(cols_ref[0], 4, xs.shape)
+    out = local_ref[...] + entry * carried + skip_ref[...] * xs
+    out_ref[...] = out
+    gate = z_ref[...]
+    gated_ref[...] = out * (gate * jax.nn.sigmoid(gate))
+
+
+def ssm_direct_kernel(g_ref, c_ref, cols_ref, direct_ref):
+    g = g_ref[...]
+    entered = (g * half_lanes(cols_ref[0], 4, g.shape)).astype(jnp.bfloat16)
+    direct_ref[0] = lax.dot_general(
+        entered,
+        c_ref[...].astype(jnp.bfloat16),
+        (((0,), (0,)), ((), ())),
+        preferred_element_type=jnp.float32,
+    )
+
+
+def ssm_backward_kernel(
+    g_ref,
+    xs_ref,
+    out_ref,
+    b_ref,
+    c_ref,
+    cols_ref,
+    rows_ref,
+    bias_ref,
+    state_ref,
+    later_ref,
+    skip_ref,
+    dxs_ref,
+    db_ref,
+    dc_ref,
+    dcols_ref,
+    drows_ref,
+    cb_ref,
+    dcb_ref,
+):
+    pair = pl.program_id(0)
+    bmat = b_ref[...]
+    cmat = c_ref[...]
+    b_low = bmat.astype(jnp.bfloat16)
+    c_low = cmat.astype(jnp.bfloat16)
+
+    @pl.when(pair == 0)
+    def _():
+        cb_ref[...] = lax.dot_general(
+            bmat,
+            cmat,
+            (((1,), (1,)), ((), ())),
+            precision=lax.Precision.HIGHEST,
+            preferred_element_type=jnp.float32,
+        )
+        dcb_ref[...] = jnp.zeros_like(dcb_ref)
+        db_ref[...] = jnp.zeros_like(db_ref)
+        dc_ref[...] = jnp.zeros_like(dc_ref)
+
+    g = g_ref[...]
+    xs = xs_ref[...]
+    skip = skip_ref[...]
+    cols = cols_ref[0]
+    rows = rows_ref[0]
+    step = half_lanes(cols, 2, xs.shape)
+    tail = half_lanes(cols, 6, xs.shape)
+    lane = lax.broadcasted_iota(jnp.int32, xs.shape, 1)
+    first = lane < SSM_HEAD
+    g_low = g.astype(jnp.bfloat16)
+    scaled = xs * step
+    parts = []
+    total = dcb_ref[...]
+    for k in range(2):
+        mine = first if k == 0 else jnp.logical_not(first)
+        kernel = jnp.exp(rows[k : k + 1, :] - cols[:, k : k + 1] + bias_ref[...])
+        parts.append(dot_nn((kernel * cb_ref[...]).astype(jnp.bfloat16), g_low))
+        crossed = lax.dot_general(
+            jnp.where(mine, scaled, 0.0).astype(jnp.bfloat16),
+            g_low,
+            (((1,), (1,)), ((), ())),
+            preferred_element_type=jnp.float32,
+        )
+        total = total + crossed * kernel
+    dcb_ref[...] = total
+    later = later_ref[0]
+    swept = tail * lax.dot_general(
+        b_low, later, (((1,), (1,)), ((), ())), preferred_element_type=jnp.float32
+    )
+    inner = jnp.where(first, parts[0], parts[1]) + swept
+    dxs_ref[...] = step * inner + skip * g
+    db_ref[...] += dot_nn((scaled * tail).astype(jnp.bfloat16), later)
+    entered = (g * half_lanes(cols, 4, g.shape)).astype(jnp.bfloat16)
+    dc_ref[...] += dot_nn(entered, state_ref[0])
+    rose = g_low.astype(jnp.float32) * (out_ref[...] - skip * xs)
+    stepped = xs * inner
+    kept = scaled.astype(jnp.bfloat16).astype(jnp.float32)
+    fell = kept * (inner - swept) + scaled * swept
+    columns = [
+        jnp.sum(jnp.where(first, value, 0.0), axis=1, keepdims=True)
+        if k == 0
+        else jnp.sum(jnp.where(first, 0.0, value), axis=1, keepdims=True)
+        for value in (rose, stepped, fell)
+        for k in range(2)
+    ]
+    spot = lax.broadcasted_iota(jnp.int32, cols.shape, 1)
+    packed = jnp.zeros_like(cols)
+    for index, column in enumerate(columns):
+        packed = jnp.where(spot == index, column, packed)
+    dcols_ref[0] = packed
+    drows_ref[0, 0:1, :] = jnp.sum(scaled * swept, axis=0, keepdims=True)
+    drows_ref[0, 1:2, :] = jnp.sum(g * xs, axis=0, keepdims=True)
+
+    @pl.when(pair == pl.num_programs(0) - 1)
+    def _():
+        low = dcb_ref[...].astype(jnp.bfloat16)
+        db_ref[...] += dot_nn(low, c_low)
+        dc_ref[...] += lax.dot_general(
+            low, b_low, (((0,), (0,)), ((), ())), preferred_element_type=jnp.float32
+        )
+
+
+def ssm_specs(count):
+    rows = count
+    block = pl.BlockSpec((rows, LANES), lambda p: (0, p))
+    bmat = pl.BlockSpec((rows, LANES), lambda p: (0, SSM_PAIRS))
+    cmat = pl.BlockSpec((rows, LANES), lambda p: (0, SSM_PAIRS + 1))
+    cols = pl.BlockSpec((1, rows, 8), lambda p: (p, 0, 0))
+    turned = pl.BlockSpec((1, 2, rows), lambda p: (p, 0, 0))
+    bias = pl.BlockSpec((rows, rows), lambda p: (0, 0))
+    state = pl.BlockSpec((1, LANES, STATE), lambda p: (p, 0, 0))
+    skip = pl.BlockSpec((1, LANES), lambda p: (0, p))
+    whole = pl.BlockSpec((rows, LANES), lambda p: (0, 0))
+    return block, bmat, cmat, cols, turned, bias, state, skip, whole
+
+
+def ssm_local(act, cols, turned, bias):
+    rows = act.shape[0]
+    block, bmat, cmat, col, turn, square, state, skip, whole = ssm_specs(rows)
+    return pl.pallas_call(
+        ssm_local_kernel,
+        grid=(SSM_PAIRS,),
+        in_specs=[block, bmat, cmat, col, turn, square],
+        out_specs=[block, state],
+        out_shape=[
+            jax.ShapeDtypeStruct((rows, SSM_PAIRS * LANES), jnp.float32),
+            jax.ShapeDtypeStruct((SSM_PAIRS, LANES, STATE), jnp.float32),
+        ],
+        scratch_shapes=[pltpu.VMEM((rows, rows), jnp.float32)],
+        name="ssm_local",
+        cost_estimate=pl.CostEstimate(flops=10**9, transcendentals=24 * rows * rows, bytes_accessed=6 * 10**6),
+    )(act, act, act, cols, turned, bias)
+
+
+def ssm_carried(local_part, act, cols, state, skip_row, projected):
+    rows = act.shape[0]
+    block, bmat, cmat, col, turn, square, states, skip, whole = ssm_specs(rows)
+    shape = jax.ShapeDtypeStruct((rows, SSM_PAIRS * LANES), jnp.float32)
+    return pl.pallas_call(
+        ssm_carry_kernel,
+        grid=(SSM_PAIRS,),
+        in_specs=[block, block, cmat, col, states, skip, block],
+        out_specs=[block, block],
+        out_shape=[shape, shape],
+        name="ssm_carried",
+        cost_estimate=pl.CostEstimate(flops=10**8, transcendentals=rows * 1536, bytes_accessed=9 * 10**6),
+    )(local_part, act, act, cols, state, skip_row, projected)
+
+
+def ssm_direct(g, act, cols):
+    rows = act.shape[0]
+    block, bmat, cmat, col, turn, square, states, skip, whole = ssm_specs(rows)
+    return pl.pallas_call(
+        ssm_direct_kernel,
+        grid=(SSM_PAIRS,),
+        in_specs=[block, cmat, col],
+        out_specs=states,
+        out_shape=jax.ShapeDtypeStruct((SSM_PAIRS, LANES, STATE), jnp.float32),
+        name="ssm_direct",
+        cost_estimate=pl.CostEstimate(flops=10**8, transcendentals=0, bytes_accessed=4 * 10**6),
+    )(g, act, cols)
+
+
+def ssm_backward(g, act, out, cols, turned, bias_turned, state, later, skip_row):
+    rows = act.shape[0]
+    block, bmat, cmat, col, turn, square, states, skip, whole = ssm_specs(rows)
+    return pl.pallas_call(
+        ssm_backward_kernel,
+        grid=(SSM_PAIRS,),
+        in_specs=[block, block, block, bmat, cmat, col, turn, square, states, states, skip],
+        out_specs=[block, whole, whole, col, pl.BlockSpec((1, 2, LANES), lambda p: (p, 0, 0))],
+        out_shape=[
+            jax.ShapeDtypeStruct((rows, SSM_PAIRS * LANES), jnp.float32),
+            jax.ShapeDtypeStruct((rows, STATE), jnp.float32),
+            jax.ShapeDtypeStruct((rows, STATE), jnp.float32),
+            jax.ShapeDtypeStruct((SSM_PAIRS, rows, 8), jnp.float32),
+            jax.ShapeDtypeStruct((SSM_PAIRS, 2, LANES), jnp.float32),
+        ],
+        scratch_shapes=[pltpu.VMEM((rows, rows), jnp.float32)] * 2,
+        name="ssm_backward",
+        cost_estimate=pl.CostEstimate(flops=2 * 10**9, transcendentals=24 * rows * rows, bytes_accessed=12 * 10**6),
+    )(g, act, out, act, act, cols, turned, bias_turned, state, later, skip_row)
+
+
+def outer_kernel(split, left_a_ref, right_a_ref, left_b_ref, right_b_ref, out_ref, turned_ref):
+    step = pl.program_id(0)
+
+    @pl.when(step == 0)
+    def _():
+        turned_ref[...] = left_a_ref[...].T
+
+    @pl.when(step == split)
+    def _():
+        turned_ref[...] = left_b_ref[...].T
+
+    @pl.when(step < split)
+    def _():
+        out_ref[...] = dot_nn(turned_ref[...], right_a_ref[...]).astype(jnp.bfloat16)
+
+    @pl.when(step >= split)
+    def _():
+        out_ref[...] = dot_nn(turned_ref[...], right_b_ref[...]).astype(jnp.bfloat16)
+
+
+def outer_pair(left_a, right_a, left_b, right_b):
+    rows, width = left_a.shape
+    wide_a = right_a.shape[1]
+    wide_b = right_b.shape[1]
+    wide = math.gcd(math.gcd(wide_a, wide_b), 512)
+    split = wide_a // wide
+    total = split + wide_b // wide
+    held = pl.BlockSpec((rows, width), lambda j: (0, 0))
+    return pl.pallas_call(
+        functools.partial(outer_kernel, split),
+        grid=(total,),
+        in_specs=[
+            held,
+            pl.BlockSpec((rows, wide), lambda j: (0, jnp.minimum(j, split - 1))),
+            held,
+            pl.BlockSpec((rows, wide), lambda j: (0, jnp.maximum(j - split, 0))),
+        ],
+        out_specs=pl.BlockSpec((width, wide), lambda j: (0, j)),
+        out_shape=jax.ShapeDtypeStruct((width, wide_a + wide_b), jnp.bfloat16),
+        scratch_shapes=[pltpu.VMEM((width, rows), jnp.bfloat16)],
+        name="outer_pair",
+        cost_estimate=pl.CostEstimate(
+            flops=2 * rows * width * (wide_a + wide_b),
+            transcendentals=0,
+            bytes_accessed=2 * width * (wide_a + wide_b),
+        ),
+    )(left_a, right_a, left_b, right_b)
 
 
 def local(
@@ -180,7 +457,7 @@
         key_ids[:, None, :] == local_ids[:, :, None]
     )
     hops = min(lax.axis_size("seq") - 1, (MAX_DOC - 2) // rows + 1)
-    spare = -(mamba_dt.shape[1] + 2) % LANES
+    spare = -(mamba_dt.shape[1] + 2) % (2 * LANES)
     shard_in = jnp.concatenate(
         [
             mamba_z,
@@ -228,20 +505,35 @@
     for tap in range(taps):
         conv_pre = conv_pre + conv_weight[tap] * extended[:, tap : tap + rows] * tap_masks[tap]
     activated = jax.nn.silu(conv_pre)
-    xs = activated[:, :, :inner_width].reshape(sequences, rows, SSM_HEADS, SSM_HEAD)
-    bmat = activated[:, :, inner_width : inner_width + STATE]
-    cmat = activated[:, :, inner_width + STATE :]
-    step = jax.nn.softplus(step_raw + dt_bias).reshape(sequences, rows, SSM_HEADS)
-    pair, inbound, outbound = block_masks(local_ids, prior_id)
-    state_local, carry = block_summary(xs, bmat, step, a_log, inbound, outbound)
+    act = activated.reshape(total_rows, channels)
+    step = jax.nn.softplus(step_raw + dt_bias)
+    ids = local_ids.reshape(total_rows)
+    order = jnp.arange(rows)
+    pair = (order[:, None] >= order[None, :]) & (ids[:, None] == ids[None, :])
+    bias = jnp.where(pair, 0.0, -1e30).astype(jnp.float32)
+    bias_turned = jnp.where(
+        (order[:, None] <= order[None, :]) & (ids[:, None] == ids[None, :]), 0.0, -1e30
+    ).astype(jnp.float32)
+    inbound = (ids == prior_id[0]).astype(jnp.float32)[:, None]
+    outbound = (ids == ids[-1]).astype(jnp.float32)[:, None]
+    rate = -jnp.exp(a_log)
+    ladder = (order[:, None] >= order[None, :]).astype(jnp.float32)
+    decay = jnp.dot(ladder, step * rate, precision=lax.Precision.HIGHEST)
+    entry = jnp.exp(decay) * inbound
+    tail = jnp.exp(decay[-1:] - decay) * outbound
+    carry = jnp.exp(decay[-1]) * inbound[-1, 0]
+    cols = jnp.stack([decay, step, entry, tail], axis=1)
+    cols = cols.reshape(rows, 4, SSM_PAIRS, 2).transpose(2, 0, 1, 3).reshape(SSM_PAIRS, rows, 8)
+    turned = decay.T.reshape(SSM_PAIRS, 2, rows)
+    skip_row = jnp.repeat(d_skip, SSM_HEAD)[None, :]
+    carry_rows = jnp.repeat(carry, SSM_HEAD).reshape(SSM_PAIRS, LANES, 1)
+    local_part, state_local = ssm_local(act, cols, turned, bias)
     outgoing = state_local
-    incoming = jnp.zeros_like(state_local)
     for hop in range(hops):
-        incoming = passed_along(outgoing.astype(jnp.bfloat16), "seq", 1).astype(outgoing.dtype)
-        outgoing = carry[:, :, None, None] * incoming + state_local
-    ssm_out = block_output(xs, bmat, cmat, step, a_log, d_skip, incoming, pair, inbound)
+        incoming = passed_along(outgoing.astype(jnp.bfloat16), "seq", 1)
+        outgoing = carry_rows * incoming.astype(jnp.float32) + state_local
+    ssm_out, gated = ssm_carried(local_part, act, cols, incoming, skip_row, projected)
     silu_z = jax.nn.silu(gate_z)
-    gated = ssm_out.reshape(total_rows, inner_width) * silu_z
     mixed_norm, factor_m = rms_forward(gated, inner_norm)
     mixed_b = mixed_norm.astype(jnp.bfloat16)
     query = projected[:, at_q:at_kv].reshape(sequences, rows, Q_HEADS, HEAD)
@@ -284,40 +576,47 @@
         (mid + matmul_nt(hidden_b, full_down)).astype(jnp.bfloat16).reshape(sequences, rows, width)
     )
     grad_flat = grad_out.reshape(total_rows, width)
-    g_down = matmul_tn(grad_flat, hidden_b).astype(jnp.bfloat16)
     d_hidden = matmul(grad_flat, full_down)
     d_gate_b = (d_hidden * up_h * silu_grad(gate_h)).astype(jnp.bfloat16)
     d_up_b = (d_hidden * jax.nn.silu(gate_h)).astype(jnp.bfloat16)
     d_gateup_b = jnp.concatenate([d_gate_b, d_up_b], axis=1)
-    g_gateup = matmul_tn(fnormed_b, d_gateup_b).astype(jnp.bfloat16)
-    owned_ffn = scattered(jnp.concatenate([g_gateup, g_down], axis=1))
+    part_ffn = scattered_dp(outer_pair(fnormed_b, d_gateup_b, grad_flat, hidden_b))
     d_fnorm = matmul_nt(d_gateup_b, full_gateup)
     d_mid_norm, g_fnorm = rms_backward(mid, factor_two, gain_two, d_fnorm)
     d_mid = grad_flat.astype(jnp.float32) + d_mid_norm
     d_mid_b = d_mid.astype(jnp.bfloat16)
-    g_mixers = matmul_tn(d_mid_b, mixers_b).astype(jnp.bfloat16)
     d_mixers = matmul(d_mid_b, full_mixer)
     d_mnorm = d_mixers[:, :inner_width]
     d_gated, g_inner = rms_backward(gated, factor_m, inner_norm, d_mnorm)
-    d_ssm = (d_gated * silu_z).reshape(sequences, rows, SSM_HEADS, SSM_HEAD)
-    d_z = d_gated * ssm_out.reshape(total_rows, inner_width) * silu_grad(gate_z)
-    entry = jnp.exp(jnp.cumsum(step * -jnp.exp(a_log), axis=1)) * inbound[:, :, None]
-    direct = jnp.einsum("sth,sthp,stn->shpn", entry, d_ssm, cmat, precision=lax.Precision.HIGHEST)
+    d_ssm = d_gated * silu_z
+    d_z = d_gated * ssm_out * silu_grad(gate_z)
+    direct = ssm_direct(d_ssm, act, cols)
     backlog = direct
-    later_grad = jnp.zeros_like(direct)
     for hop in range(hops):
-        later_grad = passed_along(backlog.astype(jnp.bfloat16), "seq", -1).astype(backlog.dtype)
-        backlog = direct + carry[:, :, None, None] * later_grad
-    d_carry = jnp.sum(later_grad * incoming, axis=(2, 3))
-
-    def local_ssm(xs_a, bmat_a, cmat_a, step_a, alog_a, skip_a):
-        result = block_output(xs_a, bmat_a, cmat_a, step_a, alog_a, skip_a, incoming, pair, inbound)
-        summary, carry_a = block_summary(xs_a, bmat_a, step_a, alog_a, inbound, outbound)
-        return (result, summary, carry_a)
-
-    primal, pullback = jax.vjp(local_ssm, xs, bmat, cmat, step, a_log, d_skip)
-    d_xs, d_bmat, d_cmat, d_step, g_alog, g_skip = pullback((d_ssm, later_grad, d_carry))
-    d_act = jnp.concatenate([d_xs.reshape(sequences, rows, inner_width), d_bmat, d_cmat], axis=2)
+        later_grad = passed_along(backlog.astype(jnp.bfloat16), "seq", -1)
+        backlog = direct + carry_rows * later_grad.astype(jnp.float32)
+    d_carry = jnp.sum(
+        (later_grad.astype(jnp.float32) * incoming.astype(jnp.float32)).reshape(
+            SSM_HEADS, SSM_HEAD, STATE
+        ),
+        axis=(1, 2),
+    )
+    d_xs, d_bmat, d_cmat, d_cols, d_rows = ssm_backward(
+        d_ssm, act, ssm_out, cols, turned, bias_turned, incoming, later_grad, skip_row
+    )
+    d_pairs = d_cols[:, :, :6].reshape(SSM_PAIRS, rows, 3, 2).transpose(2, 1, 0, 3)
+    d_pairs = d_pairs.reshape(3, rows, SSM_HEADS)
+    d_sums = jnp.sum(d_rows.reshape(SSM_PAIRS, 2, 2, SSM_HEAD), axis=3).transpose(1, 0, 2)
+    d_sums = d_sums.reshape(2, SSM_HEADS)
+    g_skip = d_sums[1]
+    d_decay = d_pairs[0] - d_pairs[2]
+    d_rise = jnp.dot(ladder.T, d_decay, precision=lax.Precision.HIGHEST)
+    d_rise = d_rise + (d_sums[0] + d_carry * carry)
+    d_step = d_pairs[1] + d_rise * rate
+    g_alog = jnp.sum(d_rise * step, axis=0) * rate
+    d_act = jnp.concatenate([d_xs, d_bmat, d_cmat], axis=1).reshape(sequences, rows, channels)
+    d_act, part_ffn = lax.optimization_barrier((d_act, part_ffn))
+    owned_ffn = scattered_seq(part_ffn)
     d_pre = d_act * silu_grad(conv_pre)
     g_cbias = jnp.sum(d_pre, axis=(0, 1))
     g_cweight = jnp.stack(
@@ -386,8 +685,9 @@
         ],
         axis=1,
     )
-    g_projected = matmul_tn(normed_b, d_projected).astype(jnp.bfloat16)
-    owned_rest = scattered(jnp.concatenate([g_projected, g_mixers], axis=1))
+    g_rest = outer_pair(normed_b, d_projected, d_mid_b, mixers_b)
+    g_rest, owned_ffn = lax.optimization_barrier((g_rest, owned_ffn))
+    owned_rest = scattered_seq(scattered_dp(g_rest))
     d_norm = matmul_nt(d_projected, full_in)
     d_in_norm, g_mnorm = rms_backward(x_in, factor_one, gain_one, d_norm)
     grad_in = (d_mid + d_in_norm).astype(jnp.bfloat16).reshape(sequences, rows, width)

time: 602 us -> 568 us (0.944)
  Pallas kernels: 0 us -> 77.5 us
  matrix products: 115 us -> 61.2 us
  other arithmetic: 78.5 us -> 50.3 us
  local copies, waits for them, and re-layouts: 64.7 us -> 44.8 us
  starting transfers between devices: 33.7 us -> 24.6 us
    pallas_call x0 -> x6, Pallas kernels: none -> 77.5 us  [the longest x2 31.8 us: outer_pair(): pl.pallas_call(functools.partial(outer_kernel, split), grid=(total,), in_...]
    dot_general x16 -> x2, matrix products: 54 us -> 1.5 us  [the longest x1 1.23 us: local(): d_rise = jnp.dot(ladder.T, d_decay, precision=lax.Precision.HIGHEST)]
    reduce_scatter x4, waiting for transfers between devices: 112 us -> 95.7 us  [the longest x2 95.6 us: scattered_dp(): return lax.psum_scatter(grad, 'dp', scatter_dimension=0, tiled=True)]
    ppermute x10, waiting for transfers between devices: 35.5 us -> 51.2 us  [passed_along(): return lax.ppermute(block, axis, route)]
    concatenate x2, other arithmetic: 16.3 us -> 4.11 us  [the longest x1 2.41 us: local(): mixers_b = jnp.concatenate([mixed_b, attended_b], axis=1)]
    ppermute x10, starting transfers between devices: 33.5 us -> 24.1 us  [passed_along(): return lax.ppermute(block, axis, route)]
    mul x5 -> x1, local copies, waits for them, and re-layouts: 9.4 us -> 0.08 us  [local(): carry = jnp.exp(decay[-1]) * inbound[-1, 0]]
    mul x6 -> x4, other arithmetic: 12.9 us -> 3.93 us  [the longest x1 2.5 us: local(): d_ssm = d_gated * silu_z]
  transfers between devices with their start and end apart: 16 -> 16, of which waited for: 7 -> 10; matrix products, arithmetic and copies ran while one was open for 36% -> 21% of each run, Pallas kernels for 0% -> 12%
where the time goes in v2:
time: 568 us; the launch traced here: 557 us
  waiting for transfers between devices  241 us (42%)
  Pallas kernels  77.5 us (14%)
  matrix products  61.2 us (11%)
  other arithmetic  50.3 us (9%)
  local copies, waits for them, and re-layouts  44.8 us (8%)
  blocking collectives  42 us (7%)
  starting transfers between devices  24.6 us (4%)
  between operations  16 us (3%)
    reduce_scatter x2, waiting for transfers between devices, scattered_dp(): return lax.psum_scatter(grad, 'dp', scatter_dimension=0, tiled=True)  95.6 us
    all_gather x1, waiting for transfers between devices, local(): full_in = lax.all_gather(shard_in, ('dp', 'seq'), axis=0, tiled=True)  69.2 us
    ppermute x10, waiting for transfers between devices, passed_along(): return lax.ppermute(block, axis, route)  51.2 us
    psum x1, blocking collectives, local(): lax.psum((g_cweight, g_cbias, g_dtb, g_alog, g_skip, g_inner, g_mnorm, g_...  42 us
    pallas_call x2, Pallas kernels, outer_pair(): pl.pallas_call(functools.partial(outer_kernel, split), grid=(total,), in_...  31.8 us
    all_gather x1, waiting for transfers between devices, local(): full_out = lax.all_gather(shard_out, ('dp', 'seq'), axis=0, tiled=True)  24.6 us
    ppermute x10, starting transfers between devices, passed_along(): return lax.ppermute(block, axis, route)  24.1 us
    dot_general x4, matrix products, matmul(): return jnp.dot(left, right, preferred_element_type=jnp.float32)  22.5 us
  transfers between devices with their start and end apart: 16, of which 10 were waited for; matrix products, arithmetic and copies ran while one was open for 21% of the time, Pallas kernels for 12%

profile of v2, /device:TPU:0, one launch (start us, length us, event | category | flops | bytes accessed | tf_op | source)
XLA Modules:
  0.0 557.2 jit_solution(2712771704142301397)
XLA Ops:
  24.2 69.2 %all-gather.3.cloned.1.call-done = bf16[1024,4352]{1,0:T(8,128)(2,1)} async-done(((bf16[32,4352]{1,0:T(8,128)(2,1)}), bf16[1024,4352]{1,0:T(8,128)(2,1)}) %all-gather.3.cloned.1.call-update) | async-done | bytes 8912912 | tf_op jit(solution)/shard_map/all_gather | solution.py:476
  95.6 6.2 %fusion.80.z_ref = f32[256,4352]{1,0:T(8,128)S(1)} fusion(bf16[256,1024]{1,0:T(8,128)(2,1)S(1)} %fusion.41.left_a_ref, bf16[1024,4352]{1,0:T(8,128)(2,1)} %all-gather.3.cloned.1.call-done), kind=kOutput, calls=%fused_computation.202 | convolution fusion | flops 2281701376 | bytes 13893632 | tf_op jit(solution)/shard_map/dot_general | solution.py:60
  129.9 11.5 %ssm_local.1 = (f32[256,1536]{1,0:T(8,128)}, f32[12,128,128]{2,1,0:T(8,128)}) custom-call(f32[256,1792]{1,0:T(8,128)} %get-tuple-element.187.xs_ref.b_ref.c_ref, f32[256,1792]{1,0:T(8,128)} %get-tuple-element.187.xs_ref.b_ref.c_ref, f32[256,1792]{1,0:T(8,128)} %get-tuple-element.187.xs_ref.b_ref.c_ref, f32[12,256,8]{2,1,0:T(8,128)} %copy.157.cols_ref, ...), custom_call_target="tpu_custom_call" | custom-call | flops 1000000000 | bytes 6000000 | tf_op jit(solution)/shard_map/ssm_local/pallas_call | solution.py:288
  149.8 13.1 %collective-permute-done.1 = bf16[12,128,128]{2,1,0:T(8,128)(2,1)S(1)} collective-permute-done((bf16[12,128,128]{2,1,0:T(8,128)(2,1)S(1)}, bf16[12,128,128]{2,1,0:T(8,128)(2,1)S(1)}, u32[]{:S(2)}, u32[]{:S(2)}) %collective-permute-start.1) | collective-permute-done | bytes 393248 | tf_op jit(solution)/shard_map/ppermute | solution.py:29
  163.1 4.8 collective-permute-start.2
  170.5 13.5 %collective-permute-done.2.state_ref = bf16[12,128,128]{2,1,0:T(8,128)(2,1)S(1)} collective-permute-done((bf16[12,128,128]{2,1,0:T(8,128)(2,1)S(1)}, bf16[12,128,128]{2,1,0:T(8,128)(2,1)S(1)}, u32[]{:S(2)}, u32[]{:S(2)}) %collective-permute-start.2) | collective-permute-done | bytes 393248 | tf_op jit(solution)/shard_map/ppermute | solution.py:29
  184.8 9.9 %ssm_carried.1 = (f32[256,1536]{1,0:T(8,128)}, f32[256,1536]{1,0:T(8,128)}) custom-call(f32[256,1536]{1,0:T(8,128)} %get-tuple-element.34.local_ref, f32[256,1792]{1,0:T(8,128)} %get-tuple-element.187.xs_ref.b_ref.c_ref, f32[256,1792]{1,0:T(8,128)} %get-tuple-element.187.xs_ref.b_ref.c_ref, f32[12,256,8]{2,1,0:T(8,128)} %copy.157.cols_ref, ...), custom_call_target="tpu_custom_call" | custom-call | flops 100000000 | bytes 9000000 | tf_op jit(solution)/shard_map/ssm_carried/pallas_call | solution.py:307
  197.8 24.6 %all-gather.5.cloned.1.call-done = bf16[1024,8192]{1,0:T(8,128)(2,1)} async-done(((bf16[32,8192]{1,0:T(8,128)(2,1)}), bf16[1024,8192]{1,0:T(8,128)(2,1)}) %all-gather.5.cloned.1.call-update) | async-done | bytes 16777232 | tf_op jit(solution)/shard_map/all_gather | solution.py:477
  227.2 5.9 %fusion.2 = f32[256,4096]{1,0:T(8,128)S(1)} fusion(bf16[256,1024]{1,0:T(8,128)(2,1)S(1)} %multiply_convert_fusion.5.left_a_ref, bf16[1024,8192]{1,0:T(8,128)(2,1)} %all-gather.5.cloned.1.call-done), kind=kOutput, calls=%fused_computation.2 | convolution fusion | flops 2147483648 | bytes 13107200 | tf_op jit(solution)/shard_map/dot_general | solution.py:60
  233.1 5.1 multiply_convert_fusion.1
  240.2 12.3 %outer_pair.2 = bf16[1024,6144]{1,0:T(8,128)(2,1)} custom-call(bf16[256,1024]{1,0:T(8,128)(2,1)} %copy-done.21, bf16[256,4096]{1,0:T(8,128)(2,1)} %pad_maximum_fusion.right_a_ref, bf16[256,1024]{1,0:T(8,128)(2,1)} %bitcast.186, bf16[256,2048]{1,0:T(8,128)(2,1)} %get-tuple-element.195.right_b_ref), custom_call_target="tpu_custom_call" | custom-call | flops 3221225472 | bytes 12582912 | tf_op jit(solution)/shard_map/outer_pair/pallas_call | solution.py:381
  255.9 6.4 %multiply_reduce_fusion.7 = (f32[1024]{0:T(1024)}, f32[256]{0:T(256)S(1)}, f32[256,1024]{1,0:T(8,128)S(1)}) fusion(f32[256,1024]{1,0:T(8,128)S(1)} %get-tuple-element.239, f32[256]{0:T(256)} %copy-done.61, f32[1024]{0:T(1024)} %get-tuple-element.152, bf16[1024,8192]{1,0:T(8,128)(2,1)} %all-gather.5.cloned.1.call-done, bf16[256,2048]{1,0:T(8,128)(2,1)S(1)} %copy-done.34, ...), kind=kOutput, calls=%fused_computation.90 | convolution fusion | flops 2153249536 | bytes 12593152 | tf_op jit(solution)/shard_map/dot_general | solution.py:64
  264.1 5.2 fusion.12
  273.5 9.7 %ssm_direct.1 = f32[12,128,128]{2,1,0:T(8,128)} custom-call(f32[256,1536]{1,0:T(8,128)} %get-tuple-element.191.g_ref, f32[256,1792]{1,0:T(8,128)} %get-tuple-element.187.xs_ref.b_ref.c_ref, f32[12,256,8]{2,1,0:T(8,128)} %copy.157.cols_ref), custom_call_target="tpu_custom_call" | custom-call | flops 100000000 | bytes 4000000 | tf_op jit(solution)/shard_map/ssm_direct/pallas_call | solution.py:321
  286.7 4.9 fusion.4
  309.0 10.8 %collective-permute-done.9 = bf16[1,256,256]{1,2,0:T(8,128)(2,1)S(1)} collective-permute-done((bf16[1,256,256]{1,2,0:T(8,128)(2,1)S(1)}, bf16[1,256,256]{1,2,0:T(8,128)(2,1)S(1)}, u32[]{:S(2)}, u32[]{:S(2)}) %collective-permute-start.9) | collective-permute-done | bytes 131104 | tf_op jit(solution)/shard_map/ppermute | solution.py:29
  320.0 7.5 %collective-permute-done.6.later_ref = bf16[12,128,128]{2,1,0:T(8,128)(2,1)S(1)} collective-permute-done((bf16[12,128,128]{2,1,0:T(8,128)(2,1)S(1)}, bf16[12,128,128]{2,1,0:T(8,128)(2,1)S(1)}, u32[]{:S(2)}, u32[]{:S(2)}) %collective-permute-start.6) | collective-permute-done | bytes 393248 | tf_op jit(solution)/shard_map/ppermute | solution.py:29
  328.3 14.6 %ssm_backward.1 = (f32[256,1536]{1,0:T(8,128)}, f32[256,128]{1,0:T(8,128)}, f32[256,128]{1,0:T(8,128)}, f32[12,256,8]{2,1,0:T(8,128)}, f32[12,2,128]{2,1,0:T(2,128)}) custom-call(f32[256,1536]{1,0:T(8,128)} %get-tuple-element.191.g_ref, f32[256,1792]{1,0:T(8,128)} %get-tuple-element.187.xs_ref.b_ref.c_ref, f32[256,1536]{1,0:T(8,128)} %get-tuple-element.37.out_ref, ...), custom_call_target="tpu_custom_call" | custom-call | flops 2000000000 | bytes 12000000 | tf_op jit(solution)/shard_map/ssm_backward/pallas_call | solution.py:335
  357.8 6.3 %collective-permute-done.7 = f32[1,3,1792]{2,1,0:T(4,128)S(1)} collective-permute-done((f32[1,3,1792]{2,1,0:T(4,128)S(1)}, f32[1,3,1792]{2,1,0:T(4,128)S(1)}, u32[]{:S(2)}, u32[]{:S(2)}) %collective-permute-start.7) | collective-permute-done | bytes 21536 | tf_op jit(solution)/shard_map/ppermute | solution.py:29
  367.3 19.5 %outer_pair.3 = bf16[1024,6400]{1,0:T(8,128)(2,1)} custom-call(bf16[256,1024]{1,0:T(8,128)(2,1)} %copy-done.19, bf16[256,4352]{1,0:T(8,128)(2,1)} %concatenate.98.right_a_ref, bf16[256,1024]{1,0:T(8,128)(2,1)} %copy-done.20, bf16[256,2048]{1,0:T(8,128)(2,1)} %pad_maximum_fusion.2.right_b_ref), custom_call_target="tpu_custom_call" | custom-call | flops 3355443200 | bytes 13107200 | tf_op jit(solution)/shard_map/outer_pair/pallas_call | solution.py:381
  389.0 95.0 %reduce-scatter.9.cloned.1.call-done = bf16[128,6400]{1,0:T(8,128)(2,1)} async-done(((bf16[1024,6400]{1,0:T(8,128)(2,1)}), bf16[128,6400]{1,0:T(8,128)(2,1)}) %reduce-scatter.9.cloned.1.call-update) | async-done | bytes 1638416 | tf_op jit(solution)/shard_map/reduce_scatter | solution.py:33
  484.1 4.7 fusion.36
  489.1 7.4 %fusion.50 = (f32[1024]{0:T(1024)S(1)}, f32[256]{0:T(256)S(1)}, f32[256,1024]{1,0:T(8,128)}) fusion(bf16[1,256,1024]{2,1,0:T(8,128)(2,1)} %param.22, f32[256]{0:T(256)S(1)} %copy-done.69, f32[1024]{0:T(1024)S(1)} %copy-done.56, bf16[256,4352]{1,0:T(8,128)(2,1)S(1)} %copy-done.7, bf16[1024,4352]{1,0:T(8,128)(2,1)} %all-gather.3.cloned.1.call-done), kind=kOutput, calls=%fused_computation.88 | convolution fusion | flops 2283535104 | bytes 12724224 | tf_op jit(solution)/shard_map/dot_general | solution.py:64
  496.5 42.0 %all-reduce.7 = (f32[1024]{0:T(1024)S(1)}, f32[1024]{0:T(1024)S(1)}, f32[4,1792]{1,0:T(4,128)}, f32[1792]{0:T(1024)}, f32[24]{0:T(128)}, /*index=5*/f32[24]{0:T(128)}, f32[24]{0:T(128)}, f32[1536]{0:T(1024)}) all-reduce(f32[1024]{0:T(1024)S(1)} %get-tuple-element.166, ...), channel_id=1, replica_groups=mesh['dp'=8,'seq'=4] {'dp','seq'}, use_global_device_ids=true, to_apply=%region_17.18 | all-reduce | flops 12616 | bytes 100928 | tf_op jit(solution)/shard_map/psum | solution.py:694
  (342 shorter events, 130.9 us)
Async XLA Ops:
  7.2 86.1 %all-gather.3.cloned.1.call-start = ((), (), s32[]{:S(2)}) async-start(), calls=%async_computation.4 | async-start | bytes 9191424 | tf_op jit(solution)/shard_map/all_gather | solution.py:476
  11.4 211.0 %all-gather.5.cloned.1.call-start = ((), (), s32[]{:S(2)}) async-start(), calls=%async_computation.5 | async-start | bytes 17301504 | tf_op jit(solution)/shard_map/all_gather | solution.py:477
  16.7 332.0 %reduce-scatter.5.cloned.1.call-start = ((), (), s32[]{:S(2)}) async-start(), calls=%async_computation.6 | async-start | bytes 14155776 | tf_op jit(solution)/shard_map/reduce_scatter | solution.py:33
  21.4 103.8 %copy-start.46 = (f32[1792]{0:T(1024)}, f32[1792]{0:T(1024)S(1)}, u32[]{:S(2)}) copy-start(f32[1792]{0:T(1024)S(1)} %get-tuple-element.168) | copy-start | bytes 21508
  21.4 103.8 %copy-start.48 = (f32[1792]{0:T(1024)}, f32[1792]{0:T(1024)S(1)}, u32[]{:S(2)}) copy-start(f32[1792]{0:T(1024)S(1)} %get-tuple-element.169) | copy-start | bytes 21508
  22.1 79.7 %copy-start.68 = (f32[256]{0:T(256)}, f32[256]{0:T(256)S(1)}, u32[]{:S(2)}) copy-start(f32[256]{0:T(256)S(1)} %add_rsqrt_fusion.2) | copy-start | bytes 3076
  104.2 42.0 %collective-permute-start.4 = (bf16[1,256,256]{1,2,0:T(8,128)(2,1)S(1)}, bf16[1,256,256]{1,2,0:T(8,128)(2,1)}, u32[]{:S(2)}, u32[]{:S(2)}) collective-permute-start(bf16[1,256,256]{1,2,0:T(8,128)(2,1)S(1)} %bitcast.200), channel_id=1, source_target_pairs={{0,1},{1,2},{2,3},{4,5},{5,6},{6,7},{8,9},{9,10},{10,11},{12,13},{... | collective-permute-start | bytes 393224 | tf_op jit(solution)/shard_map/ppermute | solution.py:29
  108.3 38.0 %collective-permute-start.3 = (bf16[1,256,256]{1,2,0:T(8,128)(2,1)S(1)}, bf16[1,256,256]{1,2,0:T(8,128)(2,1)}, u32[]{:S(2)}, u32[]{:S(2)}) collective-permute-start(bf16[1,256,256]{1,2,0:T(8,128)(2,1)S(1)} %bitcast.201), channel_id=1, source_target_pairs={{0,2},{1,3},{4,6},{5,7},{8,10},{9,11},{12,14},{13,15},{16,18},{17,... | collective-permute-start | bytes 393224 | tf_op jit(solution)/shard_map/ppermute | solution.py:29
  113.8 11.4 %collective-permute-start = (f32[1,3,1792]{2,1,0:T(4,128)}, f32[1,3,1792]{2,1,0:T(4,128)}, u32[]{:S(2)}, u32[]{:S(2)}) collective-permute-start(f32[1,3,1792]{2,1,0:T(4,128)} %slice.294), channel_id=1, source_target_pairs={{0,1},{1,2},{2,3},{4,5},{5,6},{6,7},{8,9},{9,10},{10,11},{12,13},{... | collective-permute-start | bytes 64520 | tf_op jit(solution)/shard_map/ppermute | solution.py:29
  142.7 20.2 %collective-permute-start.1 = (bf16[12,128,128]{2,1,0:T(8,128)(2,1)S(1)}, bf16[12,128,128]{2,1,0:T(8,128)(2,1)S(1)}, u32[]{:S(2)}, u32[]{:S(2)}) collective-permute-start(bf16[12,128,128]{2,1,0:T(8,128)(2,1)S(1)} %convert_element_type.200), channel_id=1, source_target_pairs={{0,1},{1,2},{2,3},{4,5},{5,6},{6,7},{8,9},{9,10},{10,11},{12,13},{... | collective-permute-start | bytes 1179656 | tf_op jit(solution)/shard_map/ppermute | solution.py:29
  163.1 20.9 %collective-permute-start.2 = (bf16[12,128,128]{2,1,0:T(8,128)(2,1)S(1)}, bf16[12,128,128]{2,1,0:T(8,128)(2,1)S(1)}, u32[]{:S(2)}, u32[]{:S(2)}) collective-permute-start(bf16[12,128,128]{2,1,0:T(8,128)(2,1)S(1)} %add_convert_fusion.1), channel_id=1, source_target_pairs={{0,1},{1,2},{2,3},{4,5},{5,6},{6,7},{8,9},{9,10},{10,11},{12,13},{... | collective-permute-start | bytes 1179656 | tf_op jit(solution)/shard_map/ppermute | solution.py:29
  226.3 35.9 %copy-start.5 = (f32[256,1024]{1,0:T(8,128)}, f32[256,1024]{1,0:T(8,128)S(1)}, u32[]{:S(2)}) copy-start(f32[256,1024]{1,0:T(8,128)S(1)} %get-tuple-element.239) | copy-start | bytes 3145732
  252.5 134.4 %reduce-scatter.7.cloned.1.call-start = ((), (), s32[]{:S(2)}) async-start(), calls=%async_computation.7 | async-start | bytes 1966080 | tf_op jit(solution)/shard_map/reduce_scatter | solution.py:37
  285.2 20.9 %collective-permute-start.5 = (bf16[12,128,128]{2,1,0:T(8,128)(2,1)}, bf16[12,128,128]{2,1,0:T(8,128)(2,1)}, u32[]{:S(2)}, u32[]{:S(2)}) collective-permute-start(bf16[12,128,128]{2,1,0:T(8,128)(2,1)} %convert_element_type.222), channel_id=1, source_target_pairs={{1,0},{2,1},{3,2},{5,4},{6,5},{7,6},{9,8},{10,9},{11,10},{13,12},{... | collective-permute-start | bytes 1179656 | tf_op jit(solution)/shard_map/ppermute | solution.py:29
  303.4 16.4 %collective-permute-start.9 = (bf16[1,256,256]{1,2,0:T(8,128)(2,1)S(1)}, bf16[1,256,256]{1,2,0:T(8,128)(2,1)S(1)}, u32[]{:S(2)}, u32[]{:S(2)}) collective-permute-start(bf16[1,256,256]{1,2,0:T(8,128)(2,1)S(1)} %get-tuple-element.215), channel_id=1, source_target_pairs={{2,0},{3,1},{6,4},{7,5},{10,8},{11,9},{14,12},{15,13},{18,16},{19,... | collective-permute-start | bytes 393224 | tf_op jit(solution)/shard_map/ppermute | solution.py:29
  304.8 15.0 %collective-permute-start.8 = (bf16[1,256,256]{1,2,0:T(8,128)(2,1)S(1)}, bf16[1,256,256]{1,2,0:T(8,128)(2,1)S(1)}, u32[]{:S(2)}, u32[]{:S(2)}) collective-permute-start(bf16[1,256,256]{1,2,0:T(8,128)(2,1)S(1)} %get-tuple-element.214), channel_id=1, source_target_pairs={{1,0},{2,1},{3,2},{5,4},{6,5},{7,6},{9,8},{10,9},{11,10},{13,12},{... | collective-permute-start | bytes 393224 | tf_op jit(solution)/shard_map/ppermute | solution.py:29
  307.4 20.1 %collective-permute-start.6 = (bf16[12,128,128]{2,1,0:T(8,128)(2,1)S(1)}, bf16[12,128,128]{2,1,0:T(8,128)(2,1)S(1)}, u32[]{:S(2)}, u32[]{:S(2)}) collective-permute-start(bf16[12,128,128]{2,1,0:T(8,128)(2,1)S(1)} %add_convert_fusion), channel_id=1, source_target_pairs={{1,0},{2,1},{3,2},{5,4},{6,5},{7,6},{9,8},{10,9},{11,10},{13,12},{... | collective-permute-start | bytes 1179656 | tf_op jit(solution)/shard_map/ppermute | solution.py:29
  348.7 135.2 %reduce-scatter.9.cloned.1.call-start = ((), (), s32[]{:S(2)}) async-start(), calls=%async_computation.8 | async-start | bytes 14745600 | tf_op jit(solution)/shard_map/reduce_scatter | solution.py:33
  355.9 8.2 %collective-permute-start.7 = (f32[1,3,1792]{2,1,0:T(4,128)S(1)}, f32[1,3,1792]{2,1,0:T(4,128)S(1)}, u32[]{:S(2)}, u32[]{:S(2)}) collective-permute-start(f32[1,3,1792]{2,1,0:T(4,128)S(1)} %pad_add_fusion.1), channel_id=1, source_target_pairs={{1,0},{2,1},{3,2},{5,4},{6,5},{7,6},{9,8},{10,9},{11,10},{13,12},{... | collective-permute-start | bytes 64520 | tf_op jit(solution)/shard_map/ppermute | solution.py:29
  388.9 95.1 %copy-start.6 = (f32[256,1024]{1,0:T(8,128)S(1)}, f32[256,1024]{1,0:T(8,128)}, u32[]{:S(2)}) copy-start(f32[256,1024]{1,0:T(8,128)} %copy-done.5) | copy-start | bytes 3145732
  388.9 155.0 %reduce-scatter.11.cloned.1.call-start = ((), (), s32[]{:S(2)}) async-start(), calls=%async_computation.9 | async-start | bytes 2048000 | tf_op jit(solution)/shard_map/reduce_scatter | solution.py:37
  489.1 50.6 %copy-start.54 = (f32[1024]{0:T(1024)S(1)}, f32[1024]{0:T(1024)}, u32[]{:S(2)}) copy-start(f32[1024]{0:T(1024)} %get-tuple-element.152) | copy-start | bytes 12292
  489.1 50.6 %copy-start.63 = (f32[256]{0:T(256)S(1)}, f32[256]{0:T(256)}, u32[]{:S(2)}) copy-start(f32[256]{0:T(256)} %copy-done.61) | copy-start | bytes 3076
  489.1 50.6 %copy-start.71 = (f32[256]{0:T(256)S(1)}, f32[256]{0:T(256)}, u32[]{:S(2)}) copy-start(f32[256]{0:T(256)} %copy-done.70) | copy-start | bytes 3076
  (78 other events, 423.0 us)
Sparse Core Ops, SparseCore 0:
  11.5 81.7 all-gather.2
  96.9 125.4 all-gather.4
  252.6 96.0 reduce-scatter.4
  350.9 36.0 reduce-scatter.6
  390.4 93.5 reduce-scatter.8
  486.1 37.1 reduce-scatter.10

commit v3 on v2

--- a/solution.py
+++ b/solution.py
@@ -21,6 +21,7 @@
 MAX_DOC = 512
 LANES = 128
 SSM_PAIRS = SSM_HEADS * SSM_HEAD // LANES
+PAIR_GROUP = 4
 
 
 def passed_along(block, axis, distance):
@@ -35,6 +36,39 @@
 
 def scattered_seq(part):
     return lax.psum_scatter(part, "seq", scatter_dimension=0, tiled=True).astype(jnp.float32)
+
+
+def gathered_seq(shard):
+    index = lax.axis_index("seq")
+    count = lax.axis_size("seq")
+    held = shard
+    bit = 1
+    while bit < count:
+        got = lax.ppermute(held, "seq", [(i, i ^ bit) for i in range(count)])
+        odd = (index // bit) % 2 == 1
+        held = jnp.concatenate([jnp.where(odd, got, held), jnp.where(odd, held, got)], axis=0)
+        bit *= 2
+    return held
+
+
+def hopped_seq(part, rider):
+    index = lax.axis_index("seq")
+    count = lax.axis_size("seq")
+    held = part.reshape(count, part.shape[0] // count, part.shape[1])
+    bit = 1
+    while bit < count:
+        halves = held.reshape(held.shape[0] // 2, 2, *held.shape[1:])
+        odd = (index // bit) % 2 == 1
+        mine = jnp.where(odd, halves[:, 1], halves[:, 0])
+        other = jnp.where(odd, halves[:, 0], halves[:, 1])
+        got = lax.ppermute(other, "seq", [(i, i ^ bit) for i in range(count)])
+        held = mine.astype(jnp.float32) + got.astype(jnp.float32)
+        bit *= 2
+        if bit < count:
+            held = held.astype(jnp.bfloat16)
+        if bit == 2 and rider is not None:
+            held, rider = lax.optimization_barrier((held, rider))
+    return held[0].astype(jnp.float32), rider
 
 
 def silu_grad(value):
@@ -108,7 +142,27 @@
     )
 
 
-def ssm_local_kernel(xs_ref, b_ref, c_ref, cols_ref, rows_ref, bias_ref, out_ref, state_ref, cb_ref):
+def each_pair(body):
+    for k in range(PAIR_GROUP):
+        body(k, pl.ds(k * LANES, LANES))
+
+
+def ssm_state_kernel(xs_ref, b_ref, cols_ref, state_ref):
+    b_low = b_ref[...].astype(jnp.bfloat16)
+
+    def one(k, lanes):
+        xs = xs_ref[:, lanes]
+        cols = cols_ref[k]
+        scaled = xs * half_lanes(cols, 2, xs.shape)
+        tailed = (scaled * half_lanes(cols, 6, xs.shape)).astype(jnp.bfloat16)
+        state_ref[k] = lax.dot_general(
+            tailed, b_low, (((0,), (0,)), ((), ())), preferred_element_type=jnp.float32
+        )
+
+    each_pair(one)
+
+
+def ssm_local_kernel(xs_ref, b_ref, c_ref, cols_ref, rows_ref, bias_ref, out_ref, cb_ref):
     bmat = b_ref[...]
 
     @pl.when(pl.program_id(0) == 0)
@@ -121,50 +175,49 @@
             preferred_element_type=jnp.float32,
         )
 
-    xs = xs_ref[...]
-    cols = cols_ref[0]
-    rows = rows_ref[0]
-    scaled = xs * half_lanes(cols, 2, xs.shape)
-    scaled_b = scaled.astype(jnp.bfloat16)
-    parts = []
-    for k in range(2):
-        kernel = jnp.exp(cols[:, k : k + 1] - rows[k : k + 1, :] + bias_ref[...])
-        parts.append(dot_nn((kernel * cb_ref[...]).astype(jnp.bfloat16), scaled_b))
-    lane = lax.broadcasted_iota(jnp.int32, xs.shape, 1)
-    out_ref[...] = jnp.where(lane < SSM_HEAD, parts[0], parts[1])
-    tailed = (scaled * half_lanes(cols, 6, xs.shape)).astype(jnp.bfloat16)
-    state_ref[0] = lax.dot_general(
-        tailed,
-        bmat.astype(jnp.bfloat16),
-        (((0,), (0,)), ((), ())),
-        preferred_element_type=jnp.float32,
-    )
+    def one(k, lanes):
+        xs = xs_ref[:, lanes]
+        cols = cols_ref[k]
+        rows = rows_ref[k]
+        scaled_b = (xs * half_lanes(cols, 2, xs.shape)).astype(jnp.bfloat16)
+        parts = []
+        for h in range(2):
+            kernel = jnp.exp(cols[:, h : h + 1] - rows[h : h + 1, :] + bias_ref[...])
+            parts.append(dot_nn((kernel * cb_ref[...]).astype(jnp.bfloat16), scaled_b))
+        lane = lax.broadcasted_iota(jnp.int32, xs.shape, 1)
+        out_ref[:, lanes] = jnp.where(lane < SSM_HEAD, parts[0], parts[1])
+
+    each_pair(one)
 
 
 def ssm_carry_kernel(local_ref, xs_ref, c_ref, cols_ref, state_ref, skip_ref, z_ref, out_ref, gated_ref):
-    xs = xs_ref[...]
-    carried = lax.dot_general(
-        c_ref[...].astype(jnp.bfloat16),
-        state_ref[0],
-        (((1,), (1,)), ((), ())),
-        preferred_element_type=jnp.float32,
-    )
-    entry = half_lanes(cols_ref[0], 4, xs.shape)
-    out = local_ref[...] + entry * carried + skip_ref[...] * xs
-    out_ref[...] = out
-    gate = z_ref[...]
-    gated_ref[...] = out * (gate * jax.nn.sigmoid(gate))
+    c_low = c_ref[...].astype(jnp.bfloat16)
+
+    def one(k, lanes):
+        xs = xs_ref[:, lanes]
+        carried = lax.dot_general(
+            c_low, state_ref[k], (((1,), (1,)), ((), ())), preferred_element_type=jnp.float32
+        )
+        entry = half_lanes(cols_ref[k], 4, xs.shape)
+        out = local_ref[:, lanes] + entry * carried + skip_ref[:, lanes] * xs
+        out_ref[:, lanes] = out
+        gate = z_ref[:, lanes]
+        gated_ref[:, lanes] = out * (gate * jax.nn.sigmoid(gate))
+
+    each_pair(one)
 
 
 def ssm_direct_kernel(g_ref, c_ref, cols_ref, direct_ref):
-    g = g_ref[...]
-    entered = (g * half_lanes(cols_ref[0], 4, g.shape)).astype(jnp.bfloat16)
-    direct_ref[0] = lax.dot_general(
-        entered,
-        c_ref[...].astype(jnp.bfloat16),
-        (((0,), (0,)), ((), ())),
-        preferred_element_type=jnp.float32,
-    )
+    c_low = c_ref[...].astype(jnp.bfloat16)
+
+    def one(k, lanes):
+        g = g_ref[:, lanes]
+        entered = (g * half_lanes(cols_ref[k], 4, g.shape)).astype(jnp.bfloat16)
+        direct_ref[k] = lax.dot_general(
+            entered, c_low, (((0,), (0,)), ((), ())), preferred_element_type=jnp.float32
+        )
+
+    each_pair(one)
 
 
 def ssm_backward_kernel(
@@ -206,58 +259,61 @@
         db_ref[...] = jnp.zeros_like(db_ref)
         dc_ref[...] = jnp.zeros_like(dc_ref)
 
-    g = g_ref[...]
-    xs = xs_ref[...]
-    skip = skip_ref[...]
-    cols = cols_ref[0]
-    rows = rows_ref[0]
-    step = half_lanes(cols, 2, xs.shape)
-    tail = half_lanes(cols, 6, xs.shape)
-    lane = lax.broadcasted_iota(jnp.int32, xs.shape, 1)
-    first = lane < SSM_HEAD
-    g_low = g.astype(jnp.bfloat16)
-    scaled = xs * step
-    parts = []
-    total = dcb_ref[...]
-    for k in range(2):
-        mine = first if k == 0 else jnp.logical_not(first)
-        kernel = jnp.exp(rows[k : k + 1, :] - cols[:, k : k + 1] + bias_ref[...])
-        parts.append(dot_nn((kernel * cb_ref[...]).astype(jnp.bfloat16), g_low))
-        crossed = lax.dot_general(
-            jnp.where(mine, scaled, 0.0).astype(jnp.bfloat16),
-            g_low,
-            (((1,), (1,)), ((), ())),
-            preferred_element_type=jnp.float32,
+    def one(at, lanes):
+        g = g_ref[:, lanes]
+        xs = xs_ref[:, lanes]
+        skip = skip_ref[:, lanes]
+        cols = cols_ref[at]
+        rows = rows_ref[at]
+        step = half_lanes(cols, 2, xs.shape)
+        tail = half_lanes(cols, 6, xs.shape)
+        lane = lax.broadcasted_iota(jnp.int32, xs.shape, 1)
+        first = lane < SSM_HEAD
+        g_low = g.astype(jnp.bfloat16)
+        scaled = xs * step
+        parts = []
+        total = dcb_ref[...]
+        for k in range(2):
+            mine = first if k == 0 else jnp.logical_not(first)
+            kernel = jnp.exp(rows[k : k + 1, :] - cols[:, k : k + 1] + bias_ref[...])
+            parts.append(dot_nn((kernel * cb_ref[...]).astype(jnp.bfloat16), g_low))
+            crossed = lax.dot_general(
+                jnp.where(mine, scaled, 0.0).astype(jnp.bfloat16),
+                g_low,
+                (((1,), (1,)), ((), ())),
+                preferred_element_type=jnp.float32,
+            )
+            total = total + crossed * kernel
+        dcb_ref[...] = total
+        later = later_ref[at]
+        swept = tail * lax.dot_general(
+            b_low, later, (((1,), (1,)), ((), ())), preferred_element_type=jnp.float32
         )
-        total = total + crossed * kernel
-    dcb_ref[...] = total
-    later = later_ref[0]
-    swept = tail * lax.dot_general(
-        b_low, later, (((1,), (1,)), ((), ())), preferred_element_type=jnp.float32
-    )
-    inner = jnp.where(first, parts[0], parts[1]) + swept
-    dxs_ref[...] = step * inner + skip * g
-    db_ref[...] += dot_nn((scaled * tail).astype(jnp.bfloat16), later)
-    entered = (g * half_lanes(cols, 4, g.shape)).astype(jnp.bfloat16)
-    dc_ref[...] += dot_nn(entered, state_ref[0])
-    rose = g_low.astype(jnp.float32) * (out_ref[...] - skip * xs)
-    stepped = xs * inner
-    kept = scaled.astype(jnp.bfloat16).astype(jnp.float32)
-    fell = kept * (inner - swept) + scaled * swept
-    columns = [
-        jnp.sum(jnp.where(first, value, 0.0), axis=1, keepdims=True)
-        if k == 0
-        else jnp.sum(jnp.where(first, 0.0, value), axis=1, keepdims=True)
-        for value in (rose, stepped, fell)
-        for k in range(2)
-    ]
-    spot = lax.broadcasted_iota(jnp.int32, cols.shape, 1)
-    packed = jnp.zeros_like(cols)
-    for index, column in enumerate(columns):
-        packed = jnp.where(spot == index, column, packed)
-    dcols_ref[0] = packed
-    drows_ref[0, 0:1, :] = jnp.sum(scaled * swept, axis=0, keepdims=True)
-    drows_ref[0, 1:2, :] = jnp.sum(g * xs, axis=0, keepdims=True)
+        inner = jnp.where(first, parts[0], parts[1]) + swept
+        dxs_ref[:, lanes] = step * inner + skip * g
+        db_ref[...] += dot_nn((scaled * tail).astype(jnp.bfloat16), later)
+        entered = (g * half_lanes(cols, 4, g.shape)).astype(jnp.bfloat16)
+        dc_ref[...] += dot_nn(entered, state_ref[at])
+        rose = g_low.astype(jnp.float32) * (out_ref[:, lanes] - skip * xs)
+        stepped = xs * inner
+        kept = scaled.astype(jnp.bfloat16).astype(jnp.float32)
+        fell = kept * (inner - swept) + scaled * swept
+        columns = [
+            jnp.sum(jnp.where(first, value, 0.0), axis=1, keepdims=True)
+            if k == 0
+            else jnp.sum(jnp.where(first, 0.0, value), axis=1, keepdims=True)
+            for value in (rose, stepped, fell)
+            for k in range(2)
+        ]
+        spot = lax.broadcasted_iota(jnp.int32, cols.shape, 1)
+        packed = jnp.zeros_like(cols)
+        for index, column in enumerate(columns):
+            packed = jnp.where(spot == index, column, packed)
+        dcols_ref[at] = packed
+        drows_ref[at, 0:1, :] = jnp.sum(scaled * swept, axis=0, keepdims=True)
+        drows_ref[at, 1:2, :] = jnp.sum(g * xs, axis=0, keepdims=True)
+
+    each_pair(one)
 
     @pl.when(pair == pl.num_programs(0) - 1)
     def _():
@@ -268,18 +324,32 @@
         )
 
 
-def ssm_specs(count):
-    rows = count
-    block = pl.BlockSpec((rows, LANES), lambda p: (0, p))
+def ssm_specs(rows):
+    wide = PAIR_GROUP * LANES
+    block = pl.BlockSpec((rows, wide), lambda p: (0, p))
     bmat = pl.BlockSpec((rows, LANES), lambda p: (0, SSM_PAIRS))
     cmat = pl.BlockSpec((rows, LANES), lambda p: (0, SSM_PAIRS + 1))
-    cols = pl.BlockSpec((1, rows, 8), lambda p: (p, 0, 0))
-    turned = pl.BlockSpec((1, 2, rows), lambda p: (p, 0, 0))
+    cols = pl.BlockSpec((PAIR_GROUP, rows, 8), lambda p: (p, 0, 0))
+    turned = pl.BlockSpec((PAIR_GROUP, 2, rows), lambda p: (p, 0, 0))
     bias = pl.BlockSpec((rows, rows), lambda p: (0, 0))
-    state = pl.BlockSpec((1, LANES, STATE), lambda p: (p, 0, 0))
-    skip = pl.BlockSpec((1, LANES), lambda p: (0, p))
+    state = pl.BlockSpec((PAIR_GROUP, LANES, STATE), lambda p: (p, 0, 0))
+    skip = pl.BlockSpec((1, wide), lambda p: (0, p))
     whole = pl.BlockSpec((rows, LANES), lambda p: (0, 0))
     return block, bmat, cmat, cols, turned, bias, state, skip, whole
+
+
+def ssm_state(act, cols):
+    rows = act.shape[0]
+    block, bmat, cmat, col, turn, square, state, skip, whole = ssm_specs(rows)
+    return pl.pallas_call(
+        ssm_state_kernel,
+        grid=(SSM_PAIRS // PAIR_GROUP,),
+        in_specs=[block, bmat, col],
+        out_specs=state,
+        out_shape=jax.ShapeDtypeStruct((SSM_PAIRS, LANES, STATE), jnp.float32),
+        name="ssm_state",
+        cost_estimate=pl.CostEstimate(flops=10**8, transcendentals=0, bytes_accessed=4 * 10**6),
+    )(act, act, cols)
 
 
 def ssm_local(act, cols, turned, bias):
@@ -287,13 +357,10 @@
     block, bmat, cmat, col, turn, square, state, skip, whole = ssm_specs(rows)
     return pl.pallas_call(
         ssm_local_kernel,
-        grid=(SSM_PAIRS,),
+        grid=(SSM_PAIRS // PAIR_GROUP,),
         in_specs=[block, bmat, cmat, col, turn, square],
-        out_specs=[block, state],
-        out_shape=[
-            jax.ShapeDtypeStruct((rows, SSM_PAIRS * LANES), jnp.float32),
-            jax.ShapeDtypeStruct((SSM_PAIRS, LANES, STATE), jnp.float32),
-        ],
+        out_specs=block,
+        out_shape=jax.ShapeDtypeStruct((rows, SSM_PAIRS * LANES), jnp.float32),
         scratch_shapes=[pltpu.VMEM((rows, rows), jnp.float32)],
         name="ssm_local",
         cost_estimate=pl.CostEstimate(flops=10**9, transcendentals=24 * rows * rows, bytes_accessed=6 * 10**6),
@@ -306,7 +373,7 @@
     shape = jax.ShapeDtypeStruct((rows, SSM_PAIRS * LANES), jnp.float32)
     return pl.pallas_call(
         ssm_carry_kernel,
-        grid=(SSM_PAIRS,),
+        grid=(SSM_PAIRS // PAIR_GROUP,),
         in_specs=[block, block, cmat, col, states, skip, block],
         out_specs=[block, block],
         out_shape=[shape, shape],
@@ -320,7 +387,7 @@
     block, bmat, cmat, col, turn, square, states, skip, whole = ssm_specs(rows)
     return pl.pallas_call(
         ssm_direct_kernel,
-        grid=(SSM_PAIRS,),
+        grid=(SSM_PAIRS // PAIR_GROUP,),
         in_specs=[block, cmat, col],
         out_specs=states,
         out_shape=jax.ShapeDtypeStruct((SSM_PAIRS, LANES, STATE), jnp.float32),
@@ -334,9 +401,9 @@
     block, bmat, cmat, col, turn, square, states, skip, whole = ssm_specs(rows)
     return pl.pallas_call(
         ssm_backward_kernel,
-        grid=(SSM_PAIRS,),
+        grid=(SSM_PAIRS // PAIR_GROUP,),
         in_specs=[block, block, block, bmat, cmat, col, turn, square, states, states, skip],
-        out_specs=[block, whole, whole, col, pl.BlockSpec((1, 2, LANES), lambda p: (p, 0, 0))],
+        out_specs=[block, whole, whole, col, pl.BlockSpec((PAIR_GROUP, 2, LANES), lambda p: (p, 0, 0))],
         out_shape=[
             jax.ShapeDtypeStruct((rows, SSM_PAIRS * LANES), jnp.float32),
             jax.ShapeDtypeStruct((rows, STATE), jnp.float32),
@@ -361,20 +428,27 @@
     def _():
         turned_ref[...] = left_b_ref[...].T
 
+    def filled(right_ref):
+        wide = right_ref.shape[1]
+        piece = math.gcd(wide, 256)
+        for at in range(0, wide, piece):
+            lanes = pl.ds(at, piece)
+            out_ref[:, lanes] = dot_nn(turned_ref[...], right_ref[:, lanes]).astype(jnp.bfloat16)
+
     @pl.when(step < split)
     def _():
-        out_ref[...] = dot_nn(turned_ref[...], right_a_ref[...]).astype(jnp.bfloat16)
+        filled(right_a_ref)
 
     @pl.when(step >= split)
     def _():
-        out_ref[...] = dot_nn(turned_ref[...], right_b_ref[...]).astype(jnp.bfloat16)
+        filled(right_b_ref)
 
 
 def outer_pair(left_a, right_a, left_b, right_b):
     rows, width = left_a.shape
     wide_a = right_a.shape[1]
     wide_b = right_b.shape[1]
-    wide = math.gcd(math.gcd(wide_a, wide_b), 512)
+    wide = math.gcd(math.gcd(wide_a, wide_b), 1024)
     split = wide_a // wide
     total = split + wide_b // wide
     held = pl.BlockSpec((rows, width), lambda j: (0, 0))
@@ -457,13 +531,13 @@
         key_ids[:, None, :] == local_ids[:, :, None]
     )
     hops = min(lax.axis_size("seq") - 1, (MAX_DOC - 2) // rows + 1)
-    spare = -(mamba_dt.shape[1] + 2) % (2 * LANES)
+    spare = -(mamba_dt.shape[1] + 2) % LANES
     shard_in = jnp.concatenate(
         [
             mamba_z,
+            attn_q,
             mamba_x,
             mamba_bc,
-            attn_q,
             attn_kv,
             mamba_dt,
             mixer_norm[:, None],
@@ -474,14 +548,14 @@
     )
     shard_out = jnp.concatenate([mamba_out, attn_out, ffn_gate, ffn_up, ffn_down], axis=1)
     full_in = lax.all_gather(shard_in, ("dp", "seq"), axis=0, tiled=True)
-    full_out = lax.all_gather(shard_out, ("dp", "seq"), axis=0, tiled=True)
+    full_out = lax.all_gather(gathered_seq(shard_out), "dp", axis=0, tiled=True)
     bc_width = mamba_bc.shape[1]
     q_width = attn_q.shape[1]
     kv_width = attn_kv.shape[1]
     hidden_width = ffn_gate.shape[1]
-    at_u = inner_width
-    at_q = at_u + inner_width + bc_width
-    at_kv = at_q + q_width
+    at_q = inner_width
+    at_u = at_q + q_width
+    at_kv = at_u + inner_width + bc_width
     at_dt = at_kv + kv_width
     at_gain = at_dt + SSM_HEADS
     mixer_width = inner_width + q_width
@@ -494,8 +568,8 @@
     normed, factor_one = rms_forward(x_in, gain_one)
     normed_b = normed.astype(jnp.bfloat16)
     projected = matmul(normed_b, full_in)
-    gate_z = projected[:, :at_u]
-    inner_u = projected[:, at_u:at_q]
+    gate_z = projected[:, :at_q]
+    inner_u = projected[:, at_u:at_kv]
     step_raw = projected[:, at_dt:at_gain]
     channels = inner_u.shape[1]
     conv_in = inner_u.reshape(sequences, rows, channels)
@@ -527,16 +601,17 @@
     turned = decay.T.reshape(SSM_PAIRS, 2, rows)
     skip_row = jnp.repeat(d_skip, SSM_HEAD)[None, :]
     carry_rows = jnp.repeat(carry, SSM_HEAD).reshape(SSM_PAIRS, LANES, 1)
-    local_part, state_local = ssm_local(act, cols, turned, bias)
+    state_local = ssm_state(act, cols)
     outgoing = state_local
     for hop in range(hops):
         incoming = passed_along(outgoing.astype(jnp.bfloat16), "seq", 1)
         outgoing = carry_rows * incoming.astype(jnp.float32) + state_local
+    local_part = ssm_local(act, cols, turned, bias)
     ssm_out, gated = ssm_carried(local_part, act, cols, incoming, skip_row, projected)
     silu_z = jax.nn.silu(gate_z)
     mixed_norm, factor_m = rms_forward(gated, inner_norm)
     mixed_b = mixed_norm.astype(jnp.bfloat16)
-    query = projected[:, at_q:at_kv].reshape(sequences, rows, Q_HEADS, HEAD)
+    query = projected[:, at_q:at_u].reshape(sequences, rows, Q_HEADS, HEAD)
     keyval = projected[:, at_kv:at_dt].reshape(sequences, rows, 2 * KV_HEADS, HEAD)
     query_b = rotate(query, cos_b, sin_b).astype(jnp.bfloat16)
     keys_local = rotate(keyval[:, :, :KV_HEADS], cos_b, sin_b)
@@ -601,40 +676,6 @@
         ),
         axis=(1, 2),
     )
-    d_xs, d_bmat, d_cmat, d_cols, d_rows = ssm_backward(
-        d_ssm, act, ssm_out, cols, turned, bias_turned, incoming, later_grad, skip_row
-    )
-    d_pairs = d_cols[:, :, :6].reshape(SSM_PAIRS, rows, 3, 2).transpose(2, 1, 0, 3)
-    d_pairs = d_pairs.reshape(3, rows, SSM_HEADS)
-    d_sums = jnp.sum(d_rows.reshape(SSM_PAIRS, 2, 2, SSM_HEAD), axis=3).transpose(1, 0, 2)
-    d_sums = d_sums.reshape(2, SSM_HEADS)
-    g_skip = d_sums[1]
-    d_decay = d_pairs[0] - d_pairs[2]
-    d_rise = jnp.dot(ladder.T, d_decay, precision=lax.Precision.HIGHEST)
-    d_rise = d_rise + (d_sums[0] + d_carry * carry)
-    d_step = d_pairs[1] + d_rise * rate
-    g_alog = jnp.sum(d_rise * step, axis=0) * rate
-    d_act = jnp.concatenate([d_xs, d_bmat, d_cmat], axis=1).reshape(sequences, rows, channels)
-    d_act, part_ffn = lax.optimization_barrier((d_act, part_ffn))
-    owned_ffn = scattered_seq(part_ffn)
-    d_pre = d_act * silu_grad(conv_pre)
-    g_cbias = jnp.sum(d_pre, axis=(0, 1))
-    g_cweight = jnp.stack(
-        [
-            jnp.sum(d_pre * extended[:, tap : tap + rows] * tap_masks[tap], axis=(0, 1))
-            for tap in range(taps)
-        ]
-    )
-    d_padded = jnp.zeros_like(extended)
-    for tap in range(taps):
-        d_padded = d_padded + jnp.pad(
-            d_pre * tap_masks[tap] * conv_weight[tap], ((0, 0), (tap, taps - 1 - tap), (0, 0))
-        )
-    edge_grad = passed_along(d_padded[:, : taps - 1], "seq", -1)
-    d_inner = d_padded[:, taps - 1 :] + jnp.pad(edge_grad, ((0, 0), (rows - taps + 1, 0), (0, 0)))
-    d_inner = d_inner.reshape(total_rows, channels)
-    d_step_raw = d_step.reshape(total_rows, SSM_HEADS) * jax.nn.sigmoid(step_raw + dt_bias)
-    g_dtb = jnp.sum(d_step_raw, axis=0)
     d_att_b = d_mixers[:, inner_width:].astype(jnp.bfloat16)
     d_att_g = d_att_b.reshape(sequences, rows, KV_HEADS, group, HEAD)
     probs = jnp.exp(attention_scores() - lse)
@@ -669,47 +710,85 @@
         .reshape(total_rows, Q_HEADS * HEAD)
         .astype(jnp.bfloat16)
     )
-    d_z_b = d_z.astype(jnp.bfloat16)
+    d_early = jnp.concatenate([d_z.astype(jnp.bfloat16), d_q_b], axis=1)
+    g_early = outer_pair(normed_b, d_early, d_mid_b, mixers_b)
+    later_grad, g_early = lax.optimization_barrier((later_grad, g_early))
+    part_early = scattered_dp(g_early)
+    d_xs, d_bmat, d_cmat, d_cols, d_rows = ssm_backward(
+        d_ssm, act, ssm_out, cols, turned, bias_turned, incoming, later_grad, skip_row
+    )
+    d_pairs = d_cols[:, :, :6].reshape(SSM_PAIRS, rows, 3, 2).transpose(2, 1, 0, 3)
+    d_pairs = d_pairs.reshape(3, rows, SSM_HEADS)
+    d_sums = jnp.sum(d_rows.reshape(SSM_PAIRS, 2, 2, SSM_HEAD), axis=3).transpose(1, 0, 2)
+    d_sums = d_sums.reshape(2, SSM_HEADS)
+    g_skip = d_sums[1]
+    d_decay = d_pairs[0] - d_pairs[2]
+    d_rise = jnp.dot(ladder.T, d_decay, precision=lax.Precision.HIGHEST)
+    d_rise = d_rise + (d_sums[0] + d_carry * carry)
+    d_step = d_pairs[1] + d_rise * rate
+    g_alog = jnp.sum(d_rise * step, axis=0) * rate
+    d_act = jnp.concatenate([d_xs, d_bmat, d_cmat], axis=1).reshape(sequences, rows, channels)
+    d_act, part_ffn = lax.optimization_barrier((d_act, part_ffn))
+    owned_ffn, _ = hopped_seq(part_ffn, None)
+    d_pre = d_act * silu_grad(conv_pre)
+    g_cbias = jnp.sum(d_pre, axis=(0, 1))
+    g_cweight = jnp.stack(
+        [
+            jnp.sum(d_pre * extended[:, tap : tap + rows] * tap_masks[tap], axis=(0, 1))
+            for tap in range(taps)
+        ]
+    )
+    d_padded = jnp.zeros_like(extended)
+    for tap in range(taps):
+        d_padded = d_padded + jnp.pad(
+            d_pre * tap_masks[tap] * conv_weight[tap], ((0, 0), (tap, taps - 1 - tap), (0, 0))
+        )
+    edge_grad = passed_along(d_padded[:, : taps - 1], "seq", -1)
+    d_inner = d_padded[:, taps - 1 :] + jnp.pad(edge_grad, ((0, 0), (rows - taps + 1, 0), (0, 0)))
+    d_inner = d_inner.reshape(total_rows, channels)
+    d_step_raw = d_step.reshape(total_rows, SSM_HEADS) * jax.nn.sigmoid(step_raw + dt_bias)
+    g_dtb = jnp.sum(d_step_raw, axis=0)
     d_x_b = d_inner[:, :inner_width].astype(jnp.bfloat16)
     d_bc_b = d_inner[:, inner_width:].astype(jnp.bfloat16)
     d_st_b = d_step_raw.astype(jnp.bfloat16)
-    d_projected = jnp.concatenate(
+    d_late = jnp.concatenate(
         [
-            d_z_b,
             d_x_b,
             d_bc_b,
-            d_q_b,
             d_kv_b,
             d_st_b,
             jnp.zeros((total_rows, spare + 2), jnp.bfloat16),
         ],
         axis=1,
     )
-    g_rest = outer_pair(normed_b, d_projected, d_mid_b, mixers_b)
-    g_rest, owned_ffn = lax.optimization_barrier((g_rest, owned_ffn))
-    owned_rest = scattered_seq(scattered_dp(g_rest))
-    d_norm = matmul_nt(d_projected, full_in)
+    part_late = scattered_dp(matmul_tn(normed_b, d_late).astype(jnp.bfloat16))
+    d_norm = matmul_nt(d_early, full_in[:, :at_u]) + matmul_nt(d_late, full_in[:, at_u:])
     d_in_norm, g_mnorm = rms_backward(x_in, factor_one, gain_one, d_norm)
     grad_in = (d_mid + d_in_norm).astype(jnp.bfloat16).reshape(sequences, rows, width)
     summed = lax.psum(
         (g_cweight, g_cbias, g_dtb, g_alog, g_skip, g_inner, g_mnorm, g_fnorm), ("dp", "seq")
     )
     gain_rows = mixer_norm.shape[0]
+    part_early, summed, grad_in = lax.optimization_barrier((part_early, summed, grad_in))
+    owned_early, part_late = hopped_seq(part_early, part_late)
+    owned_late = scattered_seq(part_late)
     first_row = (lax.axis_index("dp") * lax.axis_size("seq") + lax.axis_index("seq")) * gain_rows
     g_mnorm_own = lax.dynamic_slice_in_dim(summed[6], first_row, gain_rows, 0)
     g_fnorm_own = lax.dynamic_slice_in_dim(summed[7], first_row, gain_rows, 0)
-    at_mixers = shard_in.shape[1]
+    at_mixers = at_u
+    late_kv = at_kv - at_u
+    late_dt = at_dt - at_u
     return (
         block_out,
         grad_in,
-        owned_rest[:, :at_u],
-        owned_rest[:, at_u : at_u + inner_width],
-        owned_rest[:, at_u + inner_width : at_q],
-        owned_rest[:, at_dt:at_gain],
-        owned_rest[:, at_mixers : at_mixers + inner_width],
-        owned_rest[:, at_q:at_kv],
-        owned_rest[:, at_kv:at_dt],
-        owned_rest[:, at_mixers + inner_width :],
+        owned_early[:, :at_q],
+        owned_late[:, :inner_width],
+        owned_late[:, inner_width:late_kv],
+        owned_late[:, late_dt : late_dt + SSM_HEADS],
+        owned_early[:, at_mixers : at_mixers + inner_width],
+        owned_early[:, at_q:at_u],
+        owned_late[:, late_kv:late_dt],
+        owned_early[:, at_mixers + inner_width :],
         owned_ffn[:, :hidden_width],
         owned_ffn[:, hidden_width : 2 * hidden_width],
         owned_ffn[:, 2 * hidden_width :],

time: 568 us -> 509 us (0.90)
  waiting for transfers between devices: 241 us -> 176 us
  Pallas kernels: 77.5 us -> 51.8 us
  starting transfers between devices: 24.6 us -> 39.8 us
  matrix products: 61.2 us -> 71.4 us
  other arithmetic: 50.3 us -> 58.5 us
    ppermute x0 -> x6, waiting for transfers between devices: none -> 129 us  [the longest x2 91.6 us: gathered_seq(): got = lax.ppermute(held, 'seq', [(i, i ^ bit) for i in range(count)])]
    all_gather x1, waiting for transfers between devices: 69.2 us -> 0.01 us  [local(): full_in = lax.all_gather(shard_in, ('dp', 'seq'), axis=0, tiled=True)]
    reduce_scatter x2 -> x3, waiting for transfers between devices: 95.6 us -> 28.2 us  [scattered_dp(): return lax.psum_scatter(grad, 'dp', scatter_dimension=0, tiled=True)]
    ppermute x10, waiting for transfers between devices: 51.2 us -> 7.94 us  [passed_along(): return lax.ppermute(block, axis, route)]
    ppermute x0 -> x6, starting transfers between devices: none -> 15.9 us  [the longest x4 9.21 us: hopped_seq(): got = lax.ppermute(other, 'seq', [(i, i ^ bit) for i in range(count)])]
    pallas_call x2, Pallas kernels: 31.8 us -> 16.8 us  [outer_pair(): pl.pallas_call(functools.partial(outer_kernel, split), grid=(total,), in_...]
    all_gather x1, waiting for transfers between devices: 24.6 us -> 10.8 us  [local(): full_out = lax.all_gather(gathered_seq(shard_out), 'dp', axis=0, tiled=True)]
    pallas_call x4 -> x5, Pallas kernels: 45.7 us -> 35 us  [the longest x1 12.6 us: ssm_backward(): pl.pallas_call(ssm_backward_kernel, grid=(SSM_PAIRS // PAIR_GROUP,), in_s...]
  transfers between devices with their start and end apart: 16 -> 22, of which waited for: 10 -> 11; matrix products, arithmetic and copies ran while one was open for 21% -> 28% of each run, Pallas kernels for 12% -> 8%
where the time goes in v3:
time: 509 us; the launch traced here: 501 us
  waiting for transfers between devices  176 us (35%)
  matrix products  71.4 us (14%)
  other arithmetic  58.5 us (11%)
  Pallas kernels  51.8 us (10%)
  local copies, waits for them, and re-layouts  44.2 us (9%)
  blocking collectives  43.5 us (9%)
  starting transfers between devices  39.8 us (8%)
  between operations  15.8 us (3%)
    ppermute x2, waiting for transfers between devices, gathered_seq(): got = lax.ppermute(held, 'seq', [(i, i ^ bit) for i in range(count)])  91.6 us
    psum x1, blocking collectives, local(): lax.psum((g_cweight, g_cbias, g_dtb, g_alog, g_skip, g_inner, g_mnorm, g_...  43.5 us
    ppermute x4, waiting for transfers between devices, hopped_seq(): got = lax.ppermute(other, 'seq', [(i, i ^ bit) for i in range(count)])  36.9 us
    reduce_scatter x3, waiting for transfers between devices, scattered_dp(): return lax.psum_scatter(grad, 'dp', scatter_dimension=0, tiled=True)  28.2 us
    dot_general x5, matrix products, matmul_nt(): lax.dot_general(left, right, (((1,), (1,)), ((), ())), preferred_element_...  25.8 us
    dot_general x4, matrix products, matmul(): return jnp.dot(left, right, preferred_element_type=jnp.float32)  23.6 us
    ppermute x10, starting transfers between devices, passed_along(): return lax.ppermute(block, axis, route)  23.1 us
    pallas_call x2, Pallas kernels, outer_pair(): pl.pallas_call(functools.partial(outer_kernel, split), grid=(total,), in_...  16.8 us
  transfers between devices with their start and end apart: 22, of which 11 were waited for; matrix products, arithmetic and copies ran while one was open for 28% of the time, Pallas kernels for 8%

profile of v3, /device:TPU:0, one launch (start us, length us, event | category | flops | bytes accessed | tf_op | source)
XLA Modules:
  0.0 500.8 jit_solution(5112020425249661471)
XLA Ops:
  18.9 17.0 %collective-permute-done.5 = bf16[32,8192]{1,0:T(8,128)(2,1)S(1)} collective-permute-done((bf16[32,8192]{1,0:T(8,128)(2,1)S(1)}, bf16[32,8192]{1,0:T(8,128)(2,1)S(1)}, u32[]{:S(2)}, u32[]{:S(2)}) %collective-permute-start.5) | collective-permute-done | bytes 524320 | tf_op jit(solution)/shard_map/ppermute | solution.py:47
  39.6 74.7 %collective-permute-done.6 = bf16[64,8192]{1,0:T(8,128)(2,1)S(1)} collective-permute-done((bf16[64,8192]{1,0:T(8,128)(2,1)S(1)}, bf16[64,8192]{1,0:T(8,128)(2,1)S(1)}, u32[]{:S(2)}, u32[]{:S(2)}) %collective-permute-start.6) | collective-permute-done | bytes 1048608 | tf_op jit(solution)/shard_map/ppermute | solution.py:47
  126.5 6.4 %fusion.92.z_ref = f32[256,4224]{1,0:T(8,128)S(1)} fusion(bf16[256,1024]{1,0:T(8,128)(2,1)S(1)} %fusion.49.left_a_ref, bf16[1024,4224]{1,0:T(8,128)(2,1)} %all-gather.3.cloned.1.call-done), kind=kOutput, calls=%fused_computation.232 | convolution fusion | flops 2214592512 | bytes 13500416 | tf_op jit(solution)/shard_map/dot_general | solution.py:94
  139.4 5.8 %collective-permute-start.3 = (bf16[1,256,256]{1,2,0:T(8,128)(2,1)S(1)}, bf16[1,256,256]{1,2,0:T(8,128)(2,1)}, u32[]{:S(2)}, u32[]{:S(2)}) collective-permute-start(bf16[1,256,256]{1,2,0:T(8,128)(2,1)S(1)} %bitcast.261), channel_id=1, source_target_pairs={{0,2},{1,3},{4,6},{5,7},{8,10},{9,11},{12,14},{13,15},{16,18},{17,... | collective-permute-start | bytes 393224 | tf_op jit(solution)/shard_map/ppermute | solution.py:30
  163.7 5.8 %ssm_state.1 = f32[12,128,128]{2,1,0:T(8,128)} custom-call(f32[256,1792]{1,0:T(8,128)} %get-tuple-element.208.xs_ref.b_ref.c_ref, f32[256,1792]{1,0:T(8,128)} %get-tuple-element.208.xs_ref.b_ref.c_ref, f32[12,256,8]{2,1,0:T(8,128)} %copy.176.cols_ref), custom_call_target="tpu_custom_call" | custom-call | flops 100000000 | bytes 4000000 | tf_op jit(solution)/shard_map/ssm_state/pallas_call | solution.py:344
  172.3 5.8 %ssm_local.1.local_ref = f32[256,1536]{1,0:T(8,128)} custom-call(f32[256,1792]{1,0:T(8,128)} %get-tuple-element.208.xs_ref.b_ref.c_ref, f32[256,1792]{1,0:T(8,128)} %get-tuple-element.208.xs_ref.b_ref.c_ref, f32[256,1792]{1,0:T(8,128)} %get-tuple-element.208.xs_ref.b_ref.c_ref, f32[12,256,8]{2,1,0:T(8,128)} %copy.176.cols_ref, ...), custom_call_target="tpu_custom_call" | custom-call | flops 1000000000 | bytes 6000000 | tf_op jit(solution)/shard_map/ssm_local/pallas_call | solution.py:358
  187.5 5.0 collective-permute-done.2.state_ref
  193.3 5.8 %ssm_carried.1 = (f32[256,1536]{1,0:T(8,128)}, f32[256,1536]{1,0:T(8,128)}) custom-call(f32[256,1536]{1,0:T(8,128)} %ssm_local.1.local_ref, f32[256,1792]{1,0:T(8,128)} %get-tuple-element.208.xs_ref.b_ref.c_ref, f32[256,1792]{1,0:T(8,128)} %get-tuple-element.208.xs_ref.b_ref.c_ref, f32[12,256,8]{2,1,0:T(8,128)} %copy.176.cols_ref, ...), custom_call_target="tpu_custom_call" | custom-call | flops 100000000 | bytes 9000000 | tf_op jit(solution)/shard_map/ssm_carried/pallas_call | solution.py:374
  202.1 10.8 %all-gather.5.cloned.1.call-done = bf16[1024,8192]{1,0:T(8,128)(2,1)} async-done(((bf16[128,8192]{1,0:T(8,128)(2,1)}), bf16[1024,8192]{1,0:T(8,128)(2,1)}) %all-gather.5.cloned.1.call-update) | async-done | bytes 16777232 | tf_op jit(solution)/shard_map/all_gather | solution.py:551
  217.7 5.9 %fusion.2 = f32[256,4096]{1,0:T(8,128)S(1)} fusion(bf16[256,1024]{1,0:T(8,128)(2,1)S(1)} %multiply_convert_fusion.5.left_a_ref, bf16[1024,8192]{1,0:T(8,128)(2,1)} %all-gather.5.cloned.1.call-done), kind=kOutput, calls=%fused_computation.2 | convolution fusion | flops 2147483648 | bytes 13107200 | tf_op jit(solution)/shard_map/dot_general | solution.py:94
  223.6 5.1 %multiply_convert_fusion.1 = (bf16[256,2048]{1,0:T(8,128)(2,1)S(1)}, bf16[256,2048]{1,0:T(8,128)(2,1)S(1)}, bf16[256,2048]{1,0:T(8,128)(2,1)}) fusion(f32[256,4096]{1,0:T(8,128)S(1)} %fusion.2, bf16[1024,8192]{1,0:T(8,128)(2,1)} %all-gather.5.cloned.1.call-done, bf16[1,256,1024]{2,1,0:T(8,128)(2,1)S(1)} %copy-done.14), kind=kOutput, calls=%fused_computation.40 | convolution fusion | flops 1081606144 | bytes 12058624 | tf_op jit(solution)/shard_map/dot_general | solution.py:94
  230.7 9.5 %outer_pair.3 = bf16[1024,6144]{1,0:T(8,128)(2,1)} custom-call(bf16[256,1024]{1,0:T(8,128)(2,1)} %copy-done.24, bf16[256,4096]{1,0:T(8,128)(2,1)} %pad_maximum_fusion.1.right_a_ref, bf16[256,1024]{1,0:T(8,128)(2,1)} %bitcast.244, bf16[256,2048]{1,0:T(8,128)(2,1)} %get-tuple-element.216.right_b_ref), custom_call_target="tpu_custom_call" | custom-call | flops 3221225472 | bytes 12582912 | tf_op jit(solution)/shard_map/outer_pair/pallas_call | solution.py:455
  240.7 7.0 %multiply_reduce_fusion.7 = (f32[1024]{0:T(1024)}, f32[256]{0:T(256)S(1)}, f32[256,1024]{1,0:T(8,128)S(1)}) fusion(f32[256,1024]{1,0:T(8,128)S(1)} %get-tuple-element.262, f32[256]{0:T(256)} %copy-done.57, f32[1024]{0:T(1024)} %get-tuple-element.172, bf16[1024,8192]{1,0:T(8,128)(2,1)} %all-gather.5.cloned.1.call-done, bf16[256,2048]{1,0:T(8,128)(2,1)} %copy-done.33, ...), kind=kOutput, calls=%fused_computation.103 | convolution fusion | flops 2153249536 | bytes 12593152 | tf_op jit(solution)/shard_map/dot_general | solution.py:98
  249.5 6.2 %fusion.16 = f32[256,2048]{1,0:T(8,128)S(1)} fusion(bf16[256,1024]{1,0:T(8,128)(2,1)S(1)} %fusion.84.left_b_ref, bf16[1024,8192]{1,0:T(8,128)(2,1)} %all-gather.5.cloned.1.call-done), kind=kOutput, calls=%fused_computation.22 | convolution fusion | flops 1073741824 | bytes 6815744 | tf_op jit(solution)/shard_map/dot_general | solution.py:94
  260.0 4.8 ssm_direct.1
  268.3 5.8 %fusion.4 = (f32[2,4,256]{2,1,0:T(4,128)S(1)}, f32[2,768,256,4]{2,1,3,0:T(8,128)S(1)}) fusion(f32[2,768,256,4]{2,1,3,0:T(8,128)} %copy-done.1, f32[2,4,256]{2,1,0:T(4,128)S(1)} %bitcast.269, pred[256,768]{0,1:T(8,128)(4,1)S(1)} %fusion.63, bf16[256,2,4,64]{0,3,2,1:T(8,128)(2,1)S(1)} %bitcast.251, bf16[1,768,4,64]{1,3,2,0:T(8,128)(2,1)S(1)} %copy-done.26), kind=kOutput, calls=%fused_computation.7 | convolution fusion | flops 209188864 | bytes 13254656 | tf_op jit(solution)/shard_map/stkgd,slkd->skgtl/dot_general | solution.py:682
  286.5 7.3 %outer_pair.2 = bf16[1024,4096]{1,0:T(8,128)(2,1)} custom-call(bf16[256,1024]{1,0:T(8,128)(2,1)} %copy-done.5, bf16[256,2048]{1,0:T(8,128)(2,1)} %get-tuple-element.268.right_a_ref, bf16[256,1024]{1,0:T(8,128)(2,1)} %copy-done.23, bf16[256,2048]{1,0:T(8,128)(2,1)} %get-tuple-element.267.right_b_ref), custom_call_target="tpu_custom_call" | custom-call | flops 2147483648 | bytes 8388608 | tf_op jit(solution)/shard_map/outer_pair/pallas_call | solution.py:455
  315.1 12.6 %ssm_backward.1 = (f32[256,1536]{1,0:T(8,128)}, f32[256,128]{1,0:T(8,128)}, f32[256,128]{1,0:T(8,128)}, f32[12,256,8]{2,1,0:T(8,128)}, f32[12,2,128]{2,1,0:T(2,128)}) custom-call(f32[256,1536]{1,0:T(8,128)} %get-tuple-element.213.g_ref, f32[256,1792]{1,0:T(8,128)} %get-tuple-element.208.xs_ref.b_ref.c_ref, f32[256,1536]{1,0:T(8,128)} %get-tuple-element.45.out_ref, ...), custom_call_target="tpu_custom_call" | custom-call | flops 2000000000 | bytes 12000000 | tf_op jit(solution)/shard_map/ssm_backward/pallas_call | solution.py:402
  353.3 4.8 convolution_convert_fusion
  359.1 6.0 %fusion.58 = (f32[256]{0:T(256)S(1)}, f32[1024]{0:T(1024)S(1)}, f32[256,1024]{1,0:T(8,128)}) fusion(bf16[1,256,1024]{2,1,0:T(8,128)(2,1)S(1)} %copy-done.13, f32[1024]{0:T(1024)S(1)} %copy-done.52, f32[256]{0:T(256)S(1)} %copy-done.63, f32[256,1024]{1,0:T(8,128)} %fusion.10, bf16[256,2176]{1,0:T(8,128)(2,1)} %concatenate.110, ...), kind=kOutput, calls=%fused_computation.97 | convolution fusion | flops 1142946560 | bytes 8202240 | tf_op jit(solution)/shard_map/dot_general | solution.py:98
  365.2 43.5 %all-reduce.7 = (f32[4,1792]{1,0:T(4,128)}, f32[1792]{0:T(1024)}, f32[24]{0:T(128)}, f32[24]{0:T(128)}, f32[24]{0:T(128)}, /*index=5*/f32[1536]{0:T(1024)}, f32[1024]{0:T(1024)S(1)}, f32[1024]{0:T(1024)S(1)}) all-reduce(f32[4,1792]{1,0:T(4,128)S(1)} %pad_maximum_fusion.13, ...), channel_id=1, replica_groups=mesh['dp'=8,'seq'=4] {'dp','seq'}, use_global_device_ids=true, to_apply=%region_14.15 | all-reduce | flops 12616 | bytes 100928 | tf_op jit(solution)/shard_map/psum | solution.py:768
  418.9 16.1 %collective-permute-done.12 = bf16[2,32,4096]{2,1,0:T(8,128)(2,1)S(1)} collective-permute-done((bf16[2,32,4096]{2,1,0:T(8,128)(2,1)S(1)}, bf16[2,32,4096]{2,1,0:T(8,128)(2,1)S(1)}, u32[]{:S(2)}, u32[]{:S(2)}) %collective-permute-start.12) | collective-permute-done | bytes 524320 | tf_op jit(solution)/shard_map/ppermute | solution.py:64
  436.5 28.2 %reduce-scatter.9.cloned.1.call-done = bf16[128,2176]{1,0:T(8,128)(2,1)} async-done(((bf16[1024,2176]{1,0:T(8,128)(2,1)}), bf16[128,2176]{1,0:T(8,128)(2,1)}) %reduce-scatter.9.cloned.1.call-update) | async-done | bytes 557072 | tf_op jit(solution)/shard_map/reduce_scatter | solution.py:34
  468.1 19.7 %collective-permute-done.13 = bf16[1,32,4096]{2,1,0:T(8,128)(2,1)S(1)} collective-permute-done((bf16[1,32,4096]{2,1,0:T(8,128)(2,1)S(1)}, bf16[1,32,4096]{2,1,0:T(8,128)(2,1)S(1)}, u32[]{:S(2)}, u32[]{:S(2)}) %collective-permute-start.13) | collective-permute-done | bytes 262176 | tf_op jit(solution)/shard_map/ppermute | solution.py:64
  (364 shorter events, 165.4 us)
Async XLA Ops:
  7.2 117.0 %all-gather.3.cloned.1.call-start = ((), (), s32[]{:S(2)}) async-start(), calls=%async_computation.4 | async-start | bytes 8921088 | tf_op jit(solution)/shard_map/all_gather | solution.py:550
  11.3 201.7 %all-gather.5.cloned.1.call-start = ((), (), s32[]{:S(2)}) async-start(), calls=%async_computation.5 | async-start | bytes 18874368 | tf_op jit(solution)/shard_map/all_gather | solution.py:551
  15.8 20.1 %collective-permute-start.5 = (bf16[32,8192]{1,0:T(8,128)(2,1)S(1)}, bf16[32,8192]{1,0:T(8,128)(2,1)S(1)}, u32[]{:S(2)}, u32[]{:S(2)}) collective-permute-start(bf16[32,8192]{1,0:T(8,128)(2,1)S(1)} %constant_dynamic-update-slice_fusion), channel_id=1, source_target_pairs={{0,1},{1,0},{2,3},{3,2},{4,5},{5,4},{6,7},{7,6},{8,9},{9,8},{10,11... | collective-permute-start | bytes 1572872 | tf_op jit(solution)/shard_map/ppermute | solution.py:47
  36.0 78.2 %collective-permute-start.6 = (bf16[64,8192]{1,0:T(8,128)(2,1)S(1)}, bf16[64,8192]{1,0:T(8,128)(2,1)S(1)}, u32[]{:S(2)}, u32[]{:S(2)}) collective-permute-start(bf16[64,8192]{1,0:T(8,128)(2,1)S(1)} %pad_maximum_fusion.4), channel_id=1, source_target_pairs={{0,2},{1,3},{2,0},{3,1},{4,6},{5,7},{6,4},{7,5},{8,10},{9,11},{10,... | collective-permute-start | bytes 3145736 | tf_op jit(solution)/shard_map/ppermute | solution.py:47
  116.2 219.8 %reduce-scatter.7.cloned.1.call-start = ((), (), s32[]{:S(2)}) async-start(), calls=%async_computation.7 | async-start | bytes 14155776 | tf_op jit(solution)/shard_map/reduce_scatter | solution.py:34
  135.2 42.9 %collective-permute-start.4 = (bf16[1,256,256]{1,2,0:T(8,128)(2,1)S(1)}, bf16[1,256,256]{1,2,0:T(8,128)(2,1)}, u32[]{:S(2)}, u32[]{:S(2)}) collective-permute-start(bf16[1,256,256]{1,2,0:T(8,128)(2,1)S(1)} %bitcast.260), channel_id=1, source_target_pairs={{0,1},{1,2},{2,3},{4,5},{5,6},{6,7},{8,9},{9,10},{10,11},{12,13},{... | collective-permute-start | bytes 393224 | tf_op jit(solution)/shard_map/ppermute | solution.py:30
  139.4 38.8 %collective-permute-start.3 = (bf16[1,256,256]{1,2,0:T(8,128)(2,1)S(1)}, bf16[1,256,256]{1,2,0:T(8,128)(2,1)}, u32[]{:S(2)}, u32[]{:S(2)}) collective-permute-start(bf16[1,256,256]{1,2,0:T(8,128)(2,1)S(1)} %bitcast.261), channel_id=1, source_target_pairs={{0,2},{1,3},{4,6},{5,7},{8,10},{9,11},{12,14},{13,15},{16,18},{17,... | collective-permute-start | bytes 393224 | tf_op jit(solution)/shard_map/ppermute | solution.py:30
  147.7 11.4 %collective-permute-start = (f32[1,3,1792]{2,1,0:T(4,128)}, f32[1,3,1792]{2,1,0:T(4,128)}, u32[]{:S(2)}, u32[]{:S(2)}) collective-permute-start(f32[1,3,1792]{2,1,0:T(4,128)} %slice.342), channel_id=1, source_target_pairs={{0,1},{1,2},{2,3},{4,5},{5,6},{6,7},{8,9},{9,10},{10,11},{12,13},{... | collective-permute-start | bytes 64520 | tf_op jit(solution)/shard_map/ppermute | solution.py:30
  170.8 10.9 %collective-permute-start.1 = (bf16[12,128,128]{2,1,0:T(8,128)(2,1)S(1)}, bf16[12,128,128]{2,1,0:T(8,128)(2,1)S(1)}, u32[]{:S(2)}, u32[]{:S(2)}) collective-permute-start(bf16[12,128,128]{2,1,0:T(8,128)(2,1)S(1)} %convert_element_type.258), channel_id=1, source_target_pairs={{0,1},{1,2},{2,3},{4,5},{5,6},{6,7},{8,9},{9,10},{10,11},{12,13},{... | collective-permute-start | bytes 1179656 | tf_op jit(solution)/shard_map/ppermute | solution.py:30
  182.3 10.2 %collective-permute-start.2 = (bf16[12,128,128]{2,1,0:T(8,128)(2,1)S(1)}, bf16[12,128,128]{2,1,0:T(8,128)(2,1)S(1)}, u32[]{:S(2)}, u32[]{:S(2)}) collective-permute-start(bf16[12,128,128]{2,1,0:T(8,128)(2,1)S(1)} %add_convert_fusion.1), channel_id=1, source_target_pairs={{0,1},{1,2},{2,3},{4,5},{5,6},{6,7},{8,9},{9,10},{10,11},{12,13},{... | collective-permute-start | bytes 1179656 | tf_op jit(solution)/shard_map/ppermute | solution.py:30
  240.2 171.6 %reduce-scatter.5.cloned.1.call-start = ((), (), s32[]{:S(2)}) async-start(), calls=%async_computation.6 | async-start | bytes 9437184 | tf_op jit(solution)/shard_map/reduce_scatter | solution.py:34
  266.9 13.4 %collective-permute-start.7 = (bf16[12,128,128]{2,1,0:T(8,128)(2,1)}, bf16[12,128,128]{2,1,0:T(8,128)(2,1)}, u32[]{:S(2)}, u32[]{:S(2)}) collective-permute-start(bf16[12,128,128]{2,1,0:T(8,128)(2,1)} %convert_element_type.279), channel_id=1, source_target_pairs={{1,0},{2,1},{3,2},{5,4},{6,5},{7,6},{9,8},{10,9},{11,10},{13,12},{... | collective-permute-start | bytes 1179656 | tf_op jit(solution)/shard_map/ppermute | solution.py:30
  282.5 12.9 %collective-permute-start.8 = (bf16[12,128,128]{2,1,0:T(8,128)(2,1)}, bf16[12,128,128]{2,1,0:T(8,128)(2,1)}, u32[]{:S(2)}, u32[]{:S(2)}) collective-permute-start(bf16[12,128,128]{2,1,0:T(8,128)(2,1)} %add_convert_fusion), channel_id=1, source_target_pairs={{1,0},{2,1},{3,2},{5,4},{6,5},{7,6},{9,8},{10,9},{11,10},{13,12},{... | collective-permute-start | bytes 1179656 | tf_op jit(solution)/shard_map/ppermute | solution.py:30
  295.4 169.3 %reduce-scatter.9.cloned.1.call-start = ((), (), s32[]{:S(2)}) async-start(), calls=%async_computation.8 | async-start | bytes 5013504 | tf_op jit(solution)/shard_map/reduce_scatter | solution.py:34
  302.4 11.8 %collective-permute-start.11 = (bf16[1,256,256]{1,2,0:T(8,128)(2,1)S(1)}, bf16[1,256,256]{1,2,0:T(8,128)(2,1)S(1)}, u32[]{:S(2)}, u32[]{:S(2)}) collective-permute-start(bf16[1,256,256]{1,2,0:T(8,128)(2,1)S(1)} %get-tuple-element.236), channel_id=1, source_target_pairs={{2,0},{3,1},{6,4},{7,5},{10,8},{11,9},{14,12},{15,13},{18,16},{19,... | collective-permute-start | bytes 393224 | tf_op jit(solution)/shard_map/ppermute | solution.py:30
  303.9 10.4 %collective-permute-start.10 = (bf16[1,256,256]{1,2,0:T(8,128)(2,1)S(1)}, bf16[1,256,256]{1,2,0:T(8,128)(2,1)S(1)}, u32[]{:S(2)}, u32[]{:S(2)}) collective-permute-start(bf16[1,256,256]{1,2,0:T(8,128)(2,1)S(1)} %get-tuple-element.235), channel_id=1, source_target_pairs={{1,0},{2,1},{3,2},{5,4},{6,5},{7,6},{9,8},{10,9},{11,10},{13,12},{... | collective-permute-start | bytes 393224 | tf_op jit(solution)/shard_map/ppermute | solution.py:30
  341.9 7.2 %collective-permute-start.9 = (f32[1,3,1792]{2,1,0:T(4,128)S(1)}, f32[1,3,1792]{2,1,0:T(4,128)S(1)}, u32[]{:S(2)}, u32[]{:S(2)}) collective-permute-start(f32[1,3,1792]{2,1,0:T(4,128)S(1)} %pad_add_fusion.1), channel_id=1, source_target_pairs={{1,0},{2,1},{3,2},{5,4},{6,5},{7,6},{9,8},{10,9},{11,10},{13,12},{... | collective-permute-start | bytes 64520 | tf_op jit(solution)/shard_map/ppermute | solution.py:30
  344.5 69.9 %collective-permute-start.14 = (bf16[2,32,6144]{2,1,0:T(8,128)(2,1)}, bf16[2,32,6144]{2,1,0:T(8,128)(2,1)}, u32[]{:S(2)}, u32[]{:S(2)}) collective-permute-start(bf16[2,32,6144]{2,1,0:T(8,128)(2,1)} %select_bitcast_fusion), channel_id=1, source_target_pairs={{0,1},{1,0},{2,3},{3,2},{4,5},{5,4},{6,7},{7,6},{8,9},{9,8},{10,11... | collective-permute-start | bytes 2359304 | tf_op jit(solution)/shard_map/ppermute | solution.py:64
  358.1 50.5 %copy-start.50 = (f32[1024]{0:T(1024)S(1)}, f32[1024]{0:T(1024)}, u32[]{:S(2)}) copy-start(f32[1024]{0:T(1024)} %get-tuple-element.172) | copy-start | bytes 12292
  358.2 50.5 %copy-start.59 = (f32[256]{0:T(256)S(1)}, f32[256]{0:T(256)}, u32[]{:S(2)}) copy-start(f32[256]{0:T(256)} %copy-done.57) | copy-start | bytes 3076
  358.2 131.2 %reduce-scatter.11.cloned.1.call-start = ((), (), s32[]{:S(2)}) async-start(), calls=%async_computation.9 | async-start | bytes 696320 | tf_op jit(solution)/shard_map/reduce_scatter | solution.py:38
  413.1 21.9 %collective-permute-start.12 = (bf16[2,32,4096]{2,1,0:T(8,128)(2,1)S(1)}, bf16[2,32,4096]{2,1,0:T(8,128)(2,1)S(1)}, u32[]{:S(2)}, u32[]{:S(2)}) collective-permute-start(bf16[2,32,4096]{2,1,0:T(8,128)(2,1)S(1)} %select_bitcast_fusion.1), channel_id=1, source_target_pairs={{0,1},{1,0},{2,3},{3,2},{4,5},{5,4},{6,7},{7,6},{8,9},{9,8},{10,11... | collective-permute-start | bytes 1572872 | tf_op jit(solution)/shard_map/ppermute | solution.py:64
  415.9 20.5 %collective-permute-start.15 = (bf16[1,32,6144]{2,1,0:T(8,128)(2,1)S(1)}, bf16[1,32,6144]{2,1,0:T(8,128)(2,1)S(1)}, u32[]{:S(2)}, u32[]{:S(2)}) collective-permute-start(bf16[1,32,6144]{2,1,0:T(8,128)(2,1)S(1)} %select_bitcast_fusion.2), channel_id=1, source_target_pairs={{0,2},{1,3},{2,0},{3,1},{4,6},{5,7},{6,4},{7,5},{8,10},{9,11},{10,... | collective-permute-start | bytes 1179656 | tf_op jit(solution)/shard_map/ppermute | solution.py:64
  464.7 23.1 %collective-permute-start.13 = (bf16[1,32,4096]{2,1,0:T(8,128)(2,1)S(1)}, bf16[1,32,4096]{2,1,0:T(8,128)(2,1)S(1)}, u32[]{:S(2)}, u32[]{:S(2)}) collective-permute-start(bf16[1,32,4096]{2,1,0:T(8,128)(2,1)S(1)} %select_bitcast_fusion.3), channel_id=1, source_target_pairs={{0,2},{1,3},{2,0},{3,1},{4,6},{5,7},{6,4},{7,5},{8,10},{9,11},{10,... | collective-permute-start | bytes 786440 | tf_op jit(solution)/shard_map/ppermute | solution.py:64
  (81 other events, 528.7 us)
Sparse Core Ops, SparseCore 0:
  11.4 108.5 all-gather.2
  121.9 90.9 all-gather.4
  240.3 92.2 reduce-scatter.6
  336.0 72.7 reduce-scatter.4
  412.0 52.6 reduce-scatter.8
  468.2 21.0 reduce-scatter.10
